TPU v7x, 128 devices: a whole 4x4x4 slice. The times are simulated.
128 devices in a mesh: fluid: 4 (over y), solid: 32 (over x, z, core).
Axes of the slice: x: 4, y: 4, z: 4, core: 2. Of those that a mesh axis runs over, the one named last changes fastest.
Arguments:
- fluid_flux: bfloat16 [3, 8192, 128], P(None, ('fluid', 'solid')), may hold values from -6 to 6
- margin_blocks: bfloat16 [20480, 128, 128], P(('fluid', 'solid')), may hold values from 0 to 0.046875
- block_fluid: int32 [20480], P(('fluid', 'solid')), may hold values from 0 to 63
- block_solid: int32 [20480], P(('fluid', 'solid')), may hold values from 0 to 1023, as said below
- diag_blocks: float32 [1024, 128, 128], P('solid'), may hold values from -3 to 18, as said below
- couple_blocks: float32 [1024, 128, 128], P('solid'), may hold values from -0.15 to 0.15
- couple_offset: int32 [1024], P('solid'), may hold values from 1 to 16
Outputs:
- mapped: float32 [3, 1024, 128], P(None, 'solid')
- nodal: float32 [3, 1024, 128], P(None, 'solid')
Inputs may be any that keep to these rules, and one draw needn't show every extreme that they name: `block_solid`: the solid tiles of solid index s are s * 32 to (s + 1) * 32 - 1. Among the 160 blocks of one device at most 12 have solid tiles of one solid index, and exactly 12 do for some index. block_fluid indexes the 64 fluid tiles of the device that holds the block. `diag_blocks`: each diagonal block is symmetric.
All inputs are finite; a program needn't handle non-finite values.
Results may differ from a plain program's by a relative error of at most 0.0003.
Values sent between devices are 32-bit elements; how exact they have to be, the bound alone decides.
No kernel may reach another device: no remote copies, remote signals or barrier semaphores. Data moves between devices by JAX's collectives and lax.ppermute only.
A program may use at most 64 MiB of HBM per device.

v0:
```python
import jax
import jax.numpy as jnp
from jax import lax
from jax.sharding import PartitionSpec as P

ITERS = 3


highest = lax.Precision.HIGHEST


def from_behind(block, axis, distance):
    devices = range(lax.axis_size(axis))
    route = [(i - distance, i) for i in devices if i - distance in devices]
    return lax.ppermute(block, axis, route)


def copy_for_each(x, axis):
    copies = jnp.broadcast_to(x, (lax.axis_size(axis), *x.shape))
    return lax.all_to_all(copies, axis, split_axis=0, concat_axis=0, tiled=True)


def of_everyone(x, axis):
    everything = copy_for_each(x, axis)
    return jnp.sum(everything, axis=0)


def together(arrays, axis):
    ends = [0]
    for a in arrays:
        ends.append(ends[-1] + a.size)
    so_far = of_everyone(jnp.concatenate([a.ravel() for a in arrays]), axis)
    return tuple((so_far[b:e].reshape(a.shape) for a, b, e in zip(arrays, ends, ends[1:])))


def apply_mass(vector, diag_blocks, couple_blocks, couple_offset):
    fields = vector.shape[0]
    own_tiles = vector.shape[1]
    reach = own_tiles // 2
    own_part = jnp.einsum("tij,ftj->fti", diag_blocks, vector, precision=highest)
    ahead_rim = from_behind(vector[:, :reach], "solid", -1)
    padded = jnp.concatenate([vector, ahead_rim], axis=1)
    picked = jnp.zeros_like(vector)
    for offset in range(1, reach + 1):
        offset_hit = (couple_offset == offset)[None, :, None]
        picked = picked + jnp.where(offset_hit, padded[:, offset : offset + own_tiles], 0.0)
    ahead_part = jnp.einsum("tij,ftj->fti", couple_blocks, picked, precision=highest)
    back_terms = jnp.einsum("tji,ftj->fti", couple_blocks, vector, precision=highest)
    spread = jnp.zeros((fields, own_tiles + reach, vector.shape[2]), jnp.float32)
    for offset in range(1, reach + 1):
        offset_hit = (couple_offset == offset)[None, :, None]
        moved = jnp.where(offset_hit, back_terms, 0.0)
        spread = spread + jnp.pad(moved, ((0, 0), (offset, reach - offset), (0, 0)))
    incoming = from_behind(spread[:, own_tiles:], "solid", 1)
    incoming = jnp.pad(incoming, ((0, 0), (0, own_tiles - reach), (0, 0)))
    return own_part + ahead_part + spread[:, :own_tiles] + incoming


def field_dots(first, second):
    return jnp.sum(first * second, axis=(1, 2))


def two_products(residual, image_field):
    return together((field_dots(residual, residual), field_dots(residual, image_field)), "solid")


def local(
    fluid_flux, margin_blocks, block_fluid, block_solid, diag_blocks, couple_blocks, couple_offset
):
    fields = fluid_flux.shape[0]
    tile_width = fluid_flux.shape[2]
    owners = lax.axis_size("solid")
    own_tiles = diag_blocks.shape[0]
    block_count = block_fluid.shape[0]
    chosen = jnp.take(fluid_flux, block_fluid, axis=1)
    block_terms = jnp.einsum(
        "fbi,bij->bfj", chosen, margin_blocks, preferred_element_type=jnp.float32
    )
    capacity = 5 * block_count // (2 * owners)
    target = block_solid // own_tiles
    local_tile = block_solid - target * own_tiles
    owner_hits = (target[:, None] == jnp.arange(owners, dtype=jnp.int32)[None, :]).astype(jnp.int32)
    slot_rank = jnp.sum((jnp.cumsum(owner_hits, axis=0) - owner_hits) * owner_hits, axis=1)
    slot_index = target * capacity + slot_rank
    values = (
        jnp.zeros((owners * capacity, fields, tile_width), jnp.float32)
        .at[slot_index]
        .set(block_terms)
    )
    labels = jnp.full((owners * capacity,), -1, jnp.int32).at[slot_index].set(local_tile)
    values = values.reshape(owners, capacity, fields, tile_width)
    labels = labels.reshape(owners, capacity)
    values, labels = (
        lax.all_to_all(values, "solid", split_axis=0, concat_axis=0, tiled=True),
        lax.all_to_all(labels, "solid", split_axis=0, concat_axis=0, tiled=True),
    )
    onehot = (
        labels.reshape(-1)[None, :] == jnp.arange(own_tiles, dtype=jnp.int32)[:, None]
    ).astype(jnp.float32)
    partial_value = jnp.einsum(
        "tk,kfj->tfj", onehot, values.reshape(-1, fields, tile_width), precision=highest
    )
    mapped = of_everyone(partial_value, "fluid").transpose(1, 0, 2)
    solution = jnp.zeros_like(mapped)
    residual = mapped
    image_field = apply_mass(residual, diag_blocks, couple_blocks, couple_offset)
    norm_now, product = two_products(residual, image_field)
    step_size = norm_now / product
    direction = residual
    along = image_field
    for iteration in range(ITERS):
        solution = solution + step_size[:, None, None] * direction
        residual = residual - step_size[:, None, None] * along
        if iteration + 1 < ITERS:
            image_field = apply_mass(residual, diag_blocks, couple_blocks, couple_offset)
            norm_next, product = two_products(residual, image_field)
            beta_ratio = norm_next / norm_now
            step_size = norm_next / (product - beta_ratio * norm_next / step_size)
            direction = residual + beta_ratio[:, None, None] * direction
            along = image_field + beta_ratio[:, None, None] * along
            norm_now = norm_next
    return (mapped, solution)


def solution(mesh):
    in_specs = (
        P(None, ("fluid", "solid"), None),
        P(("fluid", "solid"), None, None),
        P(("fluid", "solid")),
        P(("fluid", "solid")),
        P("solid", None, None),
        P("solid", None, None),
        P("solid"),
    )
    out_specs = (P(None, "solid", None), P(None, "solid", None))
    return jax.shard_map(local, mesh=mesh, in_specs=in_specs, out_specs=out_specs, check_vma=False)
```

profile of v0, /device:TPU:1, one launch (start us, length us, event | category | flops | bytes accessed | tf_op | source)
XLA Modules:
  0.0 147.9 jit_solution(4399738794461743685)
XLA Ops:
  0.6 0.0 copy-start
  0.6 0.8 multiply_subtract_fusion.2
  1.5 0.6 reduce-window.6
  2.1 0.2 slice_reduce_fusion
  2.3 0.1 bitcast_bitcast_fusion
  2.5 1.1 scatter_custom_fusion
  3.6 0.7 all_to_all.24
  4.3 9.4 %all-to-all-start = ((s32[32,1,12]{2,1,0:T(1,128)}), s32[32,1,12]{2,1,0:T(1,128)S(1)}, u32[]{:S(2)}, u32[]{:S(2)}) async-start(s32[32,1,12]{2,1,0:T(1,128)} %bitcast.1), calls=%async_computation | async-start | bytes 32768 | tf_op jit(solution)/shard_map/all_to_all | solution.py:95
  13.7 0.7 compare_select_fusion
  14.4 0.7 compare_and_fusion
  15.1 2.2 %gather_fusion = bf16[160,3,128]{2,0,1:T(8,128)(2,1)S(1)} fusion(bf16[3,64,128]{2,1,0:T(8,128)(2,1)} %param.7, s32[1024]{0:T(1024)S(1)} %pad_clamp_fusion), kind=kCustom, calls=%fused_computation | custom fusion | bytes 246400 | tf_op jit(solution)/shard_map/jit(_take)/gather | solution.py:75
  17.3 0.1 select_bitcast_fusion
  17.4 3.9 %fusion.11 = f32[160,3,128]{2,1,0:T(4,128)S(1)} fusion(bf16[160,128,128]{2,1,0:T(8,128)(2,1)} %param.8, bf16[3,160,128]{2,1,0:T(8,128)(2,1)S(1)} %select_bitcast_fusion), kind=kOutput, calls=%fused_computation.107 | convolution fusion | flops 15728640 | bytes 5611520 | tf_op jit(solution)/shard_map/fbi,bij->bfj/dot_general | solution.py:76
  21.3 0.1 broadcast_in_dim.599
  21.4 5.3 %scatter_fusion = f32[384,3,128]{2,1,0:T(4,128)S(1)} fusion(f32[384,3,128]{2,1,0:T(4,128)S(1)} %broadcast_in_dim.599, s32[160]{0:T(256)S(1)} %compare_select_fusion.1, f32[160,3,128]{2,1,0:T(4,128)S(1)} %fusion.11), kind=kCustom, calls=%fused_computation.2 | custom fusion | bytes 737920 | tf_op jit(solution)/shard_map/scatter | solution.py:88
  26.7 1.0 copy.67
  27.7 7.4 %all-to-all-start.1 = ((f32[32,12,3,128]{3,1,2,0:T(8,128)}), f32[32,12,3,128]{3,1,2,0:T(8,128)S(1)}, u32[]{:S(2)}, u32[]{:S(2)}) async-start(f32[32,12,3,128]{3,1,2,0:T(8,128)} %copy.67), calls=%async_computation.1 | async-start | bytes 1572864 | tf_op jit(solution)/shard_map/all_to_all | solution.py:94
  35.1 0.5 broadcast.365
  35.6 0.7 reduce.8
  36.3 0.1 eq.59
  36.4 12.9 %all-to-all-done.1 = f32[32,12,3,128]{3,1,2,0:T(8,128)S(1)} async-done(((f32[32,12,3,128]{3,1,2,0:T(8,128)}), f32[32,12,3,128]{3,1,2,0:T(8,128)S(1)}, u32[]{:S(2)}, u32[]{:S(2)}) %all-to-all-start.1) | async-done | bytes 589856 | tf_op jit(solution)/shard_map/all_to_all | solution.py:94
  49.3 0.9 copy.68
  50.2 1.2 reshape.69
  51.4 0.3 fusion.177
  51.7 0.7 broadcast_in_dim.603
  52.4 4.2 %all-to-all-start.2 = ((f32[4,32,3,128]{3,1,2,0:T(8,128)}), f32[4,32,3,128]{3,1,2,0:T(8,128)S(1)}, u32[]{:S(2)}, u32[]{:S(2)}) async-start(f32[4,32,3,128]{3,1,2,0:T(8,128)} %broadcast_in_dim.603), calls=%async_computation.2 | async-start | bytes 393216 | tf_op jit(solution)/shard_map/all_to_all | solution.py:20
  56.6 5.7 %all-to-all-done.2 = f32[4,32,3,128]{3,1,2,0:T(8,128)S(1)} async-done(((f32[4,32,3,128]{3,1,2,0:T(8,128)}), f32[4,32,3,128]{3,1,2,0:T(8,128)S(1)}, u32[]{:S(2)}, u32[]{:S(2)}) %all-to-all-start.2) | async-done | bytes 196640 | tf_op jit(solution)/shard_map/all_to_all | solution.py:20
  62.4 2.1 %select_bitcast_fusion.48 = (f32[3,32,128]{2,0,1:T(4,128)S(1)}, f32[3,32,128]{2,0,1:T(4,128)S(1)}, f32[3,32,128]{2,0,1:T(4,128)S(1)}, f32[3,32,128]{2,0,1:T(4,12...) fusion(pred[32]{0:T(512)(128)(4,1)S(1)} %get-tuple-element.77, ...), kind=kOutput, calls=%fused_computation.313 | convolution fusion | flops 19070976 | bytes 2933248 | tf_op jit(solution)/shard_map/tji,ftj->fti/dot_general | solution.py:48
  64.5 0.1 pad_add_fusion.2
  64.7 3.2 %collective-permute-start.1 = (f32[3,16,128]{2,0,1:T(4,128)S(1)}, f32[3,16,128]{2,0,1:T(4,128)S(1)}, u32[]{:S(2)}, u32[]{:S(2)}) collective-permute-start(f32[3,16,128]{2,0,1:T(4,128)S(1)} %slice.300), channel_id=1, source_target_pairs={{0,1},{1,2},{2,3},{3,4},{4,5},{5,6},{6,7},{7,8},{8,9},{9,10},{10,1... | collective-permute-start | bytes 73736 | tf_op jit(solution)/shard_map/ppermute | solution.py:15
  67.8 1.9 %collective-permute-start = (f32[3,16,128]{2,0,1:T(4,128)S(1)}, f32[3,16,128]{2,0,1:T(4,128)S(1)}, u32[]{:S(2)}, u32[]{:S(2)}) collective-permute-start(f32[3,16,128]{2,0,1:T(4,128)S(1)} %slice.268), channel_id=1, source_target_pairs={{1,0},{2,1},{3,2},{4,3},{5,4},{6,5},{7,6},{8,7},{9,8},{10,9},{11,1... | collective-permute-start | bytes 73736 | tf_op jit(solution)/shard_map/ppermute | solution.py:15
  69.8 3.4 %fusion.234 = f32[32,3,128]{2,1,0:T(4,128)S(1)} fusion(f32[32,128,128]{2,1,0:T(8,128)S(1)} %copy-done.1, f32[32,3,128]{2,0,1:T(8,128)S(1)} %reduce_sum.100), kind=kOutput, calls=%fused_computation.384 | convolution fusion | flops 18874368 | bytes 2195456 | tf_op jit(solution)/shard_map/tij,ftj->fti/dot_general | solution.py:40
  73.1 3.6 %multiply_reduce_fusion.4 = (f32[3]{0:T(128)S(1)}, f32[3]{0:T(128)S(1)}, f32[3,32,128]{2,0,1:T(4,128)S(1)}) fusion(f32[32,3,128]{2,0,1:T(8,128)S(1)} %reduce_sum.100, f32[3,16,128]{2,0,1:T(4,128)S(1)} %collective-permute-done.1, f32[3,48,128]{2,0,1:T(4,128)S(1)} %pad_add_fusion.2, f32[32,3,128]{2,1,0:T(4,128)S(1)} %fusion.234, ...), kind=kOutput, calls=%fused_computation.314 | convolution fusion | flops 19537914 | bytes 2392600 | tf_op jit(solution)/shard_map/tij,ftj->fti/dot_general | solution.py:47
  76.7 0.1 pad_maximum_fusion.3
  76.8 14.3 %all_to_all.37 = f32[32,1,6]{2,1,0:T(1,128)S(1)} all-to-all(f32[32,1,6]{2,1,0:T(1,128)S(1)} %broadcast_in_dim.638), channel_id=1, replica_groups=mesh['fluid'=4,'solid'=32] {'solid'}, dimensions={0} | all-to-all | bytes 1536 | tf_op jit(solution)/shard_map/all_to_all | solution.py:20
  91.2 0.1 reduce_sum.103
  91.2 0.1 slice_divide_fusion.1
  91.3 0.1 multiply_subtract_fusion.1
  91.4 2.2 %select_bitcast_fusion.32 = (f32[3,32,128]{2,0,1:T(4,128)S(1)}, f32[3,32,128]{2,0,1:T(4,128)S(1)}, f32[3,32,128]{2,0,1:T(4,128)S(1)}, f32[3,32,128]{2,0,1:T(4,12...) fusion(pred[32]{0:T(512)(128)(4,1)S(1)} %get-tuple-element.77, ...), kind=kOutput, calls=%fused_computation.294 | convolution fusion | flops 19070976 | bytes 2933248 | tf_op jit(solution)/shard_map/tji,ftj->fti/dot_general | solution.py:48
  93.6 2.6 %collective-permute-start.2 = (f32[3,16,128]{2,0,1:T(4,128)S(1)}, f32[3,16,128]{2,0,1:T(4,128)S(1)}, u32[]{:S(2)}, u32[]{:S(2)}) collective-permute-start(f32[3,16,128]{2,0,1:T(4,128)S(1)} %slice.301), channel_id=1, source_target_pairs={{1,0},{2,1},{3,2},{4,3},{5,4},{6,5},{7,6},{8,7},{9,8},{10,9},{11,1... | collective-permute-start | bytes 73736 | tf_op jit(solution)/shard_map/ppermute | solution.py:15
  96.1 0.1 pad_add_fusion.1
  96.3 3.1 %collective-permute-start.3 = (f32[3,16,128]{2,0,1:T(4,128)S(1)}, f32[3,16,128]{2,0,1:T(4,128)S(1)}, u32[]{:S(2)}, u32[]{:S(2)}) collective-permute-start(f32[3,16,128]{2,0,1:T(4,128)S(1)} %slice.333), channel_id=1, source_target_pairs={{0,1},{1,2},{2,3},{3,4},{4,5},{5,6},{6,7},{7,8},{8,9},{9,10},{10,1... | collective-permute-start | bytes 73736 | tf_op jit(solution)/shard_map/ppermute | solution.py:15
  99.4 3.4 %fusion.67 = f32[32,3,128]{2,1,0:T(4,128)S(1)} fusion(f32[32,128,128]{2,1,0:T(8,128)S(1)} %copy-done, f32[3,32,128]{2,0,1:T(4,128)S(1)} %multiply_subtract_fusion.1, f32[3,16,128]{2,0,1:T(4,128)S(1)} %collective-permute-done.2, pred[32]{0:T(512)(128)(4,1)S(1)} %get-tuple-element.91, pred[32]{0:T(512)(128)(4,1)S(1)} %get-tuple-element.92, ...), kind=kOutput, calls=%fused_computation.162 | convolution fusion | flops 19451904 | bytes 2220544 | tf_op jit(solution)/shard_map/tij,ftj->fti/dot_general | solution.py:47
  102.9 3.5 %multiply_reduce_fusion.2 = (f32[3]{0:T(128)S(1)}, f32[3]{0:T(128)S(1)}, f32[3,32,128]{2,0,1:T(4,128)S(1)}) fusion(f32[3,32,128]{2,0,1:T(4,128)S(1)} %multiply_subtract_fusion.1, f32[3,16,128]{2,0,1:T(4,128)S(1)} %collective-permute-done.3, f32[3,48,128]{2,0,1:T(4,128)S(1)} %pad_add_fusion.1, f32[32,3,128]{2,1,0:T(4,128)S(1)} %fusion.67, ...), kind=kOutput, calls=%fused_computation.295 | convolution fusion | flops 18960378 | bytes 2441240 | tf_op jit(solution)/shard_map/tij,ftj->fti/dot_general | solution.py:40
  106.4 0.1 pad_maximum_fusion.4
  106.5 12.1 %all_to_all.38 = f32[32,1,6]{2,1,0:T(1,128)S(1)} all-to-all(f32[32,1,6]{2,1,0:T(1,128)S(1)} %broadcast_in_dim.639), channel_id=1, replica_groups=mesh['fluid'=4,'solid'=32] {'solid'}, dimensions={0} | all-to-all | bytes 1536 | tf_op jit(solution)/shard_map/all_to_all | solution.py:20
  118.6 0.1 reduce_sum.106
  118.7 0.1 slice_divide_fusion.3
  118.7 0.2 multiply_reduce_fusion
  119.0 2.2 %select_bitcast_fusion.16 = (f32[3,32,128]{2,0,1:T(4,128)S(1)}, f32[3,32,128]{2,0,1:T(4,128)S(1)}, f32[3,32,128]{2,0,1:T(4,128)S(1)}, f32[3,32,128]{2,0,1:T(4,12...) fusion(pred[32]{0:T(512)(128)(4,1)S(1)} %get-tuple-element.77, ...), kind=kOutput, calls=%fused_computation.275 | convolution fusion | flops 19070976 | bytes 2933248 | tf_op jit(solution)/shard_map/tji,ftj->fti/dot_general | solution.py:48
  121.2 2.6 %collective-permute-start.4 = (f32[3,16,128]{2,0,1:T(4,128)S(1)}, f32[3,16,128]{2,0,1:T(4,128)S(1)}, u32[]{:S(2)}, u32[]{:S(2)}) collective-permute-start(f32[3,16,128]{2,0,1:T(4,128)S(1)} %slice.334), channel_id=1, source_target_pairs={{1,0},{2,1},{3,2},{4,3},{5,4},{6,5},{7,6},{8,7},{9,8},{10,9},{11,1... | collective-permute-start | bytes 73736 | tf_op jit(solution)/shard_map/ppermute | solution.py:15
  123.7 0.1 pad_add_fusion
  123.9 3.2 %collective-permute-start.5 = (f32[3,16,128]{2,0,1:T(4,128)S(1)}, f32[3,16,128]{2,0,1:T(4,128)S(1)}, u32[]{:S(2)}, u32[]{:S(2)}) collective-permute-start(f32[3,16,128]{2,0,1:T(4,128)S(1)} %slice.366), channel_id=1, source_target_pairs={{0,1},{1,2},{2,3},{3,4},{4,5},{5,6},{6,7},{7,8},{8,9},{9,10},{10,1... | collective-permute-start | bytes 73736 | tf_op jit(solution)/shard_map/ppermute | solution.py:15
  127.1 3.4 %fusion.243 = f32[32,3,128]{2,1,0:T(4,128)S(1)} fusion(f32[3,32,128]{2,0,1:T(4,128)S(1)} %get-tuple-element.23, f32[32,128,128]{2,1,0:T(8,128)S(1)} %copy-done.3), kind=kOutput, calls=%fused_computation.424 | convolution fusion | flops 18874368 | bytes 2195456 | tf_op jit(solution)/shard_map/tij,ftj->fti/dot_general | solution.py:40
  130.5 3.6 %fusion.10 = f32[3]{0:T(128)S(1)} fusion(f32[3,32,128]{2,0,1:T(4,128)S(1)} %get-tuple-element.23, f32[32,3,128]{2,1,0:T(4,128)S(1)} %fusion.243, f32[32,128,128]{2,1,0:T(8,128)S(1)} %copy-done, f32[3,16,128]{2,0,1:T(4,128)S(1)} %collective-permute-done.4, f32[3,48,128]{2,0,1:T(4,128)S(1)} %pad_add_fusion, f32[3,16,128]{2,0,1:T(4,128)S(1)} %collective-permute-done.5, ...), kind=kOutput, calls=%fused_computation.16 | convolution fusion | flops 19513340 | bytes 2433036 | tf_op jit(solution)/shard_map/tij,ftj->fti/dot_general | solution.py:47
  134.0 0.1 pad_maximum_fusion.5
  134.1 0.6 broadcast_in_dim.640
  134.7 5.4 %all-to-all-start.5 = ((f32[32,1,6]{2,1,0:T(1,128)}), f32[32,1,6]{2,1,0:T(1,128)S(1)}, u32[]{:S(2)}, u32[]{:S(2)}) async-start(f32[32,1,6]{2,1,0:T(1,128)} %broadcast_in_dim.640), calls=%async_computation.5 | async-start | bytes 32768 | tf_op jit(solution)/shard_map/all_to_all | solution.py:20
  140.1 0.6 copy.73
  140.8 6.2 %all-to-all-done.5 = f32[32,1,6]{2,1,0:T(1,128)S(1)} async-done(((f32[32,1,6]{2,1,0:T(1,128)}), f32[32,1,6]{2,1,0:T(1,128)S(1)}, u32[]{:S(2)}, u32[]{:S(2)}) %all-to-all-start.5) | async-done | bytes 800 | tf_op jit(solution)/shard_map/all_to_all | solution.py:20
  147.0 0.1 reduce_sum.109
  147.1 0.1 subtract_divide_fusion
  147.1 0.1 multiply_add_fusion
  147.3 0.6 copy.74
  (34 shorter events, 0.3 us)
Async XLA Ops:
  0.6 61.7 %copy-start = (f32[32,128,128]{2,1,0:T(8,128)S(1)}, f32[32,128,128]{2,1,0:T(8,128)}, u32[]{:S(2)}) copy-start(f32[32,128,128]{2,1,0:T(8,128)} %param.12) | copy-start | bytes 6291460
  4.3 23.4 %all-to-all-start = ((s32[32,1,12]{2,1,0:T(1,128)}), s32[32,1,12]{2,1,0:T(1,128)S(1)}, u32[]{:S(2)}, u32[]{:S(2)}) async-start(s32[32,1,12]{2,1,0:T(1,128)} %bitcast.1), calls=%async_computation | async-start | bytes 32768 | tf_op jit(solution)/shard_map/all_to_all | solution.py:95
  27.7 21.6 %all-to-all-start.1 = ((f32[32,12,3,128]{3,1,2,0:T(8,128)}), f32[32,12,3,128]{3,1,2,0:T(8,128)S(1)}, u32[]{:S(2)}, u32[]{:S(2)}) async-start(f32[32,12,3,128]{3,1,2,0:T(8,128)} %copy.67), calls=%async_computation.1 | async-start | bytes 1572864 | tf_op jit(solution)/shard_map/all_to_all | solution.py:94
  36.4 20.3 %copy-start.4 = (s32[32]{0:T(128)S(1)}, s32[32]{0:T(128)}, u32[]{:S(2)}) copy-start(s32[32]{0:T(128)} %param.13) | copy-start | bytes 388
  52.4 9.9 %all-to-all-start.2 = ((f32[4,32,3,128]{3,1,2,0:T(8,128)}), f32[4,32,3,128]{3,1,2,0:T(8,128)S(1)}, u32[]{:S(2)}, u32[]{:S(2)}) async-start(f32[4,32,3,128]{3,1,2,0:T(8,128)} %broadcast_in_dim.603), calls=%async_computation.2 | async-start | bytes 393216 | tf_op jit(solution)/shard_map/all_to_all | solution.py:20
  62.4 7.4 %copy-start.1 = (f32[32,128,128]{2,1,0:T(8,128)S(1)}, f32[32,128,128]{2,1,0:T(8,128)}, u32[]{:S(2)}) copy-start(f32[32,128,128]{2,1,0:T(8,128)} %param.11) | copy-start | bytes 6291460
  64.7 8.5 %collective-permute-start.1 = (f32[3,16,128]{2,0,1:T(4,128)S(1)}, f32[3,16,128]{2,0,1:T(4,128)S(1)}, u32[]{:S(2)}, u32[]{:S(2)}) collective-permute-start(f32[3,16,128]{2,0,1:T(4,128)S(1)} %slice.300), channel_id=1, source_target_pairs={{0,1},{1,2},{2,3},{3,4},{4,5},{5,6},{6,7},{7,8},{8,9},{9,10},{10,1... | collective-permute-start | bytes 73736 | tf_op jit(solution)/shard_map/ppermute | solution.py:15
  67.8 5.3 %collective-permute-start = (f32[3,16,128]{2,0,1:T(4,128)S(1)}, f32[3,16,128]{2,0,1:T(4,128)S(1)}, u32[]{:S(2)}, u32[]{:S(2)}) collective-permute-start(f32[3,16,128]{2,0,1:T(4,128)S(1)} %slice.268), channel_id=1, source_target_pairs={{1,0},{2,1},{3,2},{4,3},{5,4},{6,5},{7,6},{8,7},{9,8},{10,9},{11,1... | collective-permute-start | bytes 73736 | tf_op jit(solution)/shard_map/ppermute | solution.py:15
  93.6 5.9 %collective-permute-start.2 = (f32[3,16,128]{2,0,1:T(4,128)S(1)}, f32[3,16,128]{2,0,1:T(4,128)S(1)}, u32[]{:S(2)}, u32[]{:S(2)}) collective-permute-start(f32[3,16,128]{2,0,1:T(4,128)S(1)} %slice.301), channel_id=1, source_target_pairs={{1,0},{2,1},{3,2},{4,3},{5,4},{6,5},{7,6},{8,7},{9,8},{10,9},{11,1... | collective-permute-start | bytes 73736 | tf_op jit(solution)/shard_map/ppermute | solution.py:15
  96.1 6.7 %copy-start.2 = (f32[32,128,128]{2,1,0:T(8,128)S(1)}, f32[32,128,128]{2,1,0:T(8,128)}, u32[]{:S(2)}) copy-start(f32[32,128,128]{2,1,0:T(8,128)} %param.11) | copy-start | bytes 6291460
  96.3 6.6 %collective-permute-start.3 = (f32[3,16,128]{2,0,1:T(4,128)S(1)}, f32[3,16,128]{2,0,1:T(4,128)S(1)}, u32[]{:S(2)}, u32[]{:S(2)}) collective-permute-start(f32[3,16,128]{2,0,1:T(4,128)S(1)} %slice.333), channel_id=1, source_target_pairs={{0,1},{1,2},{2,3},{3,4},{4,5},{5,6},{6,7},{7,8},{8,9},{9,10},{10,1... | collective-permute-start | bytes 73736 | tf_op jit(solution)/shard_map/ppermute | solution.py:15
  119.0 8.1 %copy-start.3 = (f32[32,128,128]{2,1,0:T(8,128)S(1)}, f32[32,128,128]{2,1,0:T(8,128)}, u32[]{:S(2)}) copy-start(f32[32,128,128]{2,1,0:T(8,128)} %param.11) | copy-start | bytes 6291460
  121.2 9.3 %collective-permute-start.4 = (f32[3,16,128]{2,0,1:T(4,128)S(1)}, f32[3,16,128]{2,0,1:T(4,128)S(1)}, u32[]{:S(2)}, u32[]{:S(2)}) collective-permute-start(f32[3,16,128]{2,0,1:T(4,128)S(1)} %slice.334), channel_id=1, source_target_pairs={{1,0},{2,1},{3,2},{4,3},{5,4},{6,5},{7,6},{8,7},{9,8},{10,9},{11,1... | collective-permute-start | bytes 73736 | tf_op jit(solution)/shard_map/ppermute | solution.py:15
  123.9 6.6 %collective-permute-start.5 = (f32[3,16,128]{2,0,1:T(4,128)S(1)}, f32[3,16,128]{2,0,1:T(4,128)S(1)}, u32[]{:S(2)}, u32[]{:S(2)}) collective-permute-start(f32[3,16,128]{2,0,1:T(4,128)S(1)} %slice.366), channel_id=1, source_target_pairs={{0,1},{1,2},{2,3},{3,4},{4,5},{5,6},{6,7},{7,8},{8,9},{9,10},{10,1... | collective-permute-start | bytes 73736 | tf_op jit(solution)/shard_map/ppermute | solution.py:15
  134.7 12.3 %all-to-all-start.5 = ((f32[32,1,6]{2,1,0:T(1,128)}), f32[32,1,6]{2,1,0:T(1,128)S(1)}, u32[]{:S(2)}, u32[]{:S(2)}) async-start(f32[32,1,6]{2,1,0:T(1,128)} %broadcast_in_dim.640), calls=%async_computation.5 | async-start | bytes 32768 | tf_op jit(solution)/shard_map/all_to_all | solution.py:20
where the time goes:
time: 149 us; the launch traced here: 148 us
  starting transfers between devices  43 us (29%)
  matrix products  31.6 us (21%)
  blocking collectives  26.5 us (18%)
  waiting for transfers between devices  24.8 us (17%)
  local copies, waits for them, and re-layouts  16 us (11%)
  other arithmetic  5.14 us (3%)
    all_to_all x2, blocking collectives, copy_for_each(): return lax.all_to_all(copies, axis, split_axis=0, concat_axis=0, tiled=True)  26.5 us
    ppermute x6, starting transfers between devices, from_behind(): return lax.ppermute(block, axis, route)  16.6 us
    all_to_all x1, waiting for transfers between devices, local(): lax.all_to_all(values, 'solid', split_axis=0, concat_axis=0, tiled=True)  12.9 us
    all_to_all x2, waiting for transfers between devices, copy_for_each(): return lax.all_to_all(copies, axis, split_axis=0, concat_axis=0, tiled=True)  11.9 us
    dot_general x3, matrix products, apply_mass(): jnp.einsum('tij,ftj->fti', couple_blocks, picked, precision=highest)  10.6 us
    dot_general x3, matrix products, apply_mass(): jnp.einsum('tij,ftj->fti', diag_blocks, vector, precision=highest)  10.2 us
    all_to_all x2, starting transfers between devices, copy_for_each(): return lax.all_to_all(copies, axis, split_axis=0, concat_axis=0, tiled=True)  9.58 us
    all_to_all x1, starting transfers between devices, local(): lax.all_to_all(labels, 'solid', split_axis=0, concat_axis=0, tiled=True)  9.43 us
  transfers between devices with their start and end apart: 10, of which 3 were waited for; matrix products, arithmetic and copies ran while one was open for 18% of the time, Pallas kernels for 0%

commit v1 on v0

v1 whole, which is shorter than its diff:
```python
import functools

import jax
import jax.numpy as jnp
from jax import lax
from jax.experimental import pallas as pl
from jax.experimental.pallas import tpu as pltpu
from jax.sharding import PartitionSpec as P

F32 = jnp.float32
BF16 = jnp.bfloat16
LANES = 128
ROWS = 4
SHIFT = 10.5
MOMENTS = 6
VMEM = pl.BlockSpec(memory_space=pltpu.VMEM)
SMEM = pl.BlockSpec(memory_space=pltpu.SMEM)


def dot(a, b, contract=(1, 0)):
    return lax.dot_general(
        a, b, (((contract[0],), (contract[1],)), ((), ())), preferred_element_type=F32
    )


def split(x):
    high = x.astype(BF16).astype(F32)
    return high, x - high


def margin_kernel(step_blocks, owners, capacity, own_tiles, fluid_ids, solid_ids, flux, blocks, out, fields, count):
    step = pl.program_id(0)
    chunk = capacity * ROWS
    lane = lax.broadcasted_iota(jnp.int32, (1, LANES), 1)
    lane_slot = jnp.where(lane % ROWS < 3, lane // ROWS, -1)
    lane_field = lane % ROWS

    @pl.when(step == 0)
    def _():
        out[...] = jnp.zeros_like(out)
        fields[...] = jnp.zeros_like(fields)
        tiles = flux.shape[1]
        for f in range(3):
            fields[pl.ds(f, tiles, stride=ROWS), :] = flux[f].astype(F32)
        for owner in range(owners):
            count[owner] = 0
            out[pl.ds(owner * chunk + 3, 1), :] = jnp.full((1, LANES), -1.0, F32)

    for k in range(step_blocks):
        block = step * step_blocks + k
        fluid = fluid_ids[block]
        solid = solid_ids[block]
        owner = solid // own_tiles
        tile = solid - owner * own_tiles
        rank = count[owner]
        count[owner] = rank + 1
        base = owner * chunk
        picked = fields[pl.ds(pl.multiple_of(fluid * ROWS, ROWS), ROWS), :]
        term = dot(picked.astype(BF16), blocks[k])
        for f in range(3):
            out[pl.ds(base + rank * ROWS + f, 1), :] = term[f : f + 1]
        label = out[pl.ds(base + 3, 1), :]
        own_label = (tile * ROWS + lane_field).astype(F32)
        out[pl.ds(base + 3, 1), :] = jnp.where(lane_slot == rank, own_label, label)


def margin(fluid_ids, solid_ids, flux, blocks, owners, own_tiles, capacity):
    total = blocks.shape[0]
    step_blocks = 16
    return pl.pallas_call(
        functools.partial(margin_kernel, step_blocks, owners, capacity, own_tiles),
        out_shape=jax.ShapeDtypeStruct((owners * capacity * ROWS, LANES), F32),
        grid_spec=pltpu.PrefetchScalarGridSpec(
            num_scalar_prefetch=2,
            grid=(total // step_blocks,),
            in_specs=[
                pl.BlockSpec(flux.shape, lambda i, *_: (0, 0, 0)),
                pl.BlockSpec((step_blocks, LANES, LANES), lambda i, *_: (i, 0, 0)),
            ],
            out_specs=pl.BlockSpec((owners * capacity * ROWS, LANES), lambda i, *_: (0, 0)),
            scratch_shapes=[
                pltpu.VMEM((flux.shape[1] * ROWS, LANES), F32),
                pltpu.SMEM((owners,), jnp.int32),
            ],
        ),
        compiler_params=pltpu.CompilerParams(vmem_limit_bytes=16 << 20),
        name="margin",
    )(fluid_ids, solid_ids, flux, blocks)


def prepare_kernel(diag, couple, both, turned):
    row = lax.broadcasted_iota(jnp.int32, (LANES, LANES), 0)
    column = lax.broadcasted_iota(jnp.int32, (LANES, LANES), 1)
    shift = jnp.where(row == column, SHIFT, 0.0).astype(F32)
    for t in range(diag.shape[0]):
        high, low = split(diag[t] - shift)
        both[t, 0:LANES, 0:LANES] = high.astype(BF16)
        both[t, LANES : 2 * LANES, 0:LANES] = low.astype(BF16)
        high, low = split(couple[t])
        both[t, 0:LANES, LANES : 2 * LANES] = high.astype(BF16)
        both[t, LANES : 2 * LANES, LANES : 2 * LANES] = low.astype(BF16)
        turned[t, 0:LANES, :] = high.T.astype(BF16)
        turned[t, LANES : 2 * LANES, :] = low.T.astype(BF16)


def prepare(diag, couple):
    tiles = diag.shape[0]
    step = 8
    return pl.pallas_call(
        prepare_kernel,
        out_shape=(
            jax.ShapeDtypeStruct((tiles, 2 * LANES, 2 * LANES), BF16),
            jax.ShapeDtypeStruct((tiles, 2 * LANES, LANES), BF16),
        ),
        grid=(tiles // step,),
        in_specs=[pl.BlockSpec((step, LANES, LANES), lambda i: (i, 0, 0))] * 2,
        out_specs=(
            pl.BlockSpec((step, 2 * LANES, 2 * LANES), lambda i: (i, 0, 0)),
            pl.BlockSpec((step, 2 * LANES, LANES), lambda i: (i, 0, 0)),
        ),
        compiler_params=pltpu.CompilerParams(vmem_limit_bytes=16 << 20),
        cost_estimate=pl.CostEstimate(flops=1 << 26, bytes_accessed=10 << 20, transcendentals=0),
        name="prepare",
    )(diag, couple)


def combine_kernel(owners, received, out):
    chunk = received.shape[0] // owners
    row = lax.broadcasted_iota(jnp.int32, (out.shape[0], chunk), 0).astype(F32)
    total = jnp.zeros(out.shape, F32)
    for source in range(owners):
        values = received[source * chunk : (source + 1) * chunk, :]
        label = received[source * chunk + 3 : source * chunk + 4, 0:chunk]
        hits = (row == label).astype(F32).astype(BF16)
        high, low = split(values)
        total = total + dot(hits, high.astype(BF16)) + dot(hits, low.astype(BF16))
    out[...] = total


def combine(received, owners, own_tiles):
    return pl.pallas_call(
        functools.partial(combine_kernel, owners),
        out_shape=jax.ShapeDtypeStruct((own_tiles * ROWS, LANES), F32),
        in_specs=[VMEM],
        out_specs=VMEM,
        compiler_params=pltpu.CompilerParams(vmem_limit_bytes=16 << 20),
        name="combine",
    )(received)


def put_pairs(pairs, t, value):
    high, low = split(value)
    pairs[t, 0:ROWS, :] = high
    pairs[t, ROWS : 2 * ROWS, :] = low


def load_pairs(pairs, t):
    both = pairs[t].astype(BF16)
    return jnp.concatenate([both, both], axis=1)


def fold(product):
    return product[0:ROWS] + product[ROWS : 2 * ROWS]


def local_part(tiles, offsets, pairs, spread, both, turned):
    spread[...] = jnp.zeros_like(spread)
    for t in range(tiles):
        partner = t + offsets[t]
        ahead = fold(dot(load_pairs(pairs, partner), turned[t]))
        here = fold(dot(load_pairs(pairs, t), both[t]))
        spread[t] = spread[t] + here[:, 0:LANES] + ahead
        spread[partner] = spread[partner] + here[:, LANES : 2 * LANES]


def select(flag, first, second):
    return jnp.where(flag > 0, first, second)


def first_kernel(tiles, halo, offsets, odd, part0, part1, part2, part3, both, turned, mapped, vector, image, near, far, pairs, spread):
    total = (part0[...] + part1[...]) + (part2[...] + part3[...])
    vector[...] = total
    for f in range(3):
        mapped[f] = vector[pl.ds(f, tiles, stride=ROWS), :]
    for t in range(tiles):
        put_pairs(pairs, t, vector[t * ROWS : (t + 1) * ROWS, :])
    for t in range(tiles, tiles + halo):
        pairs[t] = jnp.zeros((2 * ROWS, LANES), F32)
    local_part(tiles, offsets, pairs, spread, both, turned)
    for t in range(tiles):
        image[t * ROWS : (t + 1) * ROWS, :] = spread[t]
    flag = odd[0]
    for t in range(halo):
        rim = vector[t * ROWS : (t + 1) * ROWS, :]
        out = spread[tiles + t]
        near[t * ROWS : (t + 1) * ROWS, :] = select(flag, rim, out)
        far[t * ROWS : (t + 1) * ROWS, :] = select(flag, out, rim)


def finish_part(tiles, halo, offsets, flag, image, near, far, pairs, turned):
    for t in range(halo):
        rows = slice(t * ROWS, (t + 1) * ROWS)
        put_pairs(pairs, tiles + t, select(flag, far[rows, :], near[rows, :]))
    for t in range(tiles - halo, tiles):
        pairs[t] = jnp.zeros((2 * ROWS, LANES), F32)
    values = []
    for t in range(tiles):
        rows = slice(t * ROWS, (t + 1) * ROWS)
        value = image[rows, :]
        if t < halo:
            value = value + select(flag, near[rows, :], far[rows, :])
        if t >= tiles - halo:
            partner = jnp.maximum(t + offsets[t], tiles - halo)
            value = value + fold(dot(load_pairs(pairs, partner), turned[t]))
        values.append(value)
    return values


def second_kernel(tiles, halo, offsets, odd, image, near, far, both, turned, vector, image2, leaving, near2, far2, pairs, spread):
    flag = odd[0]
    values = finish_part(tiles, halo, offsets, flag, image, near, far, pairs, turned)
    for t in range(tiles):
        vector[t * ROWS : (t + 1) * ROWS, :] = values[t]
    for t in range(tiles):
        put_pairs(pairs, t, vector[t * ROWS : (t + 1) * ROWS, :])
    for t in range(tiles, tiles + halo):
        pairs[t] = jnp.zeros((2 * ROWS, LANES), F32)
    local_part(tiles, offsets, pairs, spread, both, turned)
    size = halo * ROWS
    for t in range(tiles):
        image2[t * ROWS : (t + 1) * ROWS, :] = spread[t]
    for t in range(halo):
        leaving[t * ROWS : (t + 1) * ROWS, :] = spread[tiles + t]
    near2[0:size, :] = select(flag, vector[0:size, :], leaving[...])
    far2[0:size, :] = select(flag, leaving[...], vector[0:size, :])
    near2[size : 2 * size, :] = image2[0:size, :]
    far2[size : 2 * size, :] = image2[0:size, :]


def third_kernel(tiles, halo, offsets, odd, last, start, vector1, image, leaving, near, far, both, turned, vector2, out, pairs, product):
    flag = odd[0]
    size = halo * ROWS
    values = finish_part(tiles, halo, offsets, flag, image, near, far, pairs, turned)
    for t in range(tiles):
        vector2[t * ROWS : (t + 1) * ROWS, :] = values[t]
    for t in range(tiles):
        put_pairs(pairs, t, vector2[t * ROWS : (t + 1) * ROWS, :])
    inside = jnp.where(last[0] > 0, 0.0, 1.0).astype(F32)
    for t in range(halo):
        rows = slice(t * ROWS, (t + 1) * ROWS)
        other = slice(size + t * ROWS, size + (t + 1) * ROWS)
        rim = select(flag, far[other, :], near[other, :]) + leaving[rows, :]
        put_pairs(pairs, tiles + t, rim * inside)
    for t in range(tiles):
        ahead = fold(dot(load_pairs(pairs, t + offsets[t]), turned[t]))
        here = fold(dot(load_pairs(pairs, t), both[t, :, 0:LANES]))
        product[t * ROWS : (t + 1) * ROWS, :] = here + 2.0 * ahead
    v0, v1, v2, v3 = start[...], vector1[...], vector2[...], product[...]
    field = lax.broadcasted_iota(jnp.int32, (2 * ROWS, LANES), 0)
    lane = lax.broadcasted_iota(jnp.int32, (2 * ROWS, LANES), 1)
    row = jnp.zeros((2 * ROWS, LANES), F32)
    for k, (a, b) in enumerate(((v0, v0), (v0, v1), (v1, v1), (v1, v2), (v2, v2), (v2, v3))):
        folded = jnp.sum((a * b).reshape(tiles * ROWS // (2 * ROWS), 2 * ROWS, LANES), axis=0)
        moment = jnp.sum(folded, axis=1, keepdims=True)
        row = row + jnp.where(lane == k * ROWS + field % ROWS, moment, 0.0)
    row = jnp.sum(row, axis=0, keepdims=True)
    out[...] = jnp.broadcast_to(row[:, None, :], out.shape)


def last_kernel(tiles, moments, start, vector1, vector2, nodal, mixed):
    total = jnp.sum(moments[...], axis=0)
    total = jnp.broadcast_to(total, (2 * ROWS, LANES))
    g = [total if k == 0 else pltpu.roll(total, LANES - k * ROWS, 1) for k in range(MOMENTS)]
    h = [g[k + 1] + SHIFT * g[k] for k in range(MOMENTS - 1)]

    def form(table, c):
        n = len(c)
        result = None
        for i in range(n):
            for j in range(i, n):
                term = (c[i] * c[j]) * table[i + j]
                term = term if i == j else 2.0 * term
                result = term if result is None else result + term
        return result

    def apply(c):
        n = len(c)
        shifted = [SHIFT * c[0]]
        for i in range(1, n):
            shifted.append(c[i - 1] + SHIFT * c[i])
        return shifted + [c[n - 1]]

    one = jnp.ones_like(total)
    rr = g[0]
    alpha = rr / h[0]
    coefficients = [alpha]
    residual = [one - alpha * SHIFT, -alpha]
    new = form(g, residual)
    beta = new / rr
    direction = [residual[0] + beta, residual[1]]
    rr = new
    alpha = rr / form(h, direction)
    coefficients = [coefficients[0] + alpha * direction[0], alpha * direction[1]]
    image = apply(direction)
    residual = [residual[0] - alpha * image[0], residual[1] - alpha * image[1], -alpha * image[2]]
    new = form(g, residual)
    beta = new / rr
    direction = [residual[0] + beta * direction[0], residual[1] + beta * direction[1], residual[2]]
    rr = new
    alpha = rr / form(h, direction)
    coefficients = [
        coefficients[0] + alpha * direction[0],
        coefficients[1] + alpha * direction[1],
        alpha * direction[2],
    ]
    field = lax.broadcasted_iota(jnp.int32, (2 * ROWS, LANES), 0)
    lane = lax.broadcasted_iota(jnp.int32, (2 * ROWS, LANES), 1)
    result = jnp.zeros(start.shape, F32).reshape(-1, 2 * ROWS, LANES)
    for c, v in zip(coefficients, (start, vector1, vector2)):
        column = jnp.sum(jnp.where(lane == field % ROWS, c, 0.0), axis=1, keepdims=True)
        result = result + column[None] * v[...].reshape(-1, 2 * ROWS, LANES)
    mixed[...] = result.reshape(start.shape)
    for f in range(3):
        nodal[f] = mixed[pl.ds(f, tiles, stride=ROWS), :]


def call(kernel, shapes, smem, vmem, scratch, name, limit=32):
    return pl.pallas_call(
        kernel,
        out_shape=tuple(jax.ShapeDtypeStruct(s, F32) for s in shapes),
        in_specs=[SMEM] * len(smem) + [VMEM] * len(vmem),
        out_specs=tuple(VMEM for _ in shapes),
        scratch_shapes=scratch,
        compiler_params=pltpu.CompilerParams(vmem_limit_bytes=limit << 20),
        name=name,
    )(*smem, *vmem)


def exchange(near, far, axis):
    n = lax.axis_size(axis)
    far_route = [(i, i + 1) for i in range(1, n - 1, 2)] + [(i + 1, i) for i in range(1, n - 1, 2)]
    near_route = [(i, i ^ 1) for i in range(n)]
    return lax.ppermute(near, axis, near_route), lax.ppermute(far, axis, far_route)


def local(fluid_flux, margin_blocks, block_fluid, block_solid, diag_blocks, couple_blocks, couple_offset):
    owners = lax.axis_size("solid")
    groups = lax.axis_size("fluid")
    tiles = diag_blocks.shape[0]
    halo = tiles // 2
    total_blocks = block_fluid.shape[0]
    capacity = 5 * total_blocks // (2 * owners)
    place = lax.axis_index("solid")
    odd = (place % 2).astype(jnp.int32).reshape(1)
    last = (place == owners - 1).astype(jnp.int32).reshape(1)

    sent = margin(block_fluid, block_solid, fluid_flux, margin_blocks, owners, tiles, capacity)
    received = lax.all_to_all(sent, "solid", split_axis=0, concat_axis=0, tiled=True)
    both, turned = prepare(diag_blocks, couple_blocks)
    part = combine(received, owners, tiles)
    parts = [part] + [
        lax.ppermute(part, "fluid", [(i, i ^ d) for i in range(groups)]) for d in (1, 2, 3)
    ]
    whole = (tiles * ROWS, LANES)
    half = (halo * ROWS, LANES)
    pairs = pltpu.VMEM((tiles + halo, 2 * ROWS, LANES), F32)
    spread = pltpu.VMEM((tiles + halo, ROWS, LANES), F32)
    (mapped, start, image, near, far) = call(
        functools.partial(first_kernel, tiles, halo),
        ((3, tiles, LANES), whole, whole, half, half),
        (couple_offset, odd),
        (*parts, both, turned),
        [pairs, spread],
        "first",
    )
    near, far = exchange(near, far, "solid")
    (vector1, image, leaving, near, far) = call(
        functools.partial(second_kernel, tiles, halo),
        (whole, whole, half, whole, whole),
        (couple_offset, odd),
        (image, near, far, both, turned),
        [pairs, spread],
        "second",
    )
    near, far = exchange(near, far, "solid")
    vector2, moments = call(
        functools.partial(third_kernel, tiles, halo),
        (whole, (owners, 1, LANES)),
        (couple_offset, odd, last),
        (start, vector1, image, leaving, near, far, both, turned),
        [pairs, pltpu.VMEM(whole, F32)],
        "third",
    )
    moments = lax.all_to_all(moments, "solid", split_axis=0, concat_axis=0, tiled=True)
    (nodal,) = call(
        functools.partial(last_kernel, tiles),
        ((3, tiles, LANES),),
        (),
        (moments, start, vector1, vector2),
        [pltpu.VMEM(whole, F32)],
        "last",
    )
    return mapped, nodal


def solution(mesh):
    in_specs = (
        P(None, ("fluid", "solid"), None),
        P(("fluid", "solid"), None, None),
        P(("fluid", "solid")),
        P(("fluid", "solid")),
        P("solid", None, None),
        P("solid", None, None),
        P("solid"),
    )
    out_specs = (P(None, "solid", None), P(None, "solid", None))
    return jax.shard_map(local, mesh=mesh, in_specs=in_specs, out_specs=out_specs, check_vma=False)
```

time: 149 us -> 76.4 us (0.51)
  starting transfers between devices: 43 us -> 9.01 us
  matrix products: 31.6 us -> 0 us
  waiting for transfers between devices: 24.8 us -> 6.66 us
  Pallas kernels: 0 us -> 11.7 us
  blocking collectives: 26.5 us -> 37.8 us
  local copies, waits for them, and re-layouts: 16 us -> 10 us
  other arithmetic: 5.14 us -> 0 us
    dot_general x11 -> x0, matrix products: 31.6 us -> none  [the longest x3 10.6 us: apply_mass(): jnp.einsum('tij,ftj->fti', couple_blocks, picked, precision=highest)]
    all_to_all x4 -> x0, starting transfers between devices: 26.4 us -> none  [the longest x2 9.58 us: copy_for_each(): return lax.all_to_all(copies, axis, split_axis=0, concat_axis=0, tiled=True)]
    all_to_all x4 -> x0, waiting for transfers between devices: 24.8 us -> none  [the longest x1 12.9 us: local(): lax.all_to_all(values, 'solid', split_axis=0, concat_axis=0, tiled=True)]
    pallas_call x0 -> x7, Pallas kernels: none -> 11.7 us  [the longest x4 6.37 us: call(): pl.pallas_call(kernel, out_shape=tuple((jax.ShapeDtypeStruct(s, F32) for...]
    all_to_all x2, blocking collectives: 26.5 us -> 37.8 us  [the longest x1 23.5 us: local(): lax.all_to_all(sent, 'solid', split_axis=0, concat_axis=0, tiled=True)]
    unnamed x12 -> x18, local copies, waits for them, and re-layouts: 1.28 us -> 10 us
    ppermute x6 -> x7, starting transfers between devices: 16.6 us -> 9.01 us  [the longest x2 4.11 us: exchange(): lax.ppermute(far, axis, far_route)]
    ppermute x6 -> x7, waiting for transfers between devices: 0.02 us -> 6.66 us  [the longest x2 6.65 us: exchange(): lax.ppermute(far, axis, far_route)]
  transfers between devices with their start and end apart: 10 -> 7, of which waited for: 3 -> 2; matrix products, arithmetic and copies ran while one was open for 18% -> 0% of each run, Pallas kernels for 0% -> 2%
where the time goes in v1:
time: 76.4 us; the launch traced here: 75.9 us
  blocking collectives  37.8 us (49%)
  Pallas kernels  11.7 us (15%)
  local copies, waits for them, and re-layouts  10 us (13%)
  starting transfers between devices  9.01 us (12%)
  waiting for transfers between devices  6.66 us (9%)
  between operations  0.77 us (1%)
    all_to_all x1, blocking collectives, local(): lax.all_to_all(sent, 'solid', split_axis=0, concat_axis=0, tiled=True)  23.5 us
    all_to_all x1, blocking collectives, local(): lax.all_to_all(moments, 'solid', split_axis=0, concat_axis=0, tiled=True)  14.3 us
    unnamed x18, local copies, waits for them, and re-layouts  10 us
    ppermute x2, waiting for transfers between devices, exchange(): lax.ppermute(far, axis, far_route)  6.65 us
    pallas_call x4, Pallas kernels, call(): pl.pallas_call(kernel, out_shape=tuple((jax.ShapeDtypeStruct(s, F32) for...  6.37 us
    ppermute x2, starting transfers between devices, exchange(): lax.ppermute(far, axis, far_route)  4.11 us
    ppermute x3, starting transfers between devices, local(): lax.ppermute(part, 'fluid', [(i, i ^ d) for i in range(groups)])  3.49 us
    pallas_call x1, Pallas kernels, margin(): pl.pallas_call(functools.partial(margin_kernel, step_blocks, owners, capa...  3.3 us
  transfers between devices with their start and end apart: 7, of which 2 were waited for; matrix products, arithmetic and copies ran while one was open for 0% of the time, Pallas kernels for 2%

profile of v1, /device:TPU:1, one launch (start us, length us, event | category | flops | bytes accessed | tf_op | source)
XLA Modules:
  0.0 75.9 jit_solution(17001341187362493009)
XLA Ops:
  0.6 0.0 copy-start.2
  0.6 2.5 %copy-done.2 = bf16[160,128,128]{2,1,0:T(8,128)(2,1)S(1)} copy-done((bf16[160,128,128]{2,1,0:T(8,128)(2,1)S(1)}, bf16[160,128,128]{2,1,0:T(8,128)(2,1)}, u32[]{:S(2)}) %copy-start.2) | copy-done | bytes 5242904
  3.1 0.0 copy-start.5
  3.1 0.8 %copy-done.5 = bf16[3,64,128]{2,1,0:T(8,128)(2,1)S(1)} copy-done((bf16[3,64,128]{2,1,0:T(8,128)(2,1)S(1)}, bf16[3,64,128]{2,1,0:T(8,128)(2,1)}, u32[]{:S(2)}) %copy-start.5) | copy-done | bytes 49176
  3.9 0.0 copy-start.7
  3.9 0.7 copy-done.7
  4.6 0.0 copy-start.8
  4.6 0.7 copy-done.8
  5.3 3.3 %margin.1 = f32[1536,128]{1,0:T(8,128)S(1)} custom-call(s32[160]{0:T(256)S(1)} %copy-done.7, s32[160]{0:T(256)S(1)} %copy-done.8, bf16[3,64,128]{2,1,0:T(8,128)(2,1)S(1)} %copy-done.5, bf16[160,128,128]{2,1,0:T(8,128)(2,1)S(1)} %copy-done.2), custom_call_target="tpu_custom_call" | custom-call | tf_op jit(solution)/shard_map/margin/pallas_call | solution.py:70
  8.6 23.5 %all_to_all.16 = f32[32,48,128]{2,1,0:T(8,128)S(1)} all-to-all(f32[32,48,128]{2,1,0:T(8,128)S(1)} %bitcast.5), channel_id=1, replica_groups=mesh['fluid'=4,'solid'=32] {'solid'}, dimensions={0} | all-to-all | bytes 1572864 | tf_op jit(solution)/shard_map/all_to_all | solution.py:358
  32.0 0.7 combine.1.part0
  32.7 2.8 %collective-permute-start.2 = (f32[128,128]{1,0:T(8,128)S(1)}, f32[128,128]{1,0:T(8,128)S(1)}, u32[]{:S(2)}, u32[]{:S(2)}) collective-permute-start(f32[128,128]{1,0:T(8,128)S(1)} %combine.1.part0), channel_id=1, source_target_pairs={{0,96},{32,64},{64,32},{96,0},{1,97},{33,65},{65,33},{97,1},{2,98}... | collective-permute-start | bytes 196616 | tf_op jit(solution)/shard_map/ppermute | solution.py:362
  35.6 0.3 collective-permute-start.1
  35.9 0.3 collective-permute-start
  36.2 0.0 copy-start.3
  36.2 1.6 %copy-done.3 = f32[32,128,128]{2,1,0:T(8,128)S(1)} copy-done((f32[32,128,128]{2,1,0:T(8,128)S(1)}, f32[32,128,128]{2,1,0:T(8,128)}, u32[]{:S(2)}) %copy-start.3) | copy-done | bytes 2097176
  37.8 0.0 copy-start.4
  37.8 1.6 %copy-done.4 = f32[32,128,128]{2,1,0:T(8,128)S(1)} copy-done((f32[32,128,128]{2,1,0:T(8,128)S(1)}, f32[32,128,128]{2,1,0:T(8,128)}, u32[]{:S(2)}) %copy-start.4) | copy-done | bytes 2097176
  39.4 0.0 copy-start.6
  39.4 1.3 %prepare.1 = (bf16[32,256,256]{2,1,0:T(8,128)(2,1)S(1)}, bf16[32,256,128]{2,1,0:T(8,128)(2,1)S(1)}) custom-call(f32[32,128,128]{2,1,0:T(8,128)S(1)} %copy-done.3, f32[32,128,128]{2,1,0:T(8,128)S(1)} %copy-done.4), custom_call_target="tpu_custom_call" | custom-call | flops 67108864 | bytes 10485760 | tf_op jit(solution)/shard_map/prepare/pallas_call | solution.py:109
  40.7 0.0 copy-start
  40.7 0.0 collective-permute-done.2.part3
  40.8 0.0 collective-permute-done.1.part2
  40.8 0.0 collective-permute-done.part1
  40.8 0.0 copy-done.6
  40.8 2.0 %first.1 = (f32[3,32,128]{2,1,0:T(8,128)}, f32[128,128]{1,0:T(8,128)S(1)}, f32[128,128]{1,0:T(8,128)S(1)}, f32[64,128]{1,0:T(8,128)S(1)}, f32[64,128]{1,0:T(8,128)S(1)}) custom-call(s32[32]{0:T(128)S(1)} %copy-done.6, s32[1]{0:T(128)} %bitcast.odd, f32[128,128]{1,0:T(8,128)S(1)} %combine.1.part0, f32[128,128]{1,0:T(8,128)S(1)} %collective-permute-done.part1, ...), custom_call_target="tpu_custom_call" | custom-call | tf_op jit(solution)/shard_map/first/pallas_call | solution.py:328
  42.8 1.3 %collective-permute-start.3 = (f32[64,128]{1,0:T(8,128)S(1)}, f32[64,128]{1,0:T(8,128)S(1)}, u32[]{:S(2)}, u32[]{:S(2)}) collective-permute-start(f32[64,128]{1,0:T(8,128)S(1)} %get-tuple-element.21), channel_id=1, source_target_pairs={{0,1},{1,0},{2,3},{3,2},{4,5},{5,4},{6,7},{7,6},{8,9},{9,8},{10,11... | collective-permute-start | bytes 98312 | tf_op jit(solution)/shard_map/ppermute | solution.py:343
  44.2 1.9 %collective-permute-start.4 = (f32[64,128]{1,0:T(8,128)S(1)}, f32[64,128]{1,0:T(8,128)S(1)}, u32[]{:S(2)}, u32[]{:S(2)}) collective-permute-start(f32[64,128]{1,0:T(8,128)S(1)} %get-tuple-element.22), channel_id=1, source_target_pairs={{1,2},{3,4},{5,6},{7,8},{9,10},{11,12},{13,14},{15,16},{17,18},{19... | collective-permute-start | bytes 98312 | tf_op jit(solution)/shard_map/ppermute | solution.py:343
  46.1 0.0 collective-permute-done.3.near
  46.1 3.3 %collective-permute-done.4.far = f32[64,128]{1,0:T(8,128)S(1)} collective-permute-done((f32[64,128]{1,0:T(8,128)S(1)}, f32[64,128]{1,0:T(8,128)S(1)}, u32[]{:S(2)}, u32[]{:S(2)}) %collective-permute-start.4) | collective-permute-done | bytes 32800 | tf_op jit(solution)/shard_map/ppermute | solution.py:343
  49.4 0.0 copy-done
  49.4 1.9 %second.1 = (f32[128,128]{1,0:T(8,128)S(1)}, f32[128,128]{1,0:T(8,128)S(1)}, f32[64,128]{1,0:T(8,128)S(1)}, f32[128,128]{1,0:T(8,128)S(1)}, f32[128,128]{1,0:T(8,128)S(1)}) custom-call(s32[32]{0:T(128)S(1)} %copy-done.6, s32[1]{0:T(128)} %bitcast.odd, f32[128,128]{1,0:T(8,128)S(1)} %get-tuple-element.20.image, f32[64,128]{1,0:T(8,128)S(1)} %collective-permute-done.3.near, ...), custom_call_target="tpu_custom_call" | custom-call | tf_op jit(solution)/shard_map/second/pallas_call | solution.py:328
  51.3 0.1 collective-permute-start.5
  51.3 2.2 %collective-permute-start.6 = (f32[128,128]{1,0:T(8,128)S(1)}, f32[128,128]{1,0:T(8,128)S(1)}, u32[]{:S(2)}, u32[]{:S(2)}) collective-permute-start(f32[128,128]{1,0:T(8,128)S(1)} %get-tuple-element.27), channel_id=1, source_target_pairs={{1,2},{3,4},{5,6},{7,8},{9,10},{11,12},{13,14},{15,16},{17,18},{19... | collective-permute-start | bytes 196616 | tf_op jit(solution)/shard_map/ppermute | solution.py:343
  53.6 0.0 collective-permute-done.5.near
  53.6 3.4 %collective-permute-done.6.far = f32[128,128]{1,0:T(8,128)S(1)} collective-permute-done((f32[128,128]{1,0:T(8,128)S(1)}, f32[128,128]{1,0:T(8,128)S(1)}, u32[]{:S(2)}, u32[]{:S(2)}) %collective-permute-start.6) | collective-permute-done | bytes 65568 | tf_op jit(solution)/shard_map/ppermute | solution.py:343
  56.9 0.0 copy-start.1
  56.9 2.2 %copy-done.1 = bf16[32,256,256]{2,1,0:T(8,128)(2,1)S(1)} copy-done((bf16[32,256,256]{2,1,0:T(8,128)(2,1)S(1)}, bf16[32,256,256]{2,1,0:T(8,128)(2,1)}, u32[]{:S(2)}) %copy-start.1) | copy-done | bytes 4194328
  59.1 1.6 %third.1 = (f32[128,128]{1,0:T(8,128)S(1)}, f32[32,1,128]{2,1,0:T(1,128)S(1)}) custom-call(s32[32]{0:T(128)S(1)} %copy-done.6, s32[1]{0:T(128)} %bitcast.odd, s32[1]{0:T(128)} %bitcast.3.last, f32[128,128]{1,0:T(8,128)S(1)} %get-tuple-element.19.start, f32[128,128]{1,0:T(8,128)S(1)} %get-tuple-element.23.vector1, f32[128,128]{1,0:T(8,128)S(1)} %get-tuple-element.24.image, ...), custom_call_target="tpu_custom_call" | custom-call | tf_op jit(solution)/shard_map/third/pallas_call | solution.py:328
  60.7 14.3 %all_to_all.17.moments = f32[32,1,128]{2,1,0:T(1,128)S(1)} all-to-all(f32[32,1,128]{2,1,0:T(1,128)S(1)} %get-tuple-element.28), channel_id=1, replica_groups=mesh['fluid'=4,'solid'=32] {'solid'}, dimensions={0} | all-to-all | bytes 32768 | tf_op jit(solution)/shard_map/all_to_all | solution.py:394
  75.1 0.9 %last.1 = f32[3,32,128]{2,1,0:T(8,128)} custom-call(f32[32,1,128]{2,1,0:T(1,128)S(1)} %all_to_all.17.moments, f32[128,128]{1,0:T(8,128)S(1)} %get-tuple-element.19.start, f32[128,128]{1,0:T(8,128)S(1)} %get-tuple-element.23.vector1, f32[128,128]{1,0:T(8,128)S(1)} %get-tuple-element.29.vector2), custom_call_target="tpu_custom_call" | custom-call | tf_op jit(solution)/shard_map/last/pallas_call | solution.py:328
Async XLA Ops:
  0.6 2.5 %copy-start.2 = (bf16[160,128,128]{2,1,0:T(8,128)(2,1)S(1)}, bf16[160,128,128]{2,1,0:T(8,128)(2,1)}, u32[]{:S(2)}) copy-start(bf16[160,128,128]{2,1,0:T(8,128)(2,1)} %blocks.1) | copy-start | bytes 15728644
  3.1 0.8 %copy-start.5 = (bf16[3,64,128]{2,1,0:T(8,128)(2,1)S(1)}, bf16[3,64,128]{2,1,0:T(8,128)(2,1)}, u32[]{:S(2)}) copy-start(bf16[3,64,128]{2,1,0:T(8,128)(2,1)} %flux.1) | copy-start | bytes 147460
  3.9 0.7 copy-start.7
  4.6 0.7 copy-start.8
  32.7 8.0 %collective-permute-start.2 = (f32[128,128]{1,0:T(8,128)S(1)}, f32[128,128]{1,0:T(8,128)S(1)}, u32[]{:S(2)}, u32[]{:S(2)}) collective-permute-start(f32[128,128]{1,0:T(8,128)S(1)} %combine.1.part0), channel_id=1, source_target_pairs={{0,96},{32,64},{64,32},{96,0},{1,97},{33,65},{65,33},{97,1},{2,98}... | collective-permute-start | bytes 196616 | tf_op jit(solution)/shard_map/ppermute | solution.py:362
  35.6 5.2 %collective-permute-start.1 = (f32[128,128]{1,0:T(8,128)S(1)}, f32[128,128]{1,0:T(8,128)S(1)}, u32[]{:S(2)}, u32[]{:S(2)}) collective-permute-start(f32[128,128]{1,0:T(8,128)S(1)} %combine.1.part0), channel_id=1, source_target_pairs={{0,64},{32,96},{64,0},{96,32},{1,65},{33,97},{65,1},{97,33},{2,66}... | collective-permute-start | bytes 196616 | tf_op jit(solution)/shard_map/ppermute | solution.py:362
  35.9 4.9 %collective-permute-start = (f32[128,128]{1,0:T(8,128)S(1)}, f32[128,128]{1,0:T(8,128)S(1)}, u32[]{:S(2)}, u32[]{:S(2)}) collective-permute-start(f32[128,128]{1,0:T(8,128)S(1)} %combine.1.part0), channel_id=1, source_target_pairs={{0,32},{32,0},{64,96},{96,64},{1,33},{33,1},{65,97},{97,65},{2,34}... | collective-permute-start | bytes 196616 | tf_op jit(solution)/shard_map/ppermute | solution.py:362
  36.2 1.6 %copy-start.3 = (f32[32,128,128]{2,1,0:T(8,128)S(1)}, f32[32,128,128]{2,1,0:T(8,128)}, u32[]{:S(2)}) copy-start(f32[32,128,128]{2,1,0:T(8,128)} %diag.1) | copy-start | bytes 6291460
  37.8 1.6 %copy-start.4 = (f32[32,128,128]{2,1,0:T(8,128)S(1)}, f32[32,128,128]{2,1,0:T(8,128)}, u32[]{:S(2)}) copy-start(f32[32,128,128]{2,1,0:T(8,128)} %couple.1) | copy-start | bytes 6291460
  39.4 1.4 %copy-start.6 = (s32[32]{0:T(128)S(1)}, s32[32]{0:T(128)}, u32[]{:S(2)}) copy-start(s32[32]{0:T(128)} %offsets.5) | copy-start | bytes 388
  40.7 8.7 %copy-start = (bf16[32,256,256]{2,1,0:T(8,128)(2,1)}, bf16[32,256,256]{2,1,0:T(8,128)(2,1)S(1)}, u32[]{:S(2)}) copy-start(bf16[32,256,256]{2,1,0:T(8,128)(2,1)S(1)} %get-tuple-element.16.both) | copy-start | bytes 12582916
  42.8 3.3 %collective-permute-start.3 = (f32[64,128]{1,0:T(8,128)S(1)}, f32[64,128]{1,0:T(8,128)S(1)}, u32[]{:S(2)}, u32[]{:S(2)}) collective-permute-start(f32[64,128]{1,0:T(8,128)S(1)} %get-tuple-element.21), channel_id=1, source_target_pairs={{0,1},{1,0},{2,3},{3,2},{4,5},{5,4},{6,7},{7,6},{8,9},{9,8},{10,11... | collective-permute-start | bytes 98312 | tf_op jit(solution)/shard_map/ppermute | solution.py:343
  44.2 5.2 %collective-permute-start.4 = (f32[64,128]{1,0:T(8,128)S(1)}, f32[64,128]{1,0:T(8,128)S(1)}, u32[]{:S(2)}, u32[]{:S(2)}) collective-permute-start(f32[64,128]{1,0:T(8,128)S(1)} %get-tuple-element.22), channel_id=1, source_target_pairs={{1,2},{3,4},{5,6},{7,8},{9,10},{11,12},{13,14},{15,16},{17,18},{19... | collective-permute-start | bytes 98312 | tf_op jit(solution)/shard_map/ppermute | solution.py:343
  51.3 2.3 %collective-permute-start.5 = (f32[128,128]{1,0:T(8,128)S(1)}, f32[128,128]{1,0:T(8,128)S(1)}, u32[]{:S(2)}, u32[]{:S(2)}) collective-permute-start(f32[128,128]{1,0:T(8,128)S(1)} %get-tuple-element.26), channel_id=1, source_target_pairs={{0,1},{1,0},{2,3},{3,2},{4,5},{5,4},{6,7},{7,6},{8,9},{9,8},{10,11... | collective-permute-start | bytes 196616 | tf_op jit(solution)/shard_map/ppermute | solution.py:343
  51.3 5.6 %collective-permute-start.6 = (f32[128,128]{1,0:T(8,128)S(1)}, f32[128,128]{1,0:T(8,128)S(1)}, u32[]{:S(2)}, u32[]{:S(2)}) collective-permute-start(f32[128,128]{1,0:T(8,128)S(1)} %get-tuple-element.27), channel_id=1, source_target_pairs={{1,2},{3,4},{5,6},{7,8},{9,10},{11,12},{13,14},{15,16},{17,18},{19... | collective-permute-start | bytes 196616 | tf_op jit(solution)/shard_map/ppermute | solution.py:343
  56.9 2.2 %copy-start.1 = (bf16[32,256,256]{2,1,0:T(8,128)(2,1)S(1)}, bf16[32,256,256]{2,1,0:T(8,128)(2,1)}, u32[]{:S(2)}) copy-start(bf16[32,256,256]{2,1,0:T(8,128)(2,1)} %copy-done) | copy-start | bytes 12582916

commit v2 on v1

v2 whole, which is shorter than its diff:
```python
import functools

import jax
import jax.numpy as jnp
from jax import lax
from jax.experimental import pallas as pl
from jax.experimental.pallas import tpu as pltpu
from jax.sharding import PartitionSpec as P

F32 = jnp.float32
BF16 = jnp.bfloat16
LANES = 128
ROWS = 4
SHIFT = 10.5
MOMENTS = 6
VMEM = pl.BlockSpec(memory_space=pltpu.VMEM)
SMEM = pl.BlockSpec(memory_space=pltpu.SMEM)
HBM = pl.BlockSpec(memory_space=pltpu.HBM)


def in_hbm(x):
    return pltpu.with_memory_space_constraint(x, pltpu.HBM)


def dot(a, b, contract=(1, 0)):
    return lax.dot_general(
        a, b, (((contract[0],), (contract[1],)), ((), ())), preferred_element_type=F32
    )


def split(x):
    high = x.astype(BF16).astype(F32)
    return high, x - high


def margin_kernel(owners, own_tiles, chunk, fluid_hbm, solid_hbm, flux_hbm, blocks_hbm, out, blocks, flux, fields, fluid_ids, solid_ids, count, sems):
    pieces = sems.shape[0] - 3
    size = blocks.shape[0] // pieces
    small = [
        pltpu.make_async_copy(source, target, sems.at[pieces + k])
        for k, (source, target) in enumerate(
            ((fluid_hbm, fluid_ids), (solid_hbm, solid_ids), (flux_hbm, flux))
        )
    ]

    def piece(k):
        rows = pl.ds(k * size, size)
        return pltpu.make_async_copy(blocks_hbm.at[rows], blocks.at[rows], sems.at[k])

    for copy in small:
        copy.start()
    for k in range(pieces):
        piece(k).start()
    label_row = chunk - ROWS
    lane = lax.broadcasted_iota(jnp.int32, (1, LANES), 1)
    lane_slot = jnp.where(lane < label_row, lane // 3, -1)
    lane_field = lane % 3
    out[...] = jnp.zeros_like(out)
    fields[...] = jnp.zeros_like(fields)
    for owner in range(owners):
        count[owner] = 0
        out[pl.ds(owner * chunk + label_row, 1), :] = jnp.full((1, LANES), -1.0, F32)
    for copy in small:
        copy.wait()
    for f in range(3):
        fields[pl.ds(f, flux.shape[1], stride=ROWS), :] = flux[f].astype(F32)

    def one_piece(k, _):
        piece(k).wait()
        for j in range(size):
            block = k * size + j
            fluid = fluid_ids[block]
            solid = solid_ids[block]
            owner = solid // own_tiles
            tile = solid - owner * own_tiles
            rank = count[owner]
            count[owner] = rank + 1
            base = owner * chunk
            picked = fields[pl.ds(pl.multiple_of(fluid * ROWS, ROWS), ROWS), :]
            term = dot(picked.astype(BF16), blocks[block])
            for f in range(3):
                out[pl.ds(base + rank * 3 + f, 1), :] = term[f : f + 1]
            label = out[pl.ds(base + label_row, 1), :]
            own_label = (tile * ROWS + lane_field).astype(F32)
            out[pl.ds(base + label_row, 1), :] = jnp.where(lane_slot == rank, own_label, label)
        return 0

    lax.fori_loop(0, pieces, one_piece, 0)


def margin(fluid_ids, solid_ids, flux, blocks, owners, own_tiles, chunk):
    pieces = 10
    return pl.pallas_call(
        functools.partial(margin_kernel, owners, own_tiles, chunk),
        out_shape=jax.ShapeDtypeStruct((owners * chunk, LANES), F32),
        in_specs=[HBM] * 4,
        out_specs=VMEM,
        scratch_shapes=[
            pltpu.VMEM(blocks.shape, BF16),
            pltpu.VMEM(flux.shape, BF16),
            pltpu.VMEM((flux.shape[1] * ROWS, LANES), F32),
            pltpu.SMEM(fluid_ids.shape, jnp.int32),
            pltpu.SMEM(solid_ids.shape, jnp.int32),
            pltpu.SMEM((owners,), jnp.int32),
            pltpu.SemaphoreType.DMA((pieces + 3,)),
        ],
        compiler_params=pltpu.CompilerParams(vmem_limit_bytes=12 << 20),
        name="margin",
    )(*(in_hbm(x) for x in (fluid_ids, solid_ids, flux, blocks)))


def prepare_kernel(diag_hbm, couple_hbm, matrices, diag, couple, sems):
    pieces = sems.shape[1]
    size = diag.shape[0] // pieces

    def piece(k):
        part = pl.ds(k * size, size)
        return [
            pltpu.make_async_copy(source.at[part], target.at[part], sems.at[i, k])
            for i, (source, target) in enumerate(((diag_hbm, diag), (couple_hbm, couple)))
        ]

    for k in range(pieces):
        for copy in piece(k):
            copy.start()
    row = lax.broadcasted_iota(jnp.int32, (LANES, LANES), 0)
    column = lax.broadcasted_iota(jnp.int32, (LANES, LANES), 1)
    shift = jnp.where(row == column, SHIFT, 0.0).astype(F32)
    for k in range(pieces):
        for copy in piece(k):
            copy.wait()
        for t in range(k * size, (k + 1) * size):
            high, low = split(diag[t] - shift)
            matrices[t, 0:LANES, :] = high.astype(BF16)
            matrices[t, LANES : 2 * LANES, :] = low.astype(BF16)
            high, low = split(couple[t])
            matrices[t, 2 * LANES : 3 * LANES, :] = high.astype(BF16)
            matrices[t, 3 * LANES : 4 * LANES, :] = low.astype(BF16)
            matrices[t, 4 * LANES : 5 * LANES, :] = high.T.astype(BF16)
            matrices[t, 5 * LANES : 6 * LANES, :] = low.T.astype(BF16)


def prepare(diag, couple):
    tiles = diag.shape[0]
    return pl.pallas_call(
        prepare_kernel,
        out_shape=jax.ShapeDtypeStruct((tiles, 6 * LANES, LANES), BF16),
        in_specs=[HBM] * 2,
        out_specs=VMEM,
        scratch_shapes=[
            pltpu.VMEM(diag.shape, F32),
            pltpu.VMEM(couple.shape, F32),
            pltpu.SemaphoreType.DMA((2, 4)),
        ],
        compiler_params=pltpu.CompilerParams(vmem_limit_bytes=12 << 20),
        cost_estimate=pl.CostEstimate(flops=1 << 26, bytes_accessed=10 << 20, transcendentals=0),
        name="prepare",
    )(in_hbm(diag), in_hbm(couple))


def views(matrices):
    return tuple(matrices.at[:, 2 * k * LANES : 2 * (k + 1) * LANES, :] for k in range(3))


def combine_kernel(owners, received, out):
    chunk = received.shape[0] // owners
    row = lax.broadcasted_iota(jnp.int32, (out.shape[0], chunk), 0).astype(F32)
    total = jnp.zeros(out.shape, F32)
    for source in range(owners):
        values = received[source * chunk : (source + 1) * chunk, :]
        label = received[(source + 1) * chunk - ROWS : (source + 1) * chunk - ROWS + 1, 0:chunk]
        hits = (row == label).astype(F32).astype(BF16)
        high, low = split(values)
        total = total + dot(hits, high.astype(BF16)) + dot(hits, low.astype(BF16))
    out[...] = total


def combine(received, owners, own_tiles):
    return pl.pallas_call(
        functools.partial(combine_kernel, owners),
        out_shape=jax.ShapeDtypeStruct((own_tiles * ROWS, LANES), F32),
        in_specs=[VMEM],
        out_specs=VMEM,
        compiler_params=pltpu.CompilerParams(vmem_limit_bytes=16 << 20),
        name="combine",
    )(received)


def put_pairs(pairs, t, value):
    high, low = split(value)
    pairs[t, 0:ROWS, :] = high
    pairs[t, ROWS : 2 * ROWS, :] = low


def load_pairs(pairs, t):
    both = pairs[t].astype(BF16)
    return jnp.concatenate([both, both], axis=1)


def fold(product):
    return product[0:ROWS] + product[ROWS : 2 * ROWS]


def ahead(t, partner, pairs, turned):
    return fold(dot(load_pairs(pairs, partner), turned[t]))


def here(t, pairs, matrix):
    return fold(dot(load_pairs(pairs, t), matrix[t]))


def rows(t, count=1):
    return slice(t * ROWS, (t + count) * ROWS)


def select(flag, first, second):
    return jnp.where(flag > 0, first, second)


def leave(tiles, halo, offsets, pairs, spread, back, first):
    for t in range(first, tiles):
        partner = t + offsets[t]
        spread[partner] = spread[partner] + here(t, pairs, back)


def first_send_kernel(tiles, halo, offsets, place, part0, part1, part2, part3, matrices, vector, kept, near, far, pairs, spread):
    own, back, turned = views(matrices)
    vector[...] = (part0[...] + part1[...]) + (part2[...] + part3[...])
    for t in range(halo, tiles):
        put_pairs(pairs, t, vector[rows(t), :])
    spread[...] = jnp.zeros_like(spread)
    leave(tiles, halo, offsets, pairs, spread, back, halo)
    flag = place[0] % 2
    for t in range(halo):
        rim = vector[rows(t), :]
        out = spread[tiles + t]
        near[rows(t), :] = select(flag, rim, out)
        far[rows(t), :] = select(flag, out, rim)
        kept[rows(t), :] = spread[halo + t]


def first_rest_kernel(tiles, halo, offsets, vector, kept, matrices, mapped, image, pairs, spread):
    own, back, turned = views(matrices)
    for f in range(3):
        mapped[f] = vector[pl.ds(f, tiles, stride=ROWS), :]
    for t in range(tiles):
        put_pairs(pairs, t, vector[rows(t), :])
    for t in range(tiles, tiles + halo):
        pairs[t] = jnp.zeros((2 * ROWS, LANES), F32)
    for t in range(halo):
        spread[t] = jnp.zeros((ROWS, LANES), F32)
        spread[halo + t] = kept[rows(t), :]
    for t in range(tiles):
        partner = t + offsets[t]
        spread[t] = spread[t] + (here(t, pairs, own) + ahead(t, partner, pairs, turned))
        if t < halo:
            spread[partner] = spread[partner] + here(t, pairs, back)
    for t in range(tiles):
        image[rows(t), :] = spread[t]


def put_rim(tiles, halo, flag, near, far, pairs):
    for t in range(halo):
        put_pairs(pairs, tiles + t, select(flag, far[rows(t), :], near[rows(t), :]))
        pairs[tiles - halo + t] = jnp.zeros((2 * ROWS, LANES), F32)


def second_send_kernel(tiles, halo, offsets, place, image, far, near, matrices, vector, inner, kept, leaving, near2, far2, pairs, spread):
    own, back, turned = views(matrices)
    flag = place[0] % 2
    put_rim(tiles, halo, flag, near, far, pairs)
    for t in range(halo):
        vector[rows(t), :] = image[rows(t), :] + select(flag, near[rows(t), :], far[rows(t), :])
    for t in range(halo, tiles):
        partner = jnp.maximum(t + offsets[t], halo)
        vector[rows(t), :] = image[rows(t), :] + ahead(t, partner, pairs, turned)
    for t in range(tiles):
        put_pairs(pairs, t, vector[rows(t), :])
    spread[...] = jnp.zeros_like(spread)
    leave(tiles, halo, offsets, pairs, spread, back, 0)
    size = halo * ROWS
    for t in range(halo):
        inner[rows(t), :] = spread[t] + (here(t, pairs, own) + ahead(t, t + offsets[t], pairs, turned))
        kept[rows(t), :] = spread[halo + t]
        leaving[rows(t), :] = spread[tiles + t]
    near2[0:size, :] = select(flag, vector[0:size, :], leaving[...])
    far2[0:size, :] = select(flag, leaving[...], vector[0:size, :])
    near2[size : 2 * size, :] = inner[...]
    far2[size : 2 * size, :] = inner[...]


def moment(a, b):
    folded = jnp.sum((a * b).reshape(-1, 2 * ROWS, LANES), axis=0)
    return jnp.sum(folded, axis=1, keepdims=True)


def placed(values, first):
    field = lax.broadcasted_iota(jnp.int32, (2 * ROWS, LANES), 0) % ROWS
    lane = lax.broadcasted_iota(jnp.int32, (2 * ROWS, LANES), 1)
    row = jnp.zeros((2 * ROWS, LANES), F32)
    for k, value in enumerate(values):
        row = row + jnp.where(lane == (first + k) * ROWS + field, value, 0.0)
    return row


def second_rest_kernel(tiles, halo, offsets, start, vector, kept, matrices, outer, row, pairs):
    own, back, turned = views(matrices)
    for t in range(halo, tiles):
        put_pairs(pairs, t, vector[rows(t), :])
    for t in range(tiles, tiles + halo):
        pairs[t] = jnp.zeros((2 * ROWS, LANES), F32)
    for t in range(halo, tiles):
        value = here(t, pairs, own) + ahead(t, t + offsets[t], pairs, turned)
        outer[rows(t - halo), :] = kept[rows(t - halo), :] + value
    v0, v1 = start[...], vector[...]
    row[...] = placed((moment(v0, v0), moment(v0, v1), moment(v1, v1)), 0)


def third_kernel(tiles, halo, last, offsets, place, vector1, inner, outer, leaving, row, far, near, matrices, vector2, out, pairs, product):
    own, back, turned = views(matrices)
    flag = place[0] % 2
    put_rim(tiles, halo, flag, near, far, pairs)
    for t in range(halo):
        vector2[rows(t), :] = inner[rows(t), :] + select(flag, near[rows(t), :], far[rows(t), :])
    for t in range(halo, tiles):
        partner = jnp.maximum(t + offsets[t], halo)
        vector2[rows(t), :] = outer[rows(t - halo), :] + ahead(t, partner, pairs, turned)
    for t in range(tiles):
        put_pairs(pairs, t, vector2[rows(t), :])
    inside = jnp.where(place[0] == last, 0.0, 1.0).astype(F32)
    for t in range(halo):
        other = rows(halo + t)
        rim = select(flag, far[other, :], near[other, :]) + leaving[rows(t), :]
        put_pairs(pairs, tiles + t, rim * inside)
    for t in range(tiles):
        product[rows(t), :] = here(t, pairs, own) + 2.0 * ahead(t, t + offsets[t], pairs, turned)
    v1, v2, v3 = vector1[...], vector2[...], product[...]
    total = row[...] + placed((moment(v1, v2), moment(v2, v2), moment(v2, v3)), 3)
    total = jnp.sum(total, axis=0, keepdims=True)
    out[...] = jnp.broadcast_to(total[:, None, :], out.shape)


def last_kernel(tiles, moments, start, vector1, vector2, nodal, mixed):
    total = jnp.sum(moments[...], axis=0)
    total = jnp.broadcast_to(total, (2 * ROWS, LANES))
    g = [total if k == 0 else pltpu.roll(total, LANES - k * ROWS, 1) for k in range(MOMENTS)]
    h = [g[k + 1] + SHIFT * g[k] for k in range(MOMENTS - 1)]

    def form(table, c):
        n = len(c)
        result = None
        for i in range(n):
            for j in range(i, n):
                term = (c[i] * c[j]) * table[i + j]
                term = term if i == j else 2.0 * term
                result = term if result is None else result + term
        return result

    def apply(c):
        n = len(c)
        shifted = [SHIFT * c[0]]
        for i in range(1, n):
            shifted.append(c[i - 1] + SHIFT * c[i])
        return shifted + [c[n - 1]]

    one = jnp.ones_like(total)
    rr = g[0]
    alpha = rr / h[0]
    coefficients = [alpha]
    residual = [one - alpha * SHIFT, -alpha]
    new = form(g, residual)
    beta = new / rr
    direction = [residual[0] + beta, residual[1]]
    rr = new
    alpha = rr / form(h, direction)
    coefficients = [coefficients[0] + alpha * direction[0], alpha * direction[1]]
    image = apply(direction)
    residual = [residual[0] - alpha * image[0], residual[1] - alpha * image[1], -alpha * image[2]]
    new = form(g, residual)
    beta = new / rr
    direction = [residual[0] + beta * direction[0], residual[1] + beta * direction[1], residual[2]]
    rr = new
    alpha = rr / form(h, direction)
    coefficients = [
        coefficients[0] + alpha * direction[0],
        coefficients[1] + alpha * direction[1],
        alpha * direction[2],
    ]
    field = lax.broadcasted_iota(jnp.int32, (2 * ROWS, LANES), 0)
    lane = lax.broadcasted_iota(jnp.int32, (2 * ROWS, LANES), 1)
    result = jnp.zeros(start.shape, F32).reshape(-1, 2 * ROWS, LANES)
    for c, v in zip(coefficients, (start, vector1, vector2)):
        column = jnp.sum(jnp.where(lane == field % ROWS, c, 0.0), axis=1, keepdims=True)
        result = result + column[None] * v[...].reshape(-1, 2 * ROWS, LANES)
    mixed[...] = result.reshape(start.shape)
    for f in range(3):
        nodal[f] = mixed[pl.ds(f, tiles, stride=ROWS), :]


def call(kernel, shapes, smem, vmem, scratch, name, work=0):
    estimate = pl.CostEstimate(flops=work << 20, bytes_accessed=work << 16, transcendentals=0)
    return pl.pallas_call(
        kernel,
        out_shape=tuple(jax.ShapeDtypeStruct(s, F32) for s in shapes),
        in_specs=[SMEM] * len(smem) + [VMEM] * len(vmem),
        out_specs=tuple(VMEM for _ in shapes),
        scratch_shapes=scratch,
        compiler_params=pltpu.CompilerParams(vmem_limit_bytes=4 << 20),
        cost_estimate=estimate if work else None,
        name=name,
    )(*smem, *vmem)


def exchange(near, far, axis):
    n = lax.axis_size(axis)
    far_route = [(i, i + 1) for i in range(1, n - 1, 2)] + [(i + 1, i) for i in range(1, n - 1, 2)]
    near_route = [(i, i ^ 1) for i in range(n)]
    far = lax.ppermute(far, axis, far_route)
    near = lax.ppermute(near, axis, near_route)
    return near, far


def local(fluid_flux, margin_blocks, block_fluid, block_solid, diag_blocks, couple_blocks, couple_offset):
    owners = lax.axis_size("solid")
    groups = lax.axis_size("fluid")
    tiles = diag_blocks.shape[0]
    halo = tiles // 2
    total_blocks = block_fluid.shape[0]
    capacity = 5 * total_blocks // (2 * owners)
    chunk = capacity * 3 + ROWS
    place = lax.axis_index("solid").astype(jnp.int32).reshape(1)

    sent = margin(block_fluid, block_solid, fluid_flux, margin_blocks, owners, tiles, chunk)
    received = lax.all_to_all(sent, "solid", split_axis=0, concat_axis=0, tiled=True)
    matrices = prepare(diag_blocks, couple_blocks)
    part = combine(received, owners, tiles)
    parts = [part] + [
        lax.ppermute(part, "fluid", [(i, i ^ d) for i in range(groups)]) for d in (1, 2, 3)
    ]
    whole = (tiles * ROWS, LANES)
    half = (halo * ROWS, LANES)
    pairs = pltpu.VMEM((tiles + halo, 2 * ROWS, LANES), F32)
    spread = pltpu.VMEM((tiles + halo, ROWS, LANES), F32)
    start, kept, near, far = call(
        functools.partial(first_send_kernel, tiles, halo),
        (whole, half, half, half),
        (couple_offset, place),
        (*parts, matrices),
        [pairs, spread],
        "first_send",
    )
    near, far = exchange(near, far, "solid")
    mapped, image = call(
        functools.partial(first_rest_kernel, tiles, halo),
        ((3, tiles, LANES), whole),
        (couple_offset,),
        (start, kept, matrices),
        [pairs, pltpu.VMEM((tiles, ROWS, LANES), F32)],
        "first_rest",
        64,
    )
    vector1, inner, kept, leaving, near, far = call(
        functools.partial(second_send_kernel, tiles, halo),
        (whole, half, half, half, whole, whole),
        (couple_offset, place),
        (image, far, near, matrices),
        [pairs, spread],
        "second_send",
    )
    near, far = exchange(near, far, "solid")
    outer, row = call(
        functools.partial(second_rest_kernel, tiles, halo),
        (half, (2 * ROWS, LANES)),
        (couple_offset,),
        (start, vector1, kept, matrices),
        [pairs],
        "second_rest",
        64,
    )
    vector2, moments = call(
        functools.partial(third_kernel, tiles, halo, owners - 1),
        (whole, (owners, 1, LANES)),
        (couple_offset, place),
        (vector1, inner, outer, leaving, row, far, near, matrices),
        [pairs, pltpu.VMEM(whole, F32)],
        "third",
    )
    moments = lax.all_to_all(moments, "solid", split_axis=0, concat_axis=0, tiled=True)
    (nodal,) = call(
        functools.partial(last_kernel, tiles),
        ((3, tiles, LANES),),
        (),
        (moments, start, vector1, vector2),
        [pltpu.VMEM(whole, F32)],
        "last",
    )
    return mapped, nodal


def solution(mesh):
    in_specs = (
        P(None, ("fluid", "solid"), None),
        P(("fluid", "solid"), None, None),
        P(("fluid", "solid")),
        P(("fluid", "solid")),
        P("solid", None, None),
        P("solid", None, None),
        P("solid"),
    )
    out_specs = (P(None, "solid", None), P(None, "solid", None))
    return jax.shard_map(local, mesh=mesh, in_specs=in_specs, out_specs=out_specs, check_vma=False)
```

time: 76.4 us -> 66.4 us (0.87)
  local copies, waits for them, and re-layouts: 10 us -> 0.01 us
  waiting for transfers between devices: 6.66 us -> 3.27 us
  Pallas kernels: 11.7 us -> 14.5 us
  starting transfers between devices: 9.01 us -> 10.1 us
    unnamed x18 -> x2, local copies, waits for them, and re-layouts: 10 us -> 0.01 us
    ppermute x4, waiting for transfers between devices: 6.66 us -> 1.31 us  [the longest x2 1.3 us: exchange(): far = lax.ppermute(far, axis, far_route)]
    ppermute x3, waiting for transfers between devices: 0.01 us -> 1.96 us  [local(): lax.ppermute(part, 'fluid', [(i, i ^ d) for i in range(groups)])]
    pallas_call x2, Pallas kernels: 4.62 us -> 6.28 us  [the longest x1 3.77 us: margin(): pl.pallas_call(functools.partial(margin_kernel, owners, own_tiles, chunk)...]
    all_to_all x1, blocking collectives: 23.5 us -> 22.2 us  [local(): lax.all_to_all(sent, 'solid', split_axis=0, concat_axis=0, tiled=True)]
    pallas_call x4 -> x6, Pallas kernels: 6.37 us -> 7.54 us  [call(): pl.pallas_call(kernel, out_shape=tuple((jax.ShapeDtypeStruct(s, F32) for...]
    ppermute x4, starting transfers between devices: 5.53 us -> 6.66 us  [the longest x2 6.49 us: exchange(): far = lax.ppermute(far, axis, far_route)]
    all_to_all x1, blocking collectives: 14.3 us -> 15.4 us  [local(): lax.all_to_all(moments, 'solid', split_axis=0, concat_axis=0, tiled=True)]
  transfers between devices with their start and end apart: 7 -> 7, of which waited for: 2 -> 2; matrix products, arithmetic and copies ran while one was open for 0% -> 0% of each run, Pallas kernels for 2% -> 8%
where the time goes in v2:
time: 66.4 us; the launch traced here: 66.2 us
  blocking collectives  37.6 us (57%)
  Pallas kernels  14.5 us (22%)
  starting transfers between devices  10.1 us (15%)
  waiting for transfers between devices  3.27 us (5%)
  between operations  0.72 us (1%)
    all_to_all x1, blocking collectives, local(): lax.all_to_all(sent, 'solid', split_axis=0, concat_axis=0, tiled=True)  22.2 us
    all_to_all x1, blocking collectives, local(): lax.all_to_all(moments, 'solid', split_axis=0, concat_axis=0, tiled=True)  15.4 us
    pallas_call x6, Pallas kernels, call(): pl.pallas_call(kernel, out_shape=tuple((jax.ShapeDtypeStruct(s, F32) for...  7.54 us
    ppermute x2, starting transfers between devices, exchange(): far = lax.ppermute(far, axis, far_route)  6.49 us
    pallas_call x1, Pallas kernels, margin(): pl.pallas_call(functools.partial(margin_kernel, owners, own_tiles, chunk)...  3.77 us
    ppermute x3, starting transfers between devices, local(): lax.ppermute(part, 'fluid', [(i, i ^ d) for i in range(groups)])  3.48 us
    pallas_call x1, Pallas kernels, prepare(): pl.pallas_call(prepare_kernel, out_shape=jax.ShapeDtypeStruct((tiles, 6 *...  2.51 us
    ppermute x3, waiting for transfers between devices, local(): lax.ppermute(part, 'fluid', [(i, i ^ d) for i in range(groups)])  1.96 us
  transfers between devices with their start and end apart: 7, of which 2 were waited for; matrix products, arithmetic and copies ran while one was open for 0% of the time, Pallas kernels for 8%

profile of v2, /device:TPU:1, one launch (start us, length us, event | category | flops | bytes accessed | tf_op | source)
XLA Modules:
  0.0 66.2 jit_solution(17967326302729255268)
XLA Ops:
  0.6 3.8 %margin.1 = f32[1280,128]{1,0:T(8,128)S(1)} custom-call(s32[160]{0:T(256)} %fluid_hbm.1, s32[160]{0:T(256)} %solid_hbm.1, bf16[3,64,128]{2,1,0:T(8,128)(2,1)} %flux_hbm.1, bf16[160,128,128]{2,1,0:T(8,128)(2,1)} %blocks_hbm.1), custom_call_target="tpu_custom_call" | custom-call | tf_op jit(solution)/shard_map/margin/pallas_call | solution.py:93
  4.4 22.2 %all_to_all.16 = f32[32,40,128]{2,1,0:T(8,128)S(1)} all-to-all(f32[32,40,128]{2,1,0:T(8,128)S(1)} %bitcast.4), channel_id=1, replica_groups=mesh['fluid'=4,'solid'=32] {'solid'}, dimensions={0} | all-to-all | bytes 1310720 | tf_op jit(solution)/shard_map/all_to_all | solution.py:434
  26.6 0.7 %combine.1.part0 = f32[128,128]{1,0:T(8,128)S(1)} custom-call(f32[1280,128]{1,0:T(8,128)S(1)} %bitcast.3), custom_call_target="tpu_custom_call" | custom-call | tf_op jit(solution)/shard_map/combine/pallas_call | solution.py:179
  27.3 2.8 %collective-permute-start.2 = (f32[128,128]{1,0:T(8,128)S(1)}, f32[128,128]{1,0:T(8,128)S(1)}, u32[]{:S(2)}, u32[]{:S(2)}) collective-permute-start(f32[128,128]{1,0:T(8,128)S(1)} %combine.1.part0), channel_id=1, source_target_pairs={{0,96},{32,64},{64,32},{96,0},{1,97},{33,65},{65,33},{97,1},{2,98}... | collective-permute-start | bytes 196616 | tf_op jit(solution)/shard_map/ppermute | solution.py:438
  30.1 0.4 collective-permute-start.1
  30.5 0.3 collective-permute-start
  30.8 0.0 copy-start
  30.8 2.5 %prepare.1.matrices = bf16[32,768,128]{2,1,0:T(8,128)(2,1)S(1)} custom-call(f32[32,128,128]{2,1,0:T(8,128)} %diag_hbm.1, f32[32,128,128]{2,1,0:T(8,128)} %couple_hbm.1), custom_call_target="tpu_custom_call" | custom-call | flops 67108864 | bytes 10485760 | tf_op jit(solution)/shard_map/prepare/pallas_call | solution.py:145
  33.3 0.0 collective-permute-done.2.part3
  33.3 2.0 %collective-permute-done.1.part2 = f32[128,128]{1,0:T(8,128)S(1)} collective-permute-done((f32[128,128]{1,0:T(8,128)S(1)}, f32[128,128]{1,0:T(8,128)S(1)}, u32[]{:S(2)}, u32[]{:S(2)}) %collective-permute-start.1) | collective-permute-done | bytes 65568 | tf_op jit(solution)/shard_map/ppermute | solution.py:438
  35.2 0.0 collective-permute-done.part1
  35.2 0.0 copy-done
  35.3 0.8 %first_send.1 = (f32[128,128]{1,0:T(8,128)S(1)}, f32[64,128]{1,0:T(8,128)S(1)}, f32[64,128]{1,0:T(8,128)S(1)}, f32[64,128]{1,0:T(8,128)S(1)}) custom-call(s32[32]{0:T(128)S(1)} %copy-done, s32[1]{0:T(128)} %bitcast.place, f32[128,128]{1,0:T(8,128)S(1)} %combine.1.part0, f32[128,128]{1,0:T(8,128)S(1)} %collective-permute-done.part1, ...), custom_call_target="tpu_custom_call" | custom-call | tf_op jit(solution)/shard_map/first_send/pallas_call | solution.py:402
  36.1 3.2 %collective-permute-start.3 = (f32[64,128]{1,0:T(8,128)S(1)}, f32[64,128]{1,0:T(8,128)S(1)}, u32[]{:S(2)}, u32[]{:S(2)}) collective-permute-start(f32[64,128]{1,0:T(8,128)S(1)} %get-tuple-element.22), channel_id=1, source_target_pairs={{1,2},{3,4},{5,6},{7,8},{9,10},{11,12},{13,14},{15,16},{17,18},{19... | collective-permute-start | bytes 98312 | tf_op jit(solution)/shard_map/ppermute | solution.py:418
  39.3 0.1 collective-permute-start.4
  39.4 1.9 %first_rest.1 = (f32[3,32,128]{2,1,0:T(8,128)}, f32[128,128]{1,0:T(8,128)S(1)}) custom-call(s32[32]{0:T(128)S(1)} %copy-done, f32[128,128]{1,0:T(8,128)S(1)} %get-tuple-element.18.vector.start, f32[64,128]{1,0:T(8,128)S(1)} %get-tuple-element.19.kept, bf16[32,768,128]{2,1,0:T(8,128)(2,1)S(1)} %prepare.1.matrices), custom_call_target="tpu_custom_call" | custom-call | flops 67108864 | bytes 4194304 | tf_op jit(solution)/shard_map/first_rest/pallas_call | solution.py:402
  41.3 0.0 collective-permute-done.3.far
  41.3 0.0 collective-permute-done.4.near
  41.3 1.4 %second_send.1 = (f32[128,128]{1,0:T(8,128)S(1)}, f32[64,128]{1,0:T(8,128)S(1)}, f32[64,128]{1,0:T(8,128)S(1)}, f32[64,128]{1,0:T(8,128)S(1)}, f32[128,128]{1,0:T(8,128)S(1)}, /*index=5*/f32[128,128]{1,0:T(8,128)S(1)}) custom-call(s32[32]{0:T(128)S(1)} %copy-done, s32[1]{0:T(128)} %bitcast.place, f32[128,128]{1,0:T(8,128)S(1)} %get-tuple-element.21.image, ...), custom_call_target="tpu_custom_call" | custom-call | tf_op jit(solution)/shard_map/second_send/pallas_call | solution.py:402
  42.7 3.2 %collective-permute-start.5 = (f32[128,128]{1,0:T(8,128)S(1)}, f32[128,128]{1,0:T(8,128)S(1)}, u32[]{:S(2)}, u32[]{:S(2)}) collective-permute-start(f32[128,128]{1,0:T(8,128)S(1)} %get-tuple-element.30), channel_id=1, source_target_pairs={{1,2},{3,4},{5,6},{7,8},{9,10},{11,12},{13,14},{15,16},{17,18},{19... | collective-permute-start | bytes 196616 | tf_op jit(solution)/shard_map/ppermute | solution.py:418
  46.0 0.1 collective-permute-start.6
  46.1 0.9 %second_rest.1 = (f32[64,128]{1,0:T(8,128)S(1)}, f32[8,128]{1,0:T(8,128)S(1)}) custom-call(s32[32]{0:T(128)S(1)} %copy-done, f32[128,128]{1,0:T(8,128)S(1)} %get-tuple-element.18.vector.start, f32[128,128]{1,0:T(8,128)S(1)} %get-tuple-element.24.vector.vector1, f32[64,128]{1,0:T(8,128)S(1)} %get-tuple-element.26.kept, bf16[32,768,128]{2,1,0:T(8,128)(2,1)S(1)} %prepare.1.matrices), custom_call_target="tpu_custom_call" | custom-call | flops 67108864 | bytes 4194304 | tf_op jit(solution)/shard_map/second_rest/pallas_call | solution.py:402
  47.0 1.3 %collective-permute-done.5.far = f32[128,128]{1,0:T(8,128)S(1)} collective-permute-done((f32[128,128]{1,0:T(8,128)S(1)}, f32[128,128]{1,0:T(8,128)S(1)}, u32[]{:S(2)}, u32[]{:S(2)}) %collective-permute-start.5) | collective-permute-done | bytes 65568 | tf_op jit(solution)/shard_map/ppermute | solution.py:418
  48.3 0.0 collective-permute-done.6.near
  48.3 1.6 %third.1 = (f32[128,128]{1,0:T(8,128)S(1)}, f32[32,1,128]{2,1,0:T(1,128)S(1)}) custom-call(s32[32]{0:T(128)S(1)} %copy-done, s32[1]{0:T(128)} %bitcast.place, f32[128,128]{1,0:T(8,128)S(1)} %get-tuple-element.24.vector.vector1, f32[64,128]{1,0:T(8,128)S(1)} %get-tuple-element.25.inner, f32[64,128]{1,0:T(8,128)S(1)} %get-tuple-element.27.outer, ...), custom_call_target="tpu_custom_call" | custom-call | tf_op jit(solution)/shard_map/third/pallas_call | solution.py:402
  49.9 15.4 %all_to_all.17.moments = f32[32,1,128]{2,1,0:T(1,128)S(1)} all-to-all(f32[32,1,128]{2,1,0:T(1,128)S(1)} %get-tuple-element.32), channel_id=1, replica_groups=mesh['fluid'=4,'solid'=32] {'solid'}, dimensions={0} | all-to-all | bytes 32768 | tf_op jit(solution)/shard_map/all_to_all | solution.py:488
  65.3 0.9 %last.1 = f32[3,32,128]{2,1,0:T(8,128)} custom-call(f32[32,1,128]{2,1,0:T(1,128)S(1)} %all_to_all.17.moments, f32[128,128]{1,0:T(8,128)S(1)} %get-tuple-element.18.vector.start, f32[128,128]{1,0:T(8,128)S(1)} %get-tuple-element.24.vector.vector1, f32[128,128]{1,0:T(8,128)S(1)} %get-tuple-element.33.vector2), custom_call_target="tpu_custom_call" | custom-call | tf_op jit(solution)/shard_map/last/pallas_call | solution.py:402
Async XLA Ops:
  27.3 6.0 %collective-permute-start.2 = (f32[128,128]{1,0:T(8,128)S(1)}, f32[128,128]{1,0:T(8,128)S(1)}, u32[]{:S(2)}, u32[]{:S(2)}) collective-permute-start(f32[128,128]{1,0:T(8,128)S(1)} %combine.1.part0), channel_id=1, source_target_pairs={{0,96},{32,64},{64,32},{96,0},{1,97},{33,65},{65,33},{97,1},{2,98}... | collective-permute-start | bytes 196616 | tf_op jit(solution)/shard_map/ppermute | solution.py:438
  30.1 5.2 %collective-permute-start.1 = (f32[128,128]{1,0:T(8,128)S(1)}, f32[128,128]{1,0:T(8,128)S(1)}, u32[]{:S(2)}, u32[]{:S(2)}) collective-permute-start(f32[128,128]{1,0:T(8,128)S(1)} %combine.1.part0), channel_id=1, source_target_pairs={{0,64},{32,96},{64,0},{96,32},{1,65},{33,97},{65,1},{97,33},{2,66}... | collective-permute-start | bytes 196616 | tf_op jit(solution)/shard_map/ppermute | solution.py:438
  30.5 4.8 %collective-permute-start = (f32[128,128]{1,0:T(8,128)S(1)}, f32[128,128]{1,0:T(8,128)S(1)}, u32[]{:S(2)}, u32[]{:S(2)}) collective-permute-start(f32[128,128]{1,0:T(8,128)S(1)} %combine.1.part0), channel_id=1, source_target_pairs={{0,32},{32,0},{64,96},{96,64},{1,33},{33,1},{65,97},{97,65},{2,34}... | collective-permute-start | bytes 196616 | tf_op jit(solution)/shard_map/ppermute | solution.py:438
  30.8 4.5 %copy-start = (s32[32]{0:T(128)S(1)}, s32[32]{0:T(128)}, u32[]{:S(2)}) copy-start(s32[32]{0:T(128)} %offsets.9) | copy-start | bytes 388
  36.1 5.2 %collective-permute-start.3 = (f32[64,128]{1,0:T(8,128)S(1)}, f32[64,128]{1,0:T(8,128)S(1)}, u32[]{:S(2)}, u32[]{:S(2)}) collective-permute-start(f32[64,128]{1,0:T(8,128)S(1)} %get-tuple-element.22), channel_id=1, source_target_pairs={{1,2},{3,4},{5,6},{7,8},{9,10},{11,12},{13,14},{15,16},{17,18},{19... | collective-permute-start | bytes 98312 | tf_op jit(solution)/shard_map/ppermute | solution.py:418
  39.3 2.0 %collective-permute-start.4 = (f32[64,128]{1,0:T(8,128)S(1)}, f32[64,128]{1,0:T(8,128)S(1)}, u32[]{:S(2)}, u32[]{:S(2)}) collective-permute-start(f32[64,128]{1,0:T(8,128)S(1)} %get-tuple-element.23), channel_id=1, source_target_pairs={{0,1},{1,0},{2,3},{3,2},{4,5},{5,4},{6,7},{7,6},{8,9},{9,8},{10,11... | collective-permute-start | bytes 98312 | tf_op jit(solution)/shard_map/ppermute | solution.py:419
  42.7 5.6 %collective-permute-start.5 = (f32[128,128]{1,0:T(8,128)S(1)}, f32[128,128]{1,0:T(8,128)S(1)}, u32[]{:S(2)}, u32[]{:S(2)}) collective-permute-start(f32[128,128]{1,0:T(8,128)S(1)} %get-tuple-element.30), channel_id=1, source_target_pairs={{1,2},{3,4},{5,6},{7,8},{9,10},{11,12},{13,14},{15,16},{17,18},{19... | collective-permute-start | bytes 196616 | tf_op jit(solution)/shard_map/ppermute | solution.py:418
  46.0 2.3 %collective-permute-start.6 = (f32[128,128]{1,0:T(8,128)S(1)}, f32[128,128]{1,0:T(8,128)S(1)}, u32[]{:S(2)}, u32[]{:S(2)}) collective-permute-start(f32[128,128]{1,0:T(8,128)S(1)} %get-tuple-element.31), channel_id=1, source_target_pairs={{0,1},{1,0},{2,3},{3,2},{4,5},{5,4},{6,7},{7,6},{8,9},{9,8},{10,11... | collective-permute-start | bytes 196616 | tf_op jit(solution)/shard_map/ppermute | solution.py:419

commit v3 on v2

--- a/solution.py
+++ b/solution.py
@@ -33,7 +33,7 @@
     return high, x - high
 
 
-def margin_kernel(owners, own_tiles, chunk, fluid_hbm, solid_hbm, flux_hbm, blocks_hbm, out, blocks, flux, fields, fluid_ids, solid_ids, count, sems):
+def margin_kernel(owners, own_tiles, chunk, fluid_hbm, solid_hbm, flux_hbm, blocks_hbm, out, blocks, flux, left, right, fluid_ids, solid_ids, count, labels, sems):
     pieces = sems.shape[0] - 3
     size = blocks.shape[0] // pieces
     small = [
@@ -44,8 +44,8 @@
     ]
 
     def piece(k):
-        rows = pl.ds(k * size, size)
-        return pltpu.make_async_copy(blocks_hbm.at[rows], blocks.at[rows], sems.at[k])
+        part = pl.ds(k * size, size)
+        return pltpu.make_async_copy(blocks_hbm.at[part], blocks.at[part], sems.at[k])
 
     for copy in small:
         copy.start()
@@ -53,43 +53,55 @@
         piece(k).start()
     label_row = chunk - ROWS
     lane = lax.broadcasted_iota(jnp.int32, (1, LANES), 1)
-    lane_slot = jnp.where(lane < label_row, lane // 3, -1)
-    lane_field = lane % 3
+    lane_first = jnp.where(lane < label_row, lane - lane % 3, -1)
+    lane_field = lane % 3 * own_tiles
     out[...] = jnp.zeros_like(out)
-    fields[...] = jnp.zeros_like(fields)
+    left[...] = jnp.zeros_like(left)
+    right[...] = jnp.zeros_like(right)
+    labels[...] = jnp.full_like(labels, -1.0)
     for owner in range(owners):
         count[owner] = 0
-        out[pl.ds(owner * chunk + label_row, 1), :] = jnp.full((1, LANES), -1.0, F32)
     for copy in small:
         copy.wait()
     for f in range(3):
-        fields[pl.ds(f, flux.shape[1], stride=ROWS), :] = flux[f].astype(F32)
-
-    def one_piece(k, _):
+        field = flux[f].astype(F32)
+        left[pl.ds(f, flux.shape[1], stride=2 * ROWS), :] = field
+        right[pl.ds(ROWS + f, flux.shape[1], stride=2 * ROWS), :] = field
+
+    def place(block):
+        solid = solid_ids[block]
+        owner = lax.shift_right_logical(solid, own_tiles.bit_length() - 1)
+        tile = solid & (own_tiles - 1)
+        used = count[owner]
+        count[owner] = used + 3
+        label = (tile + lane_field).astype(F32)
+        row = pl.ds(owner, 1)
+        labels[row, :] = jnp.where(lane_first == used, label, labels[row, :])
+        return owner * chunk + used
+
+    def chosen(table, block):
+        first = pl.multiple_of(fluid_ids[block] * (2 * ROWS), 2 * ROWS)
+        return table[pl.ds(first, 2 * ROWS), :].astype(BF16)
+
+    for k in range(pieces):
         piece(k).wait()
-        for j in range(size):
-            block = k * size + j
-            fluid = fluid_ids[block]
-            solid = solid_ids[block]
-            owner = solid // own_tiles
-            tile = solid - owner * own_tiles
-            rank = count[owner]
-            count[owner] = rank + 1
-            base = owner * chunk
-            picked = fields[pl.ds(pl.multiple_of(fluid * ROWS, ROWS), ROWS), :]
-            term = dot(picked.astype(BF16), blocks[block])
-            for f in range(3):
-                out[pl.ds(base + rank * 3 + f, 1), :] = term[f : f + 1]
-            label = out[pl.ds(base + label_row, 1), :]
-            own_label = (tile * ROWS + lane_field).astype(F32)
-            out[pl.ds(base + label_row, 1), :] = jnp.where(lane_slot == rank, own_label, label)
-        return 0
-
-    lax.fori_loop(0, pieces, one_piece, 0)
+        for block in range(k * size, (k + 1) * size, 2):
+            slots = place(block), place(block + 1)
+            fields = jnp.concatenate([chosen(left, block), chosen(right, block + 1)], axis=1)
+            terms = dot(fields, blocks[pl.ds(block, 2)].reshape(2 * LANES, LANES))
+            for half, slot in enumerate(slots):
+                for f in range(3):
+                    row = half * ROWS + f
+                    out[pl.ds(slot + f, 1), :] = terms[row : row + 1]
+    for owner in range(owners):
+        out[pl.ds(owner * chunk + label_row, 1), :] = labels[pl.ds(owner, 1), :]
 
 
 def margin(fluid_ids, solid_ids, flux, blocks, owners, own_tiles, chunk):
-    pieces = 10
+    assert own_tiles & (own_tiles - 1) == 0
+    pieces = 5
+    assert blocks.shape[0] % (2 * pieces) == 0
+    table = pltpu.VMEM((flux.shape[1] * 2 * ROWS, LANES), F32)
     return pl.pallas_call(
         functools.partial(margin_kernel, owners, own_tiles, chunk),
         out_shape=jax.ShapeDtypeStruct((owners * chunk, LANES), F32),
@@ -98,10 +110,12 @@
         scratch_shapes=[
             pltpu.VMEM(blocks.shape, BF16),
             pltpu.VMEM(flux.shape, BF16),
-            pltpu.VMEM((flux.shape[1] * ROWS, LANES), F32),
+            table,
+            table,
             pltpu.SMEM(fluid_ids.shape, jnp.int32),
             pltpu.SMEM(solid_ids.shape, jnp.int32),
             pltpu.SMEM((owners,), jnp.int32),
+            pltpu.VMEM((owners, LANES), F32),
             pltpu.SemaphoreType.DMA((pieces + 3,)),
         ],
         compiler_params=pltpu.CompilerParams(vmem_limit_bytes=12 << 20),
@@ -178,7 +192,7 @@
 def combine(received, owners, own_tiles):
     return pl.pallas_call(
         functools.partial(combine_kernel, owners),
-        out_shape=jax.ShapeDtypeStruct((own_tiles * ROWS, LANES), F32),
+        out_shape=jax.ShapeDtypeStruct((own_tiles * 3, LANES), F32),
         in_specs=[VMEM],
         out_specs=VMEM,
         compiler_params=pltpu.CompilerParams(vmem_limit_bytes=16 << 20),
@@ -217,19 +231,24 @@
     return jnp.where(flag > 0, first, second)
 
 
-def leave(tiles, halo, offsets, pairs, spread, back, first):
-    for t in range(first, tiles):
+def add_transposed(tiles, offsets, pairs, spread, back, products, first, stop):
+    for t in range(first, stop):
+        products[t] = here(t, pairs, back)
+    for t in range(first, stop):
         partner = t + offsets[t]
-        spread[partner] = spread[partner] + here(t, pairs, back)
-
-
-def first_send_kernel(tiles, halo, offsets, place, part0, part1, part2, part3, matrices, vector, kept, near, far, pairs, spread):
+        spread[partner] = spread[partner] + products[t]
+
+
+def first_send_kernel(tiles, halo, offsets, place, part0, part1, part3, part2, matrices, vector, kept, near, far, pairs, spread, products):
     own, back, turned = views(matrices)
-    vector[...] = (part0[...] + part1[...]) + (part2[...] + part3[...])
+    total = (part0[...] + part1[...]) + (part2[...] + part3[...])
+    for f in range(3):
+        vector[pl.ds(f, tiles, stride=ROWS), :] = total[f * tiles : (f + 1) * tiles]
+    vector[pl.ds(3, tiles, stride=ROWS), :] = jnp.zeros((tiles, LANES), F32)
     for t in range(halo, tiles):
         put_pairs(pairs, t, vector[rows(t), :])
     spread[...] = jnp.zeros_like(spread)
-    leave(tiles, halo, offsets, pairs, spread, back, halo)
+    add_transposed(tiles, offsets, pairs, spread, back, products, halo, tiles)
     flag = place[0] % 2
     for t in range(halo):
         rim = vector[rows(t), :]
@@ -239,7 +258,7 @@
         kept[rows(t), :] = spread[halo + t]
 
 
-def first_rest_kernel(tiles, halo, offsets, vector, kept, matrices, mapped, image, pairs, spread):
+def first_rest_kernel(tiles, halo, offsets, vector, kept, matrices, mapped, image, pairs, spread, products):
     own, back, turned = views(matrices)
     for f in range(3):
         mapped[f] = vector[pl.ds(f, tiles, stride=ROWS), :]
@@ -250,13 +269,10 @@
     for t in range(halo):
         spread[t] = jnp.zeros((ROWS, LANES), F32)
         spread[halo + t] = kept[rows(t), :]
+    add_transposed(tiles, offsets, pairs, spread, back, products, 0, halo)
     for t in range(tiles):
-        partner = t + offsets[t]
-        spread[t] = spread[t] + (here(t, pairs, own) + ahead(t, partner, pairs, turned))
-        if t < halo:
-            spread[partner] = spread[partner] + here(t, pairs, back)
-    for t in range(tiles):
-        image[rows(t), :] = spread[t]
+        value = here(t, pairs, own) + ahead(t, t + offsets[t], pairs, turned)
+        image[rows(t), :] = spread[t] + value
 
 
 def put_rim(tiles, halo, flag, near, far, pairs):
@@ -265,7 +281,7 @@
         pairs[tiles - halo + t] = jnp.zeros((2 * ROWS, LANES), F32)
 
 
-def second_send_kernel(tiles, halo, offsets, place, image, far, near, matrices, vector, inner, kept, leaving, near2, far2, pairs, spread):
+def second_send_kernel(tiles, halo, offsets, place, image, far, near, matrices, vector, inner, kept, leaving, near2, far2, pairs, spread, products):
     own, back, turned = views(matrices)
     flag = place[0] % 2
     put_rim(tiles, halo, flag, near, far, pairs)
@@ -277,7 +293,7 @@
     for t in range(tiles):
         put_pairs(pairs, t, vector[rows(t), :])
     spread[...] = jnp.zeros_like(spread)
-    leave(tiles, halo, offsets, pairs, spread, back, 0)
+    add_transposed(tiles, offsets, pairs, spread, back, products, 0, tiles)
     size = halo * ROWS
     for t in range(halo):
         inner[rows(t), :] = spread[t] + (here(t, pairs, own) + ahead(t, t + offsets[t], pairs, turned))
@@ -434,19 +450,20 @@
     received = lax.all_to_all(sent, "solid", split_axis=0, concat_axis=0, tiled=True)
     matrices = prepare(diag_blocks, couple_blocks)
     part = combine(received, owners, tiles)
-    parts = [part] + [
+    part1, part2, part3 = (
         lax.ppermute(part, "fluid", [(i, i ^ d) for i in range(groups)]) for d in (1, 2, 3)
-    ]
+    )
     whole = (tiles * ROWS, LANES)
     half = (halo * ROWS, LANES)
     pairs = pltpu.VMEM((tiles + halo, 2 * ROWS, LANES), F32)
     spread = pltpu.VMEM((tiles + halo, ROWS, LANES), F32)
+    products = pltpu.VMEM((tiles, ROWS, LANES), F32)
     start, kept, near, far = call(
         functools.partial(first_send_kernel, tiles, halo),
         (whole, half, half, half),
         (couple_offset, place),
-        (*parts, matrices),
-        [pairs, spread],
+        (part, part1, part3, part2, matrices),
+        [pairs, spread, products],
         "first_send",
     )
     near, far = exchange(near, far, "solid")
@@ -455,7 +472,7 @@
         ((3, tiles, LANES), whole),
         (couple_offset,),
         (start, kept, matrices),
-        [pairs, pltpu.VMEM((tiles, ROWS, LANES), F32)],
+        [pairs, products, products],
         "first_rest",
         64,
     )
@@ -464,7 +481,7 @@
         (whole, half, half, half, whole, whole),
         (couple_offset, place),
         (image, far, near, matrices),
-        [pairs, spread],
+        [pairs, spread, products],
         "second_send",
     )
     near, far = exchange(near, far, "solid")

time: 66.4 us -> 64.5 us (0.971)
  waiting for transfers between devices: 3.27 us -> 2.15 us
  Pallas kernels: 14.5 us -> 13.5 us
    ppermute x3, waiting for transfers between devices: 1.96 us -> 0.85 us  [local(): lax.ppermute(part, 'fluid', [(i, i ^ d) for i in range(groups)])]
    pallas_call x1, Pallas kernels: 3.77 us -> 2.89 us  [margin(): pl.pallas_call(functools.partial(margin_kernel, owners, own_tiles, chunk)...]
where the time goes in v3:
time: 64.5 us; the launch traced here: 64.3 us
  blocking collectives  37.3 us (58%)
  Pallas kernels  13.5 us (21%)
  starting transfers between devices  10.7 us (17%)
  waiting for transfers between devices  2.15 us (3%)
  between operations  0.73 us (1%)
    all_to_all x1, blocking collectives, local(): lax.all_to_all(sent, 'solid', split_axis=0, concat_axis=0, tiled=True)  22.2 us
    all_to_all x1, blocking collectives, local(): lax.all_to_all(moments, 'solid', split_axis=0, concat_axis=0, tiled=True)  15.1 us
    pallas_call x6, Pallas kernels, call(): pl.pallas_call(kernel, out_shape=tuple((jax.ShapeDtypeStruct(s, F32) for...  7.55 us
    ppermute x2, starting transfers between devices, exchange(): far = lax.ppermute(far, axis, far_route)  6.69 us
    ppermute x3, starting transfers between devices, local(): lax.ppermute(part, 'fluid', [(i, i ^ d) for i in range(groups)])  3.79 us
    pallas_call x1, Pallas kernels, margin(): pl.pallas_call(functools.partial(margin_kernel, owners, own_tiles, chunk)...  2.89 us
    pallas_call x1, Pallas kernels, prepare(): pl.pallas_call(prepare_kernel, out_shape=jax.ShapeDtypeStruct((tiles, 6 *...  2.51 us
    ppermute x2, waiting for transfers between devices, exchange(): far = lax.ppermute(far, axis, far_route)  1.29 us
  transfers between devices with their start and end apart: 7, of which 2 were waited for; matrix products, arithmetic and copies ran while one was open for 0% of the time, Pallas kernels for 8%

profile of v3, /device:TPU:1, one launch (start us, length us, event | category | flops | bytes accessed | tf_op | source)
XLA Modules:
  0.0 64.3 jit_solution(6537302820529905730)
XLA Ops:
  0.6 2.9 %margin.1 = f32[1280,128]{1,0:T(8,128)S(1)} custom-call(s32[160]{0:T(256)} %fluid_hbm.1, s32[160]{0:T(256)} %solid_hbm.1, bf16[3,64,128]{2,1,0:T(8,128)(2,1)} %flux_hbm.1, bf16[160,128,128]{2,1,0:T(8,128)(2,1)} %blocks_hbm.1), custom_call_target="tpu_custom_call" | custom-call | tf_op jit(solution)/shard_map/margin/pallas_call | solution.py:105
  3.5 22.2 %all_to_all.16 = f32[32,40,128]{2,1,0:T(8,128)S(1)} all-to-all(f32[32,40,128]{2,1,0:T(8,128)S(1)} %bitcast.4), channel_id=1, replica_groups=mesh['fluid'=4,'solid'=32] {'solid'}, dimensions={0} | all-to-all | bytes 1310720 | tf_op jit(solution)/shard_map/all_to_all | solution.py:450
  25.7 0.5 combine.1.part0
  26.3 3.0 %collective-permute-start.2 = (f32[96,128]{1,0:T(8,128)S(1)}, f32[96,128]{1,0:T(8,128)S(1)}, u32[]{:S(2)}, u32[]{:S(2)}) collective-permute-start(f32[96,128]{1,0:T(8,128)S(1)} %combine.1.part0), channel_id=1, source_target_pairs={{0,64},{32,96},{64,0},{96,32},{1,65},{33,97},{65,1},{97,33},{2,66}... | collective-permute-start | bytes 147464 | tf_op jit(solution)/shard_map/ppermute | solution.py:454
  29.2 0.8 %collective-permute-start.1 = (f32[96,128]{1,0:T(8,128)S(1)}, f32[96,128]{1,0:T(8,128)S(1)}, u32[]{:S(2)}, u32[]{:S(2)}) collective-permute-start(f32[96,128]{1,0:T(8,128)S(1)} %combine.1.part0), channel_id=1, source_target_pairs={{0,96},{32,64},{64,32},{96,0},{1,97},{33,65},{65,33},{97,1},{2,98}... | collective-permute-start | bytes 147464 | tf_op jit(solution)/shard_map/ppermute | solution.py:454
  30.0 0.0 collective-permute-start
  30.0 0.0 copy-start
  30.0 2.5 %prepare.1.matrices = bf16[32,768,128]{2,1,0:T(8,128)(2,1)S(1)} custom-call(f32[32,128,128]{2,1,0:T(8,128)} %diag_hbm.1, f32[32,128,128]{2,1,0:T(8,128)} %couple_hbm.1), custom_call_target="tpu_custom_call" | custom-call | flops 67108864 | bytes 10485760 | tf_op jit(solution)/shard_map/prepare/pallas_call | solution.py:159
  32.6 0.0 collective-permute-done.2.part2
  32.6 0.8 %collective-permute-done.1.part3 = f32[96,128]{1,0:T(8,128)S(1)} collective-permute-done((f32[96,128]{1,0:T(8,128)S(1)}, f32[96,128]{1,0:T(8,128)S(1)}, u32[]{:S(2)}, u32[]{:S(2)}) %collective-permute-start.1) | collective-permute-done | bytes 49184 | tf_op jit(solution)/shard_map/ppermute | solution.py:454
  33.4 0.0 collective-permute-done.part1
  33.4 0.0 copy-done
  33.4 0.8 %first_send.1 = (f32[128,128]{1,0:T(8,128)S(1)}, f32[64,128]{1,0:T(8,128)S(1)}, f32[64,128]{1,0:T(8,128)S(1)}, f32[64,128]{1,0:T(8,128)S(1)}) custom-call(s32[32]{0:T(128)S(1)} %copy-done, s32[1]{0:T(128)} %bitcast.place, f32[96,128]{1,0:T(8,128)S(1)} %combine.1.part0, f32[96,128]{1,0:T(8,128)S(1)} %collective-permute-done.part1, ...), custom_call_target="tpu_custom_call" | custom-call | tf_op jit(solution)/shard_map/first_send/pallas_call | solution.py:418
  34.3 3.4 %collective-permute-start.3 = (f32[64,128]{1,0:T(8,128)S(1)}, f32[64,128]{1,0:T(8,128)S(1)}, u32[]{:S(2)}, u32[]{:S(2)}) collective-permute-start(f32[64,128]{1,0:T(8,128)S(1)} %get-tuple-element.22), channel_id=1, source_target_pairs={{1,2},{3,4},{5,6},{7,8},{9,10},{11,12},{13,14},{15,16},{17,18},{19... | collective-permute-start | bytes 98312 | tf_op jit(solution)/shard_map/ppermute | solution.py:434
  37.7 0.1 collective-permute-start.4
  37.8 1.9 %first_rest.1 = (f32[3,32,128]{2,1,0:T(8,128)}, f32[128,128]{1,0:T(8,128)S(1)}) custom-call(s32[32]{0:T(128)S(1)} %copy-done, f32[128,128]{1,0:T(8,128)S(1)} %get-tuple-element.18.vector.start, f32[64,128]{1,0:T(8,128)S(1)} %get-tuple-element.19.kept, bf16[32,768,128]{2,1,0:T(8,128)(2,1)S(1)} %prepare.1.matrices), custom_call_target="tpu_custom_call" | custom-call | flops 67108864 | bytes 4194304 | tf_op jit(solution)/shard_map/first_rest/pallas_call | solution.py:418
  39.7 0.0 collective-permute-done.3.far
  39.7 0.0 collective-permute-done.4.near
  39.7 1.4 %second_send.1 = (f32[128,128]{1,0:T(8,128)S(1)}, f32[64,128]{1,0:T(8,128)S(1)}, f32[64,128]{1,0:T(8,128)S(1)}, f32[64,128]{1,0:T(8,128)S(1)}, f32[128,128]{1,0:T(8,128)S(1)}, /*index=5*/f32[128,128]{1,0:T(8,128)S(1)}) custom-call(s32[32]{0:T(128)S(1)} %copy-done, s32[1]{0:T(128)} %bitcast.place, f32[128,128]{1,0:T(8,128)S(1)} %get-tuple-element.21.image, ...), custom_call_target="tpu_custom_call" | custom-call | tf_op jit(solution)/shard_map/second_send/pallas_call | solution.py:418
  41.1 3.3 %collective-permute-start.5 = (f32[128,128]{1,0:T(8,128)S(1)}, f32[128,128]{1,0:T(8,128)S(1)}, u32[]{:S(2)}, u32[]{:S(2)}) collective-permute-start(f32[128,128]{1,0:T(8,128)S(1)} %get-tuple-element.30), channel_id=1, source_target_pairs={{1,2},{3,4},{5,6},{7,8},{9,10},{11,12},{13,14},{15,16},{17,18},{19... | collective-permute-start | bytes 196616 | tf_op jit(solution)/shard_map/ppermute | solution.py:434
  44.4 0.1 collective-permute-start.6
  44.5 0.9 %second_rest.1 = (f32[64,128]{1,0:T(8,128)S(1)}, f32[8,128]{1,0:T(8,128)S(1)}) custom-call(s32[32]{0:T(128)S(1)} %copy-done, f32[128,128]{1,0:T(8,128)S(1)} %get-tuple-element.18.vector.start, f32[128,128]{1,0:T(8,128)S(1)} %get-tuple-element.24.vector.vector1, f32[64,128]{1,0:T(8,128)S(1)} %get-tuple-element.26.kept, bf16[32,768,128]{2,1,0:T(8,128)(2,1)S(1)} %prepare.1.matrices), custom_call_target="tpu_custom_call" | custom-call | flops 67108864 | bytes 4194304 | tf_op jit(solution)/shard_map/second_rest/pallas_call | solution.py:418
  45.4 1.3 %collective-permute-done.5.far = f32[128,128]{1,0:T(8,128)S(1)} collective-permute-done((f32[128,128]{1,0:T(8,128)S(1)}, f32[128,128]{1,0:T(8,128)S(1)}, u32[]{:S(2)}, u32[]{:S(2)}) %collective-permute-start.5) | collective-permute-done | bytes 65568 | tf_op jit(solution)/shard_map/ppermute | solution.py:434
  46.7 0.0 collective-permute-done.6.near
  46.7 1.6 %third.1 = (f32[128,128]{1,0:T(8,128)S(1)}, f32[32,1,128]{2,1,0:T(1,128)S(1)}) custom-call(s32[32]{0:T(128)S(1)} %copy-done, s32[1]{0:T(128)} %bitcast.place, f32[128,128]{1,0:T(8,128)S(1)} %get-tuple-element.24.vector.vector1, f32[64,128]{1,0:T(8,128)S(1)} %get-tuple-element.25.inner, f32[64,128]{1,0:T(8,128)S(1)} %get-tuple-element.27.outer, ...), custom_call_target="tpu_custom_call" | custom-call | tf_op jit(solution)/shard_map/third/pallas_call | solution.py:418
  48.3 15.1 %all_to_all.17.moments = f32[32,1,128]{2,1,0:T(1,128)S(1)} all-to-all(f32[32,1,128]{2,1,0:T(1,128)S(1)} %get-tuple-element.32), channel_id=1, replica_groups=mesh['fluid'=4,'solid'=32] {'solid'}, dimensions={0} | all-to-all | bytes 32768 | tf_op jit(solution)/shard_map/all_to_all | solution.py:505
  63.4 0.9 %last.1 = f32[3,32,128]{2,1,0:T(8,128)} custom-call(f32[32,1,128]{2,1,0:T(1,128)S(1)} %all_to_all.17.moments, f32[128,128]{1,0:T(8,128)S(1)} %get-tuple-element.18.vector.start, f32[128,128]{1,0:T(8,128)S(1)} %get-tuple-element.24.vector.vector1, f32[128,128]{1,0:T(8,128)S(1)} %get-tuple-element.33.vector2), custom_call_target="tpu_custom_call" | custom-call | tf_op jit(solution)/shard_map/last/pallas_call | solution.py:418
Async XLA Ops:
  26.3 6.3 %collective-permute-start.2 = (f32[96,128]{1,0:T(8,128)S(1)}, f32[96,128]{1,0:T(8,128)S(1)}, u32[]{:S(2)}, u32[]{:S(2)}) collective-permute-start(f32[96,128]{1,0:T(8,128)S(1)} %combine.1.part0), channel_id=1, source_target_pairs={{0,64},{32,96},{64,0},{96,32},{1,65},{33,97},{65,1},{97,33},{2,66}... | collective-permute-start | bytes 147464 | tf_op jit(solution)/shard_map/ppermute | solution.py:454
  29.2 4.2 %collective-permute-start.1 = (f32[96,128]{1,0:T(8,128)S(1)}, f32[96,128]{1,0:T(8,128)S(1)}, u32[]{:S(2)}, u32[]{:S(2)}) collective-permute-start(f32[96,128]{1,0:T(8,128)S(1)} %combine.1.part0), channel_id=1, source_target_pairs={{0,96},{32,64},{64,32},{96,0},{1,97},{33,65},{65,33},{97,1},{2,98}... | collective-permute-start | bytes 147464 | tf_op jit(solution)/shard_map/ppermute | solution.py:454
  30.0 3.4 %collective-permute-start = (f32[96,128]{1,0:T(8,128)S(1)}, f32[96,128]{1,0:T(8,128)S(1)}, u32[]{:S(2)}, u32[]{:S(2)}) collective-permute-start(f32[96,128]{1,0:T(8,128)S(1)} %combine.1.part0), channel_id=1, source_target_pairs={{0,32},{32,0},{64,96},{96,64},{1,33},{33,1},{65,97},{97,65},{2,34}... | collective-permute-start | bytes 147464 | tf_op jit(solution)/shard_map/ppermute | solution.py:454
  30.0 3.4 %copy-start = (s32[32]{0:T(128)S(1)}, s32[32]{0:T(128)}, u32[]{:S(2)}) copy-start(s32[32]{0:T(128)} %offsets.9) | copy-start | bytes 388
  34.3 5.4 %collective-permute-start.3 = (f32[64,128]{1,0:T(8,128)S(1)}, f32[64,128]{1,0:T(8,128)S(1)}, u32[]{:S(2)}, u32[]{:S(2)}) collective-permute-start(f32[64,128]{1,0:T(8,128)S(1)} %get-tuple-element.22), channel_id=1, source_target_pairs={{1,2},{3,4},{5,6},{7,8},{9,10},{11,12},{13,14},{15,16},{17,18},{19... | collective-permute-start | bytes 98312 | tf_op jit(solution)/shard_map/ppermute | solution.py:434
  37.7 2.0 %collective-permute-start.4 = (f32[64,128]{1,0:T(8,128)S(1)}, f32[64,128]{1,0:T(8,128)S(1)}, u32[]{:S(2)}, u32[]{:S(2)}) collective-permute-start(f32[64,128]{1,0:T(8,128)S(1)} %get-tuple-element.23), channel_id=1, source_target_pairs={{0,1},{1,0},{2,3},{3,2},{4,5},{5,4},{6,7},{7,6},{8,9},{9,8},{10,11... | collective-permute-start | bytes 98312 | tf_op jit(solution)/shard_map/ppermute | solution.py:435
  41.1 5.6 %collective-permute-start.5 = (f32[128,128]{1,0:T(8,128)S(1)}, f32[128,128]{1,0:T(8,128)S(1)}, u32[]{:S(2)}, u32[]{:S(2)}) collective-permute-start(f32[128,128]{1,0:T(8,128)S(1)} %get-tuple-element.30), channel_id=1, source_target_pairs={{1,2},{3,4},{5,6},{7,8},{9,10},{11,12},{13,14},{15,16},{17,18},{19... | collective-permute-start | bytes 196616 | tf_op jit(solution)/shard_map/ppermute | solution.py:434
  44.4 2.3 %collective-permute-start.6 = (f32[128,128]{1,0:T(8,128)S(1)}, f32[128,128]{1,0:T(8,128)S(1)}, u32[]{:S(2)}, u32[]{:S(2)}) collective-permute-start(f32[128,128]{1,0:T(8,128)S(1)} %get-tuple-element.31), channel_id=1, source_target_pairs={{0,1},{1,0},{2,3},{3,2},{4,5},{5,4},{6,7},{7,6},{8,9},{9,8},{10,11... | collective-permute-start | bytes 196616 | tf_op jit(solution)/shard_map/ppermute | solution.py:435

commit v4 on v3

--- a/solution.py
+++ b/solution.py
@@ -231,15 +231,16 @@
     return jnp.where(flag > 0, first, second)
 
 
-def add_transposed(tiles, offsets, pairs, spread, back, products, first, stop):
+def add_transposed(tiles, arrived, pairs, spread, back, products, first, stop):
     for t in range(first, stop):
         products[t] = here(t, pairs, back)
+    offsets = arrived()
     for t in range(first, stop):
         partner = t + offsets[t]
         spread[partner] = spread[partner] + products[t]
 
 
-def first_send_kernel(tiles, halo, offsets, place, part0, part1, part3, part2, matrices, vector, kept, near, far, pairs, spread, products):
+def first_send_kernel(tiles, halo, arrived, part0, part1, part3, part2, matrices, vector, kept, near, far, pairs, spread, products):
     own, back, turned = views(matrices)
     total = (part0[...] + part1[...]) + (part2[...] + part3[...])
     for f in range(3):
@@ -248,8 +249,8 @@
     for t in range(halo, tiles):
         put_pairs(pairs, t, vector[rows(t), :])
     spread[...] = jnp.zeros_like(spread)
-    add_transposed(tiles, offsets, pairs, spread, back, products, halo, tiles)
-    flag = place[0] % 2
+    add_transposed(tiles, arrived, pairs, spread, back, products, halo, tiles)
+    flag = lax.axis_index("solid") % 2
     for t in range(halo):
         rim = vector[rows(t), :]
         out = spread[tiles + t]
@@ -258,7 +259,7 @@
         kept[rows(t), :] = spread[halo + t]
 
 
-def first_rest_kernel(tiles, halo, offsets, vector, kept, matrices, mapped, image, pairs, spread, products):
+def first_rest_kernel(tiles, halo, arrived, vector, kept, matrices, mapped, image, pairs, spread, products):
     own, back, turned = views(matrices)
     for f in range(3):
         mapped[f] = vector[pl.ds(f, tiles, stride=ROWS), :]
@@ -269,7 +270,8 @@
     for t in range(halo):
         spread[t] = jnp.zeros((ROWS, LANES), F32)
         spread[halo + t] = kept[rows(t), :]
-    add_transposed(tiles, offsets, pairs, spread, back, products, 0, halo)
+    offsets = arrived()
+    add_transposed(tiles, lambda: offsets, pairs, spread, back, products, 0, halo)
     for t in range(tiles):
         value = here(t, pairs, own) + ahead(t, t + offsets[t], pairs, turned)
         image[rows(t), :] = spread[t] + value
@@ -281,10 +283,11 @@
         pairs[tiles - halo + t] = jnp.zeros((2 * ROWS, LANES), F32)
 
 
-def second_send_kernel(tiles, halo, offsets, place, image, far, near, matrices, vector, inner, kept, leaving, near2, far2, pairs, spread, products):
+def second_send_kernel(tiles, halo, arrived, image, far, near, matrices, vector, inner, kept, leaving, near2, far2, pairs, spread, products):
     own, back, turned = views(matrices)
-    flag = place[0] % 2
+    flag = lax.axis_index("solid") % 2
     put_rim(tiles, halo, flag, near, far, pairs)
+    offsets = arrived()
     for t in range(halo):
         vector[rows(t), :] = image[rows(t), :] + select(flag, near[rows(t), :], far[rows(t), :])
     for t in range(halo, tiles):
@@ -293,7 +296,7 @@
     for t in range(tiles):
         put_pairs(pairs, t, vector[rows(t), :])
     spread[...] = jnp.zeros_like(spread)
-    add_transposed(tiles, offsets, pairs, spread, back, products, 0, tiles)
+    add_transposed(tiles, lambda: offsets, pairs, spread, back, products, 0, tiles)
     size = halo * ROWS
     for t in range(halo):
         inner[rows(t), :] = spread[t] + (here(t, pairs, own) + ahead(t, t + offsets[t], pairs, turned))
@@ -319,12 +322,13 @@
     return row
 
 
-def second_rest_kernel(tiles, halo, offsets, start, vector, kept, matrices, outer, row, pairs):
+def second_rest_kernel(tiles, halo, arrived, start, vector, kept, matrices, outer, row, pairs):
     own, back, turned = views(matrices)
     for t in range(halo, tiles):
         put_pairs(pairs, t, vector[rows(t), :])
     for t in range(tiles, tiles + halo):
         pairs[t] = jnp.zeros((2 * ROWS, LANES), F32)
+    offsets = arrived()
     for t in range(halo, tiles):
         value = here(t, pairs, own) + ahead(t, t + offsets[t], pairs, turned)
         outer[rows(t - halo), :] = kept[rows(t - halo), :] + value
@@ -332,33 +336,47 @@
     row[...] = placed((moment(v0, v0), moment(v0, v1), moment(v1, v1)), 0)
 
 
-def third_kernel(tiles, halo, last, offsets, place, vector1, inner, outer, leaving, row, far, near, matrices, vector2, out, pairs, product):
+def third_kernel(tiles, halo, last, arrived, vector1, inner, outer, leaving, row, far, near, matrices, vector2, out, pairs):
     own, back, turned = views(matrices)
-    flag = place[0] % 2
+    flag = lax.axis_index("solid") % 2
     put_rim(tiles, halo, flag, near, far, pairs)
-    for t in range(halo):
-        vector2[rows(t), :] = inner[rows(t), :] + select(flag, near[rows(t), :], far[rows(t), :])
+    offsets = arrived()
+    outside = [
+        ahead(t, jnp.maximum(t + offsets[t], halo), pairs, turned) for t in range(halo, tiles)
+    ]
+    size = halo * ROWS
+    vector2[0:size, :] = inner[...] + select(flag, near[0:size, :], far[0:size, :])
+    for t in range(halo):
+        put_pairs(pairs, t, vector2[rows(t), :])
+    quadratic = jnp.zeros((ROWS, LANES), F32)
+    for t in range(halo):
+        quadratic = quadratic + vector2[rows(t), :] * here(t, pairs, own)
     for t in range(halo, tiles):
-        partner = jnp.maximum(t + offsets[t], halo)
-        vector2[rows(t), :] = outer[rows(t - halo), :] + ahead(t, partner, pairs, turned)
-    for t in range(tiles):
-        put_pairs(pairs, t, vector2[rows(t), :])
-    inside = jnp.where(place[0] == last, 0.0, 1.0).astype(F32)
+        value = outer[rows(t - halo), :] + outside[t - halo]
+        vector2[rows(t), :] = value
+        put_pairs(pairs, t, value)
+    inside = jnp.where(lax.axis_index("solid") == last, 0.0, 1.0).astype(F32)
     for t in range(halo):
         other = rows(halo + t)
         rim = select(flag, far[other, :], near[other, :]) + leaving[rows(t), :]
         put_pairs(pairs, tiles + t, rim * inside)
+    for t in range(halo, tiles):
+        quadratic = quadratic + vector2[rows(t), :] * here(t, pairs, own)
+    v1, v2 = vector1[...], vector2[...]
+    total = row[...] + placed((moment(v1, v2), moment(v2, v2)), 3)
+    coupled = jnp.zeros((ROWS, LANES), F32)
     for t in range(tiles):
-        product[rows(t), :] = here(t, pairs, own) + 2.0 * ahead(t, t + offsets[t], pairs, turned)
-    v1, v2, v3 = vector1[...], vector2[...], product[...]
-    total = row[...] + placed((moment(v1, v2), moment(v2, v2), moment(v2, v3)), 3)
+        coupled = coupled + vector2[rows(t), :] * ahead(t, t + offsets[t], pairs, turned)
+    quadratic = jnp.sum(quadratic + 2.0 * coupled, axis=1, keepdims=True)
+    quadratic = jnp.concatenate([quadratic, jnp.zeros((ROWS, 1), F32)], axis=0)
+    total = total + placed((quadratic,), 5)
     total = jnp.sum(total, axis=0, keepdims=True)
-    out[...] = jnp.broadcast_to(total[:, None, :], out.shape)
+    out[...] = jnp.broadcast_to(total, out.shape)
 
 
 def last_kernel(tiles, moments, start, vector1, vector2, nodal, mixed):
-    total = jnp.sum(moments[...], axis=0)
-    total = jnp.broadcast_to(total, (2 * ROWS, LANES))
+    total = jnp.sum(moments[...].reshape(-1, 2 * ROWS, LANES), axis=0)
+    total = jnp.broadcast_to(jnp.sum(total, axis=0, keepdims=True), total.shape)
     g = [total if k == 0 else pltpu.roll(total, LANES - k * ROWS, 1) for k in range(MOMENTS)]
     h = [g[k + 1] + SHIFT * g[k] for k in range(MOMENTS - 1)]
 
@@ -413,18 +431,37 @@
         nodal[f] = mixed[pl.ds(f, tiles, stride=ROWS), :]
 
 
-def call(kernel, shapes, smem, vmem, scratch, name, work=0):
+def with_offsets(kernel):
+    def run(source, *refs):
+        *refs, offsets, sem = refs
+        copy = pltpu.make_async_copy(source, offsets, sem)
+        copy.start()
+
+        def arrived():
+            copy.wait()
+            return offsets
+
+        kernel(arrived, *refs)
+
+    return run
+
+
+def call(kernel, shapes, offsets, vmem, scratch, name, work=0):
     estimate = pl.CostEstimate(flops=work << 20, bytes_accessed=work << 16, transcendentals=0)
     return pl.pallas_call(
-        kernel,
+        with_offsets(kernel),
         out_shape=tuple(jax.ShapeDtypeStruct(s, F32) for s in shapes),
-        in_specs=[SMEM] * len(smem) + [VMEM] * len(vmem),
+        in_specs=[pl.BlockSpec(memory_space=pl.ANY)] + [VMEM] * len(vmem),
         out_specs=tuple(VMEM for _ in shapes),
-        scratch_shapes=scratch,
+        scratch_shapes=[
+            *scratch,
+            pltpu.SMEM(offsets.shape, jnp.int32),
+            pltpu.SemaphoreType.DMA(()),
+        ],
         compiler_params=pltpu.CompilerParams(vmem_limit_bytes=4 << 20),
         cost_estimate=estimate if work else None,
         name=name,
-    )(*smem, *vmem)
+    )(offsets, *vmem)
 
 
 def exchange(near, far, axis):
@@ -444,7 +481,6 @@
     total_blocks = block_fluid.shape[0]
     capacity = 5 * total_blocks // (2 * owners)
     chunk = capacity * 3 + ROWS
-    place = lax.axis_index("solid").astype(jnp.int32).reshape(1)
 
     sent = margin(block_fluid, block_solid, fluid_flux, margin_blocks, owners, tiles, chunk)
     received = lax.all_to_all(sent, "solid", split_axis=0, concat_axis=0, tiled=True)
@@ -461,7 +497,7 @@
     start, kept, near, far = call(
         functools.partial(first_send_kernel, tiles, halo),
         (whole, half, half, half),
-        (couple_offset, place),
+        couple_offset,
         (part, part1, part3, part2, matrices),
         [pairs, spread, products],
         "first_send",
@@ -470,7 +506,7 @@
     mapped, image = call(
         functools.partial(first_rest_kernel, tiles, halo),
         ((3, tiles, LANES), whole),
-        (couple_offset,),
+        couple_offset,
         (start, kept, matrices),
         [pairs, products, products],
         "first_rest",
@@ -479,7 +515,7 @@
     vector1, inner, kept, leaving, near, far = call(
         functools.partial(second_send_kernel, tiles, halo),
         (whole, half, half, half, whole, whole),
-        (couple_offset, place),
+        couple_offset,
         (image, far, near, matrices),
         [pairs, spread, products],
         "second_send",
@@ -488,7 +524,7 @@
     outer, row = call(
         functools.partial(second_rest_kernel, tiles, halo),
         (half, (2 * ROWS, LANES)),
-        (couple_offset,),
+        couple_offset,
         (start, vector1, kept, matrices),
         [pairs],
         "second_rest",
@@ -496,21 +532,24 @@
     )
     vector2, moments = call(
         functools.partial(third_kernel, tiles, halo, owners - 1),
-        (whole, (owners, 1, LANES)),
-        (couple_offset, place),
+        (whole, (owners, LANES)),
+        couple_offset,
         (vector1, inner, outer, leaving, row, far, near, matrices),
-        [pairs, pltpu.VMEM(whole, F32)],
+        [pairs],
         "third",
     )
+    moments = moments.reshape(owners, 1, LANES)
     moments = lax.all_to_all(moments, "solid", split_axis=0, concat_axis=0, tiled=True)
-    (nodal,) = call(
+    moments = moments.reshape(owners, LANES)
+    nodal = pl.pallas_call(
         functools.partial(last_kernel, tiles),
-        ((3, tiles, LANES),),
-        (),
-        (moments, start, vector1, vector2),
-        [pltpu.VMEM(whole, F32)],
-        "last",
-    )
+        out_shape=jax.ShapeDtypeStruct((3, tiles, LANES), F32),
+        in_specs=[VMEM] * 4,
+        out_specs=VMEM,
+        scratch_shapes=[pltpu.VMEM(whole, F32)],
+        compiler_params=pltpu.CompilerParams(vmem_limit_bytes=4 << 20),
+        name="last",
+    )(moments, start, vector1, vector2)
     return mapped, nodal
 
 

time: 64.5 us -> 64.3 us (level)
  no operation moved by 1% of the time
where the time goes in v4:
time: 64.3 us; the launch traced here: 64.1 us
  blocking collectives  37.4 us (58%)
  Pallas kernels  13.1 us (20%)
  starting transfers between devices  10.7 us (17%)
  waiting for transfers between devices  2.03 us (3%)
  between operations  0.76 us (1%)
    all_to_all x1, blocking collectives, local(): lax.all_to_all(sent, 'solid', split_axis=0, concat_axis=0, tiled=True)  22.2 us
    all_to_all x1, blocking collectives, local(): lax.all_to_all(moments, 'solid', split_axis=0, concat_axis=0, tiled=True)  15.2 us
    ppermute x2, starting transfers between devices, exchange(): far = lax.ppermute(far, axis, far_route)  6.78 us
    pallas_call x5, Pallas kernels, call(): pl.pallas_call(with_offsets(kernel), out_shape=tuple((jax.ShapeDtypeStruc...  6.35 us
    ppermute x3, starting transfers between devices, local(): lax.ppermute(part, 'fluid', [(i, i ^ d) for i in range(groups)])  3.79 us
    pallas_call x1, Pallas kernels, margin(): pl.pallas_call(functools.partial(margin_kernel, owners, own_tiles, chunk)...  2.88 us
    pallas_call x1, Pallas kernels, prepare(): pl.pallas_call(prepare_kernel, out_shape=jax.ShapeDtypeStruct((tiles, 6 *...  2.5 us
  transfers between devices with their start and end apart: 7, of which 2 were waited for; matrix products, arithmetic and copies ran while one was open for 0% of the time, Pallas kernels for 8%

profile of v4, /device:TPU:1, one launch (start us, length us, event | category | flops | bytes accessed | tf_op | source)
XLA Modules:
  0.0 64.1 jit_solution(4436172264360318093)
XLA Ops:
  0.6 2.9 %margin.1 = f32[1280,128]{1,0:T(8,128)S(1)} custom-call(s32[160]{0:T(256)} %fluid_hbm.1, s32[160]{0:T(256)} %solid_hbm.1, bf16[3,64,128]{2,1,0:T(8,128)(2,1)} %flux_hbm.1, bf16[160,128,128]{2,1,0:T(8,128)(2,1)} %blocks_hbm.1), custom_call_target="tpu_custom_call" | custom-call | tf_op jit(solution)/shard_map/margin/pallas_call | solution.py:105
  3.5 22.2 %all_to_all.16 = f32[32,40,128]{2,1,0:T(8,128)S(1)} all-to-all(f32[32,40,128]{2,1,0:T(8,128)S(1)} %bitcast.7), channel_id=1, replica_groups=mesh['fluid'=4,'solid'=32] {'solid'}, dimensions={0} | all-to-all | bytes 1310720 | tf_op jit(solution)/shard_map/all_to_all | solution.py:486
  25.7 0.5 combine.1.refs_0_
  26.2 0.0 copy-start
  26.3 3.0 %collective-permute-start.2 = (f32[96,128]{1,0:T(8,128)S(1)}, f32[96,128]{1,0:T(8,128)S(1)}, u32[]{:S(2)}, u32[]{:S(2)}) collective-permute-start(f32[96,128]{1,0:T(8,128)S(1)} %combine.1.refs_0_), channel_id=1, source_target_pairs={{0,64},{32,96},{64,0},{96,32},{1,65},{33,97},{65,1},{97,33},{2,66}... | collective-permute-start | bytes 147464 | tf_op jit(solution)/shard_map/ppermute | solution.py:490
  29.3 0.8 %collective-permute-start.1 = (f32[96,128]{1,0:T(8,128)S(1)}, f32[96,128]{1,0:T(8,128)S(1)}, u32[]{:S(2)}, u32[]{:S(2)}) collective-permute-start(f32[96,128]{1,0:T(8,128)S(1)} %combine.1.refs_0_), channel_id=1, source_target_pairs={{0,96},{32,64},{64,32},{96,0},{1,97},{33,65},{65,33},{97,1},{2,98}... | collective-permute-start | bytes 147464 | tf_op jit(solution)/shard_map/ppermute | solution.py:490
  30.1 0.0 collective-permute-start
  30.1 2.5 %prepare.1.refs_4_.refs_2_.refs_3_.refs_7_ = bf16[32,768,128]{2,1,0:T(8,128)(2,1)S(1)} custom-call(f32[32,128,128]{2,1,0:T(8,128)} %diag_hbm.1, f32[32,128,128]{2,1,0:T(8,128)} %couple_hbm.1), custom_call_target="tpu_custom_call" | custom-call | flops 67108864 | bytes 10485760 | tf_op jit(solution)/shard_map/prepare/pallas_call | solution.py:159
  32.6 0.0 collective-permute-done.2.refs_3_
  32.6 0.9 %collective-permute-done.1.refs_2_ = f32[96,128]{1,0:T(8,128)S(1)} collective-permute-done((f32[96,128]{1,0:T(8,128)S(1)}, f32[96,128]{1,0:T(8,128)S(1)}, u32[]{:S(2)}, u32[]{:S(2)}) %collective-permute-start.1) | collective-permute-done | bytes 49184 | tf_op jit(solution)/shard_map/ppermute | solution.py:490
  33.4 0.0 collective-permute-done.refs_1_
  33.4 0.0 copy-done
  33.4 0.6 first_send.1
  34.1 3.4 %collective-permute-start.3 = (f32[64,128]{1,0:T(8,128)S(1)}, f32[64,128]{1,0:T(8,128)S(1)}, u32[]{:S(2)}, u32[]{:S(2)}) collective-permute-start(f32[64,128]{1,0:T(8,128)S(1)} %get-tuple-element.22), channel_id=1, source_target_pairs={{1,2},{3,4},{5,6},{7,8},{9,10},{11,12},{13,14},{15,16},{17,18},{19... | collective-permute-start | bytes 98312 | tf_op jit(solution)/shard_map/ppermute | solution.py:471
  37.5 0.1 collective-permute-start.4
  37.6 1.7 %first_rest.1 = (f32[3,32,128]{2,1,0:T(8,128)}, f32[128,128]{1,0:T(8,128)S(1)}) custom-call(s32[32]{0:T(128)S(1)} %copy-done, f32[128,128]{1,0:T(8,128)S(1)} %get-tuple-element.18.refs_0_.start, f32[64,128]{1,0:T(8,128)S(1)} %get-tuple-element.19.refs_1_, bf16[32,768,128]{2,1,0:T(8,128)(2,1)S(1)} %prepare.1.refs_4_.refs_2_.refs_3_.refs_7_), custom_call_target="tpu_custom_call" | custom-call | flops 67108864 | bytes 4194304 | tf_op jit(solution)/shard_map/first_rest/pallas_call | solution.py:451
  39.4 0.0 collective-permute-done.3.refs_1_
  39.4 0.0 collective-permute-done.4.refs_2_
  39.4 1.5 %second_send.1 = (f32[128,128]{1,0:T(8,128)S(1)}, f32[64,128]{1,0:T(8,128)S(1)}, f32[64,128]{1,0:T(8,128)S(1)}, f32[64,128]{1,0:T(8,128)S(1)}, f32[128,128]{1,0:T(8,128)S(1)}, /*index=5*/f32[128,128]{1,0:T(8,128)S(1)}) custom-call(s32[32]{0:T(128)S(1)} %copy-done, f32[128,128]{1,0:T(8,128)S(1)} %get-tuple-element.21.refs_0_, ...), custom_call_target="tpu_custom_call" | custom-call | tf_op jit(solution)/shard_map/second_send/pallas_call | solution.py:451
  40.9 3.4 %collective-permute-start.5 = (f32[128,128]{1,0:T(8,128)S(1)}, f32[128,128]{1,0:T(8,128)S(1)}, u32[]{:S(2)}, u32[]{:S(2)}) collective-permute-start(f32[128,128]{1,0:T(8,128)S(1)} %get-tuple-element.30), channel_id=1, source_target_pairs={{1,2},{3,4},{5,6},{7,8},{9,10},{11,12},{13,14},{15,16},{17,18},{19... | collective-permute-start | bytes 196616 | tf_op jit(solution)/shard_map/ppermute | solution.py:471
  44.2 0.1 collective-permute-start.6
  44.3 0.9 %second_rest.1 = (f32[64,128]{1,0:T(8,128)S(1)}, f32[8,128]{1,0:T(8,128)S(1)}) custom-call(s32[32]{0:T(128)S(1)} %copy-done, f32[128,128]{1,0:T(8,128)S(1)} %get-tuple-element.18.refs_0_.start, f32[128,128]{1,0:T(8,128)S(1)} %get-tuple-element.24.refs_1_.refs_0_.vector1, f32[64,128]{1,0:T(8,128)S(1)} %get-tuple-element.26.refs_2_, ...), custom_call_target="tpu_custom_call" | custom-call | flops 67108864 | bytes 4194304 | tf_op jit(solution)/shard_map/second_rest/pallas_call | solution.py:451
  45.3 1.2 %collective-permute-done.5.refs_5_ = f32[128,128]{1,0:T(8,128)S(1)} collective-permute-done((f32[128,128]{1,0:T(8,128)S(1)}, f32[128,128]{1,0:T(8,128)S(1)}, u32[]{:S(2)}, u32[]{:S(2)}) %collective-permute-start.5) | collective-permute-done | bytes 65568 | tf_op jit(solution)/shard_map/ppermute | solution.py:471
  46.4 0.0 collective-permute-done.6.refs_6_
  46.4 1.6 %third.1 = (f32[128,128]{1,0:T(8,128)S(1)}, f32[32,128]{1,0:T(8,128)S(1)}) custom-call(s32[32]{0:T(128)S(1)} %copy-done, f32[128,128]{1,0:T(8,128)S(1)} %get-tuple-element.24.refs_1_.refs_0_.vector1, f32[64,128]{1,0:T(8,128)S(1)} %get-tuple-element.25.refs_1_, f32[64,128]{1,0:T(8,128)S(1)} %get-tuple-element.27.refs_2_, ...), custom_call_target="tpu_custom_call" | custom-call | tf_op jit(solution)/shard_map/third/pallas_call | solution.py:451
  48.0 15.2 %all_to_all.17 = f32[32,1,128]{2,1,0:T(1,128)S(1)} all-to-all(f32[32,1,128]{2,1,0:T(1,128)S(1)} %bitcast.9), channel_id=1, replica_groups=mesh['fluid'=4,'solid'=32] {'solid'}, dimensions={0} | all-to-all | bytes 32768 | tf_op jit(solution)/shard_map/all_to_all | solution.py:542
  63.2 0.9 %last.1 = f32[3,32,128]{2,1,0:T(8,128)} custom-call(f32[32,128]{1,0:T(8,128)S(1)} %bitcast.8, f32[128,128]{1,0:T(8,128)S(1)} %get-tuple-element.18.refs_0_.start, f32[128,128]{1,0:T(8,128)S(1)} %get-tuple-element.24.refs_1_.refs_0_.vector1, f32[128,128]{1,0:T(8,128)S(1)} %get-tuple-element.33.vector2), custom_call_target="tpu_custom_call" | custom-call | tf_op jit(solution)/shard_map/last/pallas_call | solution.py:544
Async XLA Ops:
  26.2 7.2 %copy-start = (s32[32]{0:T(128)S(1)}, s32[32]{0:T(128)}, u32[]{:S(2)}) copy-start(s32[32]{0:T(128)} %source.9) | copy-start | bytes 388
  26.3 6.3 %collective-permute-start.2 = (f32[96,128]{1,0:T(8,128)S(1)}, f32[96,128]{1,0:T(8,128)S(1)}, u32[]{:S(2)}, u32[]{:S(2)}) collective-permute-start(f32[96,128]{1,0:T(8,128)S(1)} %combine.1.refs_0_), channel_id=1, source_target_pairs={{0,64},{32,96},{64,0},{96,32},{1,65},{33,97},{65,1},{97,33},{2,66}... | collective-permute-start | bytes 147464 | tf_op jit(solution)/shard_map/ppermute | solution.py:490
  29.3 4.2 %collective-permute-start.1 = (f32[96,128]{1,0:T(8,128)S(1)}, f32[96,128]{1,0:T(8,128)S(1)}, u32[]{:S(2)}, u32[]{:S(2)}) collective-permute-start(f32[96,128]{1,0:T(8,128)S(1)} %combine.1.refs_0_), channel_id=1, source_target_pairs={{0,96},{32,64},{64,32},{96,0},{1,97},{33,65},{65,33},{97,1},{2,98}... | collective-permute-start | bytes 147464 | tf_op jit(solution)/shard_map/ppermute | solution.py:490
  30.1 3.4 %collective-permute-start = (f32[96,128]{1,0:T(8,128)S(1)}, f32[96,128]{1,0:T(8,128)S(1)}, u32[]{:S(2)}, u32[]{:S(2)}) collective-permute-start(f32[96,128]{1,0:T(8,128)S(1)} %combine.1.refs_0_), channel_id=1, source_target_pairs={{0,32},{32,0},{64,96},{96,64},{1,33},{33,1},{65,97},{97,65},{2,34}... | collective-permute-start | bytes 147464 | tf_op jit(solution)/shard_map/ppermute | solution.py:490
  34.1 5.3 %collective-permute-start.3 = (f32[64,128]{1,0:T(8,128)S(1)}, f32[64,128]{1,0:T(8,128)S(1)}, u32[]{:S(2)}, u32[]{:S(2)}) collective-permute-start(f32[64,128]{1,0:T(8,128)S(1)} %get-tuple-element.22), channel_id=1, source_target_pairs={{1,2},{3,4},{5,6},{7,8},{9,10},{11,12},{13,14},{15,16},{17,18},{19... | collective-permute-start | bytes 98312 | tf_op jit(solution)/shard_map/ppermute | solution.py:471
  37.5 1.9 %collective-permute-start.4 = (f32[64,128]{1,0:T(8,128)S(1)}, f32[64,128]{1,0:T(8,128)S(1)}, u32[]{:S(2)}, u32[]{:S(2)}) collective-permute-start(f32[64,128]{1,0:T(8,128)S(1)} %get-tuple-element.23), channel_id=1, source_target_pairs={{0,1},{1,0},{2,3},{3,2},{4,5},{5,4},{6,7},{7,6},{8,9},{9,8},{10,11... | collective-permute-start | bytes 98312 | tf_op jit(solution)/shard_map/ppermute | solution.py:472
  40.9 5.6 %collective-permute-start.5 = (f32[128,128]{1,0:T(8,128)S(1)}, f32[128,128]{1,0:T(8,128)S(1)}, u32[]{:S(2)}, u32[]{:S(2)}) collective-permute-start(f32[128,128]{1,0:T(8,128)S(1)} %get-tuple-element.30), channel_id=1, source_target_pairs={{1,2},{3,4},{5,6},{7,8},{9,10},{11,12},{13,14},{15,16},{17,18},{19... | collective-permute-start | bytes 196616 | tf_op jit(solution)/shard_map/ppermute | solution.py:471
  44.2 2.2 %collective-permute-start.6 = (f32[128,128]{1,0:T(8,128)S(1)}, f32[128,128]{1,0:T(8,128)S(1)}, u32[]{:S(2)}, u32[]{:S(2)}) collective-permute-start(f32[128,128]{1,0:T(8,128)S(1)} %get-tuple-element.31), channel_id=1, source_target_pairs={{0,1},{1,0},{2,3},{3,2},{4,5},{5,4},{6,7},{7,6},{8,9},{9,8},{10,11... | collective-permute-start | bytes 196616 | tf_op jit(solution)/shard_map/ppermute | solution.py:472

commit v5 on v4

--- a/solution.py
+++ b/solution.py
@@ -283,29 +283,54 @@
         pairs[tiles - halo + t] = jnp.zeros((2 * ROWS, LANES), F32)
 
 
-def second_send_kernel(tiles, halo, arrived, image, far, near, matrices, vector, inner, kept, leaving, near2, far2, pairs, spread, products):
+def inner_part(t, offsets, pairs, spread, own, turned):
+    return spread[t] + (here(t, pairs, own) + ahead(t, t + offsets[t], pairs, turned))
+
+
+def second_far_kernel(tiles, halo, arrived, image, far, near, matrices, vector, far2, pairs, spread, products):
     own, back, turned = views(matrices)
     flag = lax.axis_index("solid") % 2
+    size = halo * ROWS
     put_rim(tiles, halo, flag, near, far, pairs)
     offsets = arrived()
-    for t in range(halo):
-        vector[rows(t), :] = image[rows(t), :] + select(flag, near[rows(t), :], far[rows(t), :])
+    vector[0:size, :] = image[0:size, :] + select(flag, near[...], far[...])
     for t in range(halo, tiles):
         partner = jnp.maximum(t + offsets[t], halo)
         vector[rows(t), :] = image[rows(t), :] + ahead(t, partner, pairs, turned)
     for t in range(tiles):
         put_pairs(pairs, t, vector[rows(t), :])
     spread[...] = jnp.zeros_like(spread)
+
+    @pl.when(flag == 1)
+    def _():
+        add_transposed(tiles, lambda: offsets, pairs, spread, back, products, halo, tiles)
+        for t in range(halo):
+            far2[rows(t), :] = spread[tiles + t]
+        far2[size : 2 * size, :] = jnp.zeros((size, LANES), F32)
+
+    @pl.when(flag == 0)
+    def _():
+        add_transposed(tiles, lambda: offsets, pairs, spread, back, products, 0, halo)
+        far2[0:size, :] = vector[0:size, :]
+        for t in range(halo):
+            far2[rows(halo + t), :] = inner_part(t, offsets, pairs, spread, own, turned)
+
+
+def second_near_kernel(tiles, halo, arrived, vector, matrices, inner, kept, leaving, near2, pairs, spread, products):
+    own, back, turned = views(matrices)
+    flag = lax.axis_index("solid") % 2
+    size = halo * ROWS
+    for t in range(tiles):
+        put_pairs(pairs, t, vector[rows(t), :])
+    spread[...] = jnp.zeros_like(spread)
+    offsets = arrived()
     add_transposed(tiles, lambda: offsets, pairs, spread, back, products, 0, tiles)
-    size = halo * ROWS
     for t in range(halo):
-        inner[rows(t), :] = spread[t] + (here(t, pairs, own) + ahead(t, t + offsets[t], pairs, turned))
+        inner[rows(t), :] = inner_part(t, offsets, pairs, spread, own, turned)
         kept[rows(t), :] = spread[halo + t]
         leaving[rows(t), :] = spread[tiles + t]
     near2[0:size, :] = select(flag, vector[0:size, :], leaving[...])
-    far2[0:size, :] = select(flag, leaving[...], vector[0:size, :])
     near2[size : 2 * size, :] = inner[...]
-    far2[size : 2 * size, :] = inner[...]
 
 
 def moment(a, b):
@@ -464,18 +489,16 @@
     )(offsets, *vmem)
 
 
-def exchange(near, far, axis):
-    n = lax.axis_size(axis)
+def halo_routes(n):
     far_route = [(i, i + 1) for i in range(1, n - 1, 2)] + [(i + 1, i) for i in range(1, n - 1, 2)]
     near_route = [(i, i ^ 1) for i in range(n)]
-    far = lax.ppermute(far, axis, far_route)
-    near = lax.ppermute(near, axis, near_route)
-    return near, far
+    return near_route, far_route
 
 
 def local(fluid_flux, margin_blocks, block_fluid, block_solid, diag_blocks, couple_blocks, couple_offset):
     owners = lax.axis_size("solid")
     groups = lax.axis_size("fluid")
+    near_route, far_route = halo_routes(owners)
     tiles = diag_blocks.shape[0]
     halo = tiles // 2
     total_blocks = block_fluid.shape[0]
@@ -502,7 +525,8 @@
         [pairs, spread, products],
         "first_send",
     )
-    near, far = exchange(near, far, "solid")
+    far = lax.ppermute(far, "solid", far_route)
+    near = lax.ppermute(near, "solid", near_route)
     mapped, image = call(
         functools.partial(first_rest_kernel, tiles, halo),
         ((3, tiles, LANES), whole),
@@ -512,15 +536,25 @@
         "first_rest",
         64,
     )
-    vector1, inner, kept, leaving, near, far = call(
-        functools.partial(second_send_kernel, tiles, halo),
-        (whole, half, half, half, whole, whole),
+    vector1, far = call(
+        functools.partial(second_far_kernel, tiles, halo),
+        (whole, whole),
         couple_offset,
         (image, far, near, matrices),
         [pairs, spread, products],
-        "second_send",
-    )
-    near, far = exchange(near, far, "solid")
+        "second_far",
+    )
+    far = lax.ppermute(far, "solid", far_route)
+    inner, kept, leaving, near = call(
+        functools.partial(second_near_kernel, tiles, halo),
+        (half, half, half, whole),
+        couple_offset,
+        (vector1, matrices),
+        [pairs, spread, products],
+        "second_near",
+        64,
+    )
+    near = lax.ppermute(near, "solid", near_route)
     outer, row = call(
         functools.partial(second_rest_kernel, tiles, halo),
         (half, (2 * ROWS, LANES)),

time: 64.3 us -> 64.2 us (level)
  Pallas kernels: 13.1 us -> 14 us
  waiting for transfers between devices: 2.03 us -> 1.15 us
    ppermute x4, waiting for transfers between devices: 1.17 us -> 0.28 us  [the longest x2 0.28 us: local(): near = lax.ppermute(near, 'solid', near_route)]
    pallas_call x5 -> x6, Pallas kernels: 6.35 us -> 7.21 us  [call(): pl.pallas_call(with_offsets(kernel), out_shape=tuple((jax.ShapeDtypeStruc...]
  transfers between devices with their start and end apart: 7 -> 7, of which waited for: 2 -> 2; matrix products, arithmetic and copies ran while one was open for 0% -> 0% of each run, Pallas kernels for 8% -> 10%
where the time goes in v5:
time: 64.2 us; the launch traced here: 64 us
  blocking collectives  37 us (58%)
  Pallas kernels  14 us (22%)
  starting transfers between devices  11.1 us (17%)
  waiting for transfers between devices  1.15 us (2%)
  between operations  0.78 us (1%)
    all_to_all x1, blocking collectives, local(): lax.all_to_all(sent, 'solid', split_axis=0, concat_axis=0, tiled=True)  22.2 us
    all_to_all x1, blocking collectives, local(): lax.all_to_all(moments, 'solid', split_axis=0, concat_axis=0, tiled=True)  14.8 us
    pallas_call x6, Pallas kernels, call(): pl.pallas_call(with_offsets(kernel), out_shape=tuple((jax.ShapeDtypeStruc...  7.21 us
    ppermute x2, starting transfers between devices, local(): far = lax.ppermute(far, 'solid', far_route)  7.09 us
    ppermute x3, starting transfers between devices, local(): lax.ppermute(part, 'fluid', [(i, i ^ d) for i in range(groups)])  3.8 us
    pallas_call x1, Pallas kernels, margin(): pl.pallas_call(functools.partial(margin_kernel, owners, own_tiles, chunk)...  2.89 us
    pallas_call x1, Pallas kernels, prepare(): pl.pallas_call(prepare_kernel, out_shape=jax.ShapeDtypeStruct((tiles, 6 *...  2.5 us
  transfers between devices with their start and end apart: 7, of which 2 were waited for; matrix products, arithmetic and copies ran while one was open for 0% of the time, Pallas kernels for 10%

profile of v5, /device:TPU:1, one launch (start us, length us, event | category | flops | bytes accessed | tf_op | source)
XLA Modules:
  0.0 64.0 jit_solution(7642732273131762361)
XLA Ops:
  0.6 2.9 %margin.1 = f32[1280,128]{1,0:T(8,128)S(1)} custom-call(s32[160]{0:T(256)} %fluid_hbm.1, s32[160]{0:T(256)} %solid_hbm.1, bf16[3,64,128]{2,1,0:T(8,128)(2,1)} %flux_hbm.1, bf16[160,128,128]{2,1,0:T(8,128)(2,1)} %blocks_hbm.1), custom_call_target="tpu_custom_call" | custom-call | tf_op jit(solution)/shard_map/margin/pallas_call | solution.py:105
  3.5 22.2 %all_to_all.16 = f32[32,40,128]{2,1,0:T(8,128)S(1)} all-to-all(f32[32,40,128]{2,1,0:T(8,128)S(1)} %bitcast.7), channel_id=1, replica_groups=mesh['fluid'=4,'solid'=32] {'solid'}, dimensions={0} | all-to-all | bytes 1310720 | tf_op jit(solution)/shard_map/all_to_all | solution.py:509
  25.7 0.5 combine.1.refs_0_
  26.2 0.0 copy-start
  26.3 3.0 %collective-permute-start.2 = (f32[96,128]{1,0:T(8,128)S(1)}, f32[96,128]{1,0:T(8,128)S(1)}, u32[]{:S(2)}, u32[]{:S(2)}) collective-permute-start(f32[96,128]{1,0:T(8,128)S(1)} %combine.1.refs_0_), channel_id=1, source_target_pairs={{0,64},{32,96},{64,0},{96,32},{1,65},{33,97},{65,1},{97,33},{2,66}... | collective-permute-start | bytes 147464 | tf_op jit(solution)/shard_map/ppermute | solution.py:513
  29.3 0.8 %collective-permute-start.1 = (f32[96,128]{1,0:T(8,128)S(1)}, f32[96,128]{1,0:T(8,128)S(1)}, u32[]{:S(2)}, u32[]{:S(2)}) collective-permute-start(f32[96,128]{1,0:T(8,128)S(1)} %combine.1.refs_0_), channel_id=1, source_target_pairs={{0,96},{32,64},{64,32},{96,0},{1,97},{33,65},{65,33},{97,1},{2,98}... | collective-permute-start | bytes 147464 | tf_op jit(solution)/shard_map/ppermute | solution.py:513
  30.1 0.0 collective-permute-start
  30.1 2.5 %prepare.1.refs_4_.refs_2_.refs_3_.refs_1_.refs_7_ = bf16[32,768,128]{2,1,0:T(8,128)(2,1)S(1)} custom-call(f32[32,128,128]{2,1,0:T(8,128)} %diag_hbm.1, f32[32,128,128]{2,1,0:T(8,128)} %couple_hbm.1), custom_call_target="tpu_custom_call" | custom-call | flops 67108864 | bytes 10485760 | tf_op jit(solution)/shard_map/prepare/pallas_call | solution.py:159
  32.6 0.0 collective-permute-done.2.refs_3_
  32.6 0.9 %collective-permute-done.1.refs_2_ = f32[96,128]{1,0:T(8,128)S(1)} collective-permute-done((f32[96,128]{1,0:T(8,128)S(1)}, f32[96,128]{1,0:T(8,128)S(1)}, u32[]{:S(2)}, u32[]{:S(2)}) %collective-permute-start.1) | collective-permute-done | bytes 49184 | tf_op jit(solution)/shard_map/ppermute | solution.py:513
  33.4 0.0 collective-permute-done.refs_1_
  33.4 0.0 copy-done
  33.4 0.6 first_send.1
  34.1 3.4 %collective-permute-start.3 = (f32[64,128]{1,0:T(8,128)S(1)}, f32[64,128]{1,0:T(8,128)S(1)}, u32[]{:S(2)}, u32[]{:S(2)}) collective-permute-start(f32[64,128]{1,0:T(8,128)S(1)} %get-tuple-element.22), channel_id=1, source_target_pairs={{1,2},{3,4},{5,6},{7,8},{9,10},{11,12},{13,14},{15,16},{17,18},{19... | collective-permute-start | bytes 98312 | tf_op jit(solution)/shard_map/ppermute | solution.py:528
  37.5 0.1 collective-permute-start.4
  37.6 1.7 %first_rest.1 = (f32[3,32,128]{2,1,0:T(8,128)}, f32[128,128]{1,0:T(8,128)S(1)}) custom-call(s32[32]{0:T(128)S(1)} %copy-done, f32[128,128]{1,0:T(8,128)S(1)} %get-tuple-element.18.refs_0_.start, f32[64,128]{1,0:T(8,128)S(1)} %get-tuple-element.19.refs_1_, bf16[32,768,128]{2,1,0:T(8,128)(2,1)S(1)} %prepare.1.refs_4_.refs_2_.refs_3_.refs_1_.refs_7_), custom_call_target="tpu_custom_call" | custom-call | flops 67108864 | bytes 4194304 | tf_op jit(solution)/shard_map/first_rest/pallas_call | solution.py:476
  39.4 0.0 collective-permute-done.3.refs_1_
  39.4 0.0 collective-permute-done.4.refs_2_
  39.4 1.1 %second_far.1 = (f32[128,128]{1,0:T(8,128)S(1)}, f32[128,128]{1,0:T(8,128)S(1)}) custom-call(s32[32]{0:T(128)S(1)} %copy-done, f32[128,128]{1,0:T(8,128)S(1)} %get-tuple-element.21.refs_0_, f32[64,128]{1,0:T(8,128)S(1)} %collective-permute-done.3.refs_1_, f32[64,128]{1,0:T(8,128)S(1)} %collective-permute-done.4.refs_2_, ...), custom_call_target="tpu_custom_call" | custom-call | tf_op jit(solution)/shard_map/second_far/pallas_call | solution.py:476
  40.5 3.7 %collective-permute-start.5 = (f32[128,128]{1,0:T(8,128)S(1)}, f32[128,128]{1,0:T(8,128)S(1)}, u32[]{:S(2)}, u32[]{:S(2)}) collective-permute-start(f32[128,128]{1,0:T(8,128)S(1)} %get-tuple-element.30), channel_id=1, source_target_pairs={{1,2},{3,4},{5,6},{7,8},{9,10},{11,12},{13,14},{15,16},{17,18},{19... | collective-permute-start | bytes 196616 | tf_op jit(solution)/shard_map/ppermute | solution.py:547
  44.1 1.3 %second_near.1 = (f32[64,128]{1,0:T(8,128)S(1)}, f32[64,128]{1,0:T(8,128)S(1)}, f32[64,128]{1,0:T(8,128)S(1)}, f32[128,128]{1,0:T(8,128)S(1)}) custom-call(s32[32]{0:T(128)S(1)} %copy-done, f32[128,128]{1,0:T(8,128)S(1)} %get-tuple-element.24.refs_0_.refs_1_.vector1, bf16[32,768,128]{2,1,0:T(8,128)(2,1)S(1)} %prepare.1.refs_4_.refs_2_.refs_3_.refs_1_.refs_7_), custom_call_target="tpu_custom_call" | custom-call | flops 67108864 | bytes 4194304 | tf_op jit(solution)/shard_map/second_near/pallas_call | solution.py:476
  45.4 0.1 collective-permute-start.6
  45.5 0.9 %second_rest.1 = (f32[64,128]{1,0:T(8,128)S(1)}, f32[8,128]{1,0:T(8,128)S(1)}) custom-call(s32[32]{0:T(128)S(1)} %copy-done, f32[128,128]{1,0:T(8,128)S(1)} %get-tuple-element.18.refs_0_.start, f32[128,128]{1,0:T(8,128)S(1)} %get-tuple-element.24.refs_0_.refs_1_.vector1, f32[64,128]{1,0:T(8,128)S(1)} %get-tuple-element.26.refs_2_, ...), custom_call_target="tpu_custom_call" | custom-call | flops 67108864 | bytes 4194304 | tf_op jit(solution)/shard_map/second_rest/pallas_call | solution.py:476
  46.5 0.0 collective-permute-done.5.refs_5_
  46.5 0.3 collective-permute-done.6.refs_6_
  46.7 1.6 %third.1 = (f32[128,128]{1,0:T(8,128)S(1)}, f32[32,128]{1,0:T(8,128)S(1)}) custom-call(s32[32]{0:T(128)S(1)} %copy-done, f32[128,128]{1,0:T(8,128)S(1)} %get-tuple-element.24.refs_0_.refs_1_.vector1, f32[64,128]{1,0:T(8,128)S(1)} %get-tuple-element.25.refs_1_, f32[64,128]{1,0:T(8,128)S(1)} %get-tuple-element.27.refs_2_, ...), custom_call_target="tpu_custom_call" | custom-call | tf_op jit(solution)/shard_map/third/pallas_call | solution.py:476
  48.3 14.8 %all_to_all.17 = f32[32,1,128]{2,1,0:T(1,128)S(1)} all-to-all(f32[32,1,128]{2,1,0:T(1,128)S(1)} %bitcast.9), channel_id=1, replica_groups=mesh['fluid'=4,'solid'=32] {'solid'}, dimensions={0} | all-to-all | bytes 32768 | tf_op jit(solution)/shard_map/all_to_all | solution.py:576
  63.1 0.9 %last.1 = f32[3,32,128]{2,1,0:T(8,128)} custom-call(f32[32,128]{1,0:T(8,128)S(1)} %bitcast.8, f32[128,128]{1,0:T(8,128)S(1)} %get-tuple-element.18.refs_0_.start, f32[128,128]{1,0:T(8,128)S(1)} %get-tuple-element.24.refs_0_.refs_1_.vector1, f32[128,128]{1,0:T(8,128)S(1)} %get-tuple-element.33.vector2), custom_call_target="tpu_custom_call" | custom-call | tf_op jit(solution)/shard_map/last/pallas_call | solution.py:578
Async XLA Ops:
  26.2 7.2 %copy-start = (s32[32]{0:T(128)S(1)}, s32[32]{0:T(128)}, u32[]{:S(2)}) copy-start(s32[32]{0:T(128)} %source.11) | copy-start | bytes 388
  26.3 6.3 %collective-permute-start.2 = (f32[96,128]{1,0:T(8,128)S(1)}, f32[96,128]{1,0:T(8,128)S(1)}, u32[]{:S(2)}, u32[]{:S(2)}) collective-permute-start(f32[96,128]{1,0:T(8,128)S(1)} %combine.1.refs_0_), channel_id=1, source_target_pairs={{0,64},{32,96},{64,0},{96,32},{1,65},{33,97},{65,1},{97,33},{2,66}... | collective-permute-start | bytes 147464 | tf_op jit(solution)/shard_map/ppermute | solution.py:513
  29.3 4.2 %collective-permute-start.1 = (f32[96,128]{1,0:T(8,128)S(1)}, f32[96,128]{1,0:T(8,128)S(1)}, u32[]{:S(2)}, u32[]{:S(2)}) collective-permute-start(f32[96,128]{1,0:T(8,128)S(1)} %combine.1.refs_0_), channel_id=1, source_target_pairs={{0,96},{32,64},{64,32},{96,0},{1,97},{33,65},{65,33},{97,1},{2,98}... | collective-permute-start | bytes 147464 | tf_op jit(solution)/shard_map/ppermute | solution.py:513
  30.1 3.4 %collective-permute-start = (f32[96,128]{1,0:T(8,128)S(1)}, f32[96,128]{1,0:T(8,128)S(1)}, u32[]{:S(2)}, u32[]{:S(2)}) collective-permute-start(f32[96,128]{1,0:T(8,128)S(1)} %combine.1.refs_0_), channel_id=1, source_target_pairs={{0,32},{32,0},{64,96},{96,64},{1,33},{33,1},{65,97},{97,65},{2,34}... | collective-permute-start | bytes 147464 | tf_op jit(solution)/shard_map/ppermute | solution.py:513
  34.1 5.3 %collective-permute-start.3 = (f32[64,128]{1,0:T(8,128)S(1)}, f32[64,128]{1,0:T(8,128)S(1)}, u32[]{:S(2)}, u32[]{:S(2)}) collective-permute-start(f32[64,128]{1,0:T(8,128)S(1)} %get-tuple-element.22), channel_id=1, source_target_pairs={{1,2},{3,4},{5,6},{7,8},{9,10},{11,12},{13,14},{15,16},{17,18},{19... | collective-permute-start | bytes 98312 | tf_op jit(solution)/shard_map/ppermute | solution.py:528
  37.5 1.9 %collective-permute-start.4 = (f32[64,128]{1,0:T(8,128)S(1)}, f32[64,128]{1,0:T(8,128)S(1)}, u32[]{:S(2)}, u32[]{:S(2)}) collective-permute-start(f32[64,128]{1,0:T(8,128)S(1)} %get-tuple-element.23), channel_id=1, source_target_pairs={{0,1},{1,0},{2,3},{3,2},{4,5},{5,4},{6,7},{7,6},{8,9},{9,8},{10,11... | collective-permute-start | bytes 98312 | tf_op jit(solution)/shard_map/ppermute | solution.py:529
  40.5 6.0 %collective-permute-start.5 = (f32[128,128]{1,0:T(8,128)S(1)}, f32[128,128]{1,0:T(8,128)S(1)}, u32[]{:S(2)}, u32[]{:S(2)}) collective-permute-start(f32[128,128]{1,0:T(8,128)S(1)} %get-tuple-element.30), channel_id=1, source_target_pairs={{1,2},{3,4},{5,6},{7,8},{9,10},{11,12},{13,14},{15,16},{17,18},{19... | collective-permute-start | bytes 196616 | tf_op jit(solution)/shard_map/ppermute | solution.py:547
  45.4 1.3 %collective-permute-start.6 = (f32[128,128]{1,0:T(8,128)S(1)}, f32[128,128]{1,0:T(8,128)S(1)}, u32[]{:S(2)}, u32[]{:S(2)}) collective-permute-start(f32[128,128]{1,0:T(8,128)S(1)} %get-tuple-element.31), channel_id=1, source_target_pairs={{0,1},{1,0},{2,3},{3,2},{4,5},{5,4},{6,7},{7,6},{8,9},{9,8},{10,11... | collective-permute-start | bytes 196616 | tf_op jit(solution)/shard_map/ppermute | solution.py:557

commit v6 on v4

--- a/solution.py
+++ b/solution.py
@@ -99,7 +99,7 @@
 
 def margin(fluid_ids, solid_ids, flux, blocks, owners, own_tiles, chunk):
     assert own_tiles & (own_tiles - 1) == 0
-    pieces = 5
+    pieces = 8
     assert blocks.shape[0] % (2 * pieces) == 0
     table = pltpu.VMEM((flux.shape[1] * 2 * ROWS, LANES), F32)
     return pl.pallas_call(

time: 64.3 us -> 64.3 us (level)
  no operation moved by 1% of the time
where the time goes in v6:
time: 64.3 us; the launch traced here: 64 us
  blocking collectives  37.4 us (58%)
  Pallas kernels  13.1 us (20%)
  starting transfers between devices  10.8 us (17%)
  waiting for transfers between devices  2.04 us (3%)
  between operations  0.76 us (1%)
    all_to_all x1, blocking collectives, local(): lax.all_to_all(sent, 'solid', split_axis=0, concat_axis=0, tiled=True)  22.2 us
    all_to_all x1, blocking collectives, local(): lax.all_to_all(moments, 'solid', split_axis=0, concat_axis=0, tiled=True)  15.2 us
    ppermute x2, starting transfers between devices, exchange(): far = lax.ppermute(far, axis, far_route)  6.79 us
    pallas_call x5, Pallas kernels, call(): pl.pallas_call(with_offsets(kernel), out_shape=tuple((jax.ShapeDtypeStruc...  6.33 us
    ppermute x3, starting transfers between devices, local(): lax.ppermute(part, 'fluid', [(i, i ^ d) for i in range(groups)])  3.79 us
    pallas_call x1, Pallas kernels, margin(): pl.pallas_call(functools.partial(margin_kernel, owners, own_tiles, chunk)...  2.87 us
    pallas_call x1, Pallas kernels, prepare(): pl.pallas_call(prepare_kernel, out_shape=jax.ShapeDtypeStruct((tiles, 6 *...  2.5 us
  transfers between devices with their start and end apart: 7, of which 2 were waited for; matrix products, arithmetic and copies ran while one was open for 0% of the time, Pallas kernels for 8%

profile of v6, /device:TPU:1, one launch (start us, length us, event | category | flops | bytes accessed | tf_op | source)
XLA Modules:
  0.0 64.0 jit_solution(6494029619746228666)
XLA Ops:
  0.6 2.9 %margin.1 = f32[1280,128]{1,0:T(8,128)S(1)} custom-call(s32[160]{0:T(256)} %fluid_hbm.1, s32[160]{0:T(256)} %solid_hbm.1, bf16[3,64,128]{2,1,0:T(8,128)(2,1)} %flux_hbm.1, bf16[160,128,128]{2,1,0:T(8,128)(2,1)} %blocks_hbm.1), custom_call_target="tpu_custom_call" | custom-call | tf_op jit(solution)/shard_map/margin/pallas_call | solution.py:105
  3.5 22.2 %all_to_all.16 = f32[32,40,128]{2,1,0:T(8,128)S(1)} all-to-all(f32[32,40,128]{2,1,0:T(8,128)S(1)} %bitcast.7), channel_id=1, replica_groups=mesh['fluid'=4,'solid'=32] {'solid'}, dimensions={0} | all-to-all | bytes 1310720 | tf_op jit(solution)/shard_map/all_to_all | solution.py:486
  25.7 0.5 combine.1.refs_0_
  26.2 0.0 copy-start
  26.2 3.0 %collective-permute-start.2 = (f32[96,128]{1,0:T(8,128)S(1)}, f32[96,128]{1,0:T(8,128)S(1)}, u32[]{:S(2)}, u32[]{:S(2)}) collective-permute-start(f32[96,128]{1,0:T(8,128)S(1)} %combine.1.refs_0_), channel_id=1, source_target_pairs={{0,64},{32,96},{64,0},{96,32},{1,65},{33,97},{65,1},{97,33},{2,66}... | collective-permute-start | bytes 147464 | tf_op jit(solution)/shard_map/ppermute | solution.py:490
  29.2 0.8 %collective-permute-start.1 = (f32[96,128]{1,0:T(8,128)S(1)}, f32[96,128]{1,0:T(8,128)S(1)}, u32[]{:S(2)}, u32[]{:S(2)}) collective-permute-start(f32[96,128]{1,0:T(8,128)S(1)} %combine.1.refs_0_), channel_id=1, source_target_pairs={{0,96},{32,64},{64,32},{96,0},{1,97},{33,65},{65,33},{97,1},{2,98}... | collective-permute-start | bytes 147464 | tf_op jit(solution)/shard_map/ppermute | solution.py:490
  30.0 0.0 collective-permute-start
  30.0 2.5 %prepare.1.refs_4_.refs_2_.refs_3_.refs_7_ = bf16[32,768,128]{2,1,0:T(8,128)(2,1)S(1)} custom-call(f32[32,128,128]{2,1,0:T(8,128)} %diag_hbm.1, f32[32,128,128]{2,1,0:T(8,128)} %couple_hbm.1), custom_call_target="tpu_custom_call" | custom-call | flops 67108864 | bytes 10485760 | tf_op jit(solution)/shard_map/prepare/pallas_call | solution.py:159
  32.5 0.0 collective-permute-done.2.refs_3_
  32.6 0.9 %collective-permute-done.1.refs_2_ = f32[96,128]{1,0:T(8,128)S(1)} collective-permute-done((f32[96,128]{1,0:T(8,128)S(1)}, f32[96,128]{1,0:T(8,128)S(1)}, u32[]{:S(2)}, u32[]{:S(2)}) %collective-permute-start.1) | collective-permute-done | bytes 49184 | tf_op jit(solution)/shard_map/ppermute | solution.py:490
  33.4 0.0 collective-permute-done.refs_1_
  33.4 0.0 copy-done
  33.4 0.6 first_send.1
  34.1 3.4 %collective-permute-start.3 = (f32[64,128]{1,0:T(8,128)S(1)}, f32[64,128]{1,0:T(8,128)S(1)}, u32[]{:S(2)}, u32[]{:S(2)}) collective-permute-start(f32[64,128]{1,0:T(8,128)S(1)} %get-tuple-element.22), channel_id=1, source_target_pairs={{1,2},{3,4},{5,6},{7,8},{9,10},{11,12},{13,14},{15,16},{17,18},{19... | collective-permute-start | bytes 98312 | tf_op jit(solution)/shard_map/ppermute | solution.py:471
  37.5 0.1 collective-permute-start.4
  37.6 1.7 %first_rest.1 = (f32[3,32,128]{2,1,0:T(8,128)}, f32[128,128]{1,0:T(8,128)S(1)}) custom-call(s32[32]{0:T(128)S(1)} %copy-done, f32[128,128]{1,0:T(8,128)S(1)} %get-tuple-element.18.refs_0_.start, f32[64,128]{1,0:T(8,128)S(1)} %get-tuple-element.19.refs_1_, bf16[32,768,128]{2,1,0:T(8,128)(2,1)S(1)} %prepare.1.refs_4_.refs_2_.refs_3_.refs_7_), custom_call_target="tpu_custom_call" | custom-call | flops 67108864 | bytes 4194304 | tf_op jit(solution)/shard_map/first_rest/pallas_call | solution.py:451
  39.3 0.0 collective-permute-done.3.refs_1_
  39.4 0.0 collective-permute-done.4.refs_2_
  39.4 1.5 %second_send.1 = (f32[128,128]{1,0:T(8,128)S(1)}, f32[64,128]{1,0:T(8,128)S(1)}, f32[64,128]{1,0:T(8,128)S(1)}, f32[64,128]{1,0:T(8,128)S(1)}, f32[128,128]{1,0:T(8,128)S(1)}, /*index=5*/f32[128,128]{1,0:T(8,128)S(1)}) custom-call(s32[32]{0:T(128)S(1)} %copy-done, f32[128,128]{1,0:T(8,128)S(1)} %get-tuple-element.21.refs_0_, ...), custom_call_target="tpu_custom_call" | custom-call | tf_op jit(solution)/shard_map/second_send/pallas_call | solution.py:451
  40.8 3.4 %collective-permute-start.5 = (f32[128,128]{1,0:T(8,128)S(1)}, f32[128,128]{1,0:T(8,128)S(1)}, u32[]{:S(2)}, u32[]{:S(2)}) collective-permute-start(f32[128,128]{1,0:T(8,128)S(1)} %get-tuple-element.30), channel_id=1, source_target_pairs={{1,2},{3,4},{5,6},{7,8},{9,10},{11,12},{13,14},{15,16},{17,18},{19... | collective-permute-start | bytes 196616 | tf_op jit(solution)/shard_map/ppermute | solution.py:471
  44.2 0.1 collective-permute-start.6
  44.3 0.9 %second_rest.1 = (f32[64,128]{1,0:T(8,128)S(1)}, f32[8,128]{1,0:T(8,128)S(1)}) custom-call(s32[32]{0:T(128)S(1)} %copy-done, f32[128,128]{1,0:T(8,128)S(1)} %get-tuple-element.18.refs_0_.start, f32[128,128]{1,0:T(8,128)S(1)} %get-tuple-element.24.refs_1_.refs_0_.vector1, f32[64,128]{1,0:T(8,128)S(1)} %get-tuple-element.26.refs_2_, ...), custom_call_target="tpu_custom_call" | custom-call | flops 67108864 | bytes 4194304 | tf_op jit(solution)/shard_map/second_rest/pallas_call | solution.py:451
  45.2 1.2 %collective-permute-done.5.refs_5_ = f32[128,128]{1,0:T(8,128)S(1)} collective-permute-done((f32[128,128]{1,0:T(8,128)S(1)}, f32[128,128]{1,0:T(8,128)S(1)}, u32[]{:S(2)}, u32[]{:S(2)}) %collective-permute-start.5) | collective-permute-done | bytes 65568 | tf_op jit(solution)/shard_map/ppermute | solution.py:471
  46.4 0.0 collective-permute-done.6.refs_6_
  46.4 1.6 %third.1 = (f32[128,128]{1,0:T(8,128)S(1)}, f32[32,128]{1,0:T(8,128)S(1)}) custom-call(s32[32]{0:T(128)S(1)} %copy-done, f32[128,128]{1,0:T(8,128)S(1)} %get-tuple-element.24.refs_1_.refs_0_.vector1, f32[64,128]{1,0:T(8,128)S(1)} %get-tuple-element.25.refs_1_, f32[64,128]{1,0:T(8,128)S(1)} %get-tuple-element.27.refs_2_, ...), custom_call_target="tpu_custom_call" | custom-call | tf_op jit(solution)/shard_map/third/pallas_call | solution.py:451
  48.0 15.2 %all_to_all.17 = f32[32,1,128]{2,1,0:T(1,128)S(1)} all-to-all(f32[32,1,128]{2,1,0:T(1,128)S(1)} %bitcast.9), channel_id=1, replica_groups=mesh['fluid'=4,'solid'=32] {'solid'}, dimensions={0} | all-to-all | bytes 32768 | tf_op jit(solution)/shard_map/all_to_all | solution.py:542
  63.2 0.9 %last.1 = f32[3,32,128]{2,1,0:T(8,128)} custom-call(f32[32,128]{1,0:T(8,128)S(1)} %bitcast.8, f32[128,128]{1,0:T(8,128)S(1)} %get-tuple-element.18.refs_0_.start, f32[128,128]{1,0:T(8,128)S(1)} %get-tuple-element.24.refs_1_.refs_0_.vector1, f32[128,128]{1,0:T(8,128)S(1)} %get-tuple-element.33.vector2), custom_call_target="tpu_custom_call" | custom-call | tf_op jit(solution)/shard_map/last/pallas_call | solution.py:544
Async XLA Ops:
  26.2 7.2 %copy-start = (s32[32]{0:T(128)S(1)}, s32[32]{0:T(128)}, u32[]{:S(2)}) copy-start(s32[32]{0:T(128)} %source.9) | copy-start | bytes 388
  26.2 6.3 %collective-permute-start.2 = (f32[96,128]{1,0:T(8,128)S(1)}, f32[96,128]{1,0:T(8,128)S(1)}, u32[]{:S(2)}, u32[]{:S(2)}) collective-permute-start(f32[96,128]{1,0:T(8,128)S(1)} %combine.1.refs_0_), channel_id=1, source_target_pairs={{0,64},{32,96},{64,0},{96,32},{1,65},{33,97},{65,1},{97,33},{2,66}... | collective-permute-start | bytes 147464 | tf_op jit(solution)/shard_map/ppermute | solution.py:490
  29.2 4.2 %collective-permute-start.1 = (f32[96,128]{1,0:T(8,128)S(1)}, f32[96,128]{1,0:T(8,128)S(1)}, u32[]{:S(2)}, u32[]{:S(2)}) collective-permute-start(f32[96,128]{1,0:T(8,128)S(1)} %combine.1.refs_0_), channel_id=1, source_target_pairs={{0,96},{32,64},{64,32},{96,0},{1,97},{33,65},{65,33},{97,1},{2,98}... | collective-permute-start | bytes 147464 | tf_op jit(solution)/shard_map/ppermute | solution.py:490
  30.0 3.4 %collective-permute-start = (f32[96,128]{1,0:T(8,128)S(1)}, f32[96,128]{1,0:T(8,128)S(1)}, u32[]{:S(2)}, u32[]{:S(2)}) collective-permute-start(f32[96,128]{1,0:T(8,128)S(1)} %combine.1.refs_0_), channel_id=1, source_target_pairs={{0,32},{32,0},{64,96},{96,64},{1,33},{33,1},{65,97},{97,65},{2,34}... | collective-permute-start | bytes 147464 | tf_op jit(solution)/shard_map/ppermute | solution.py:490
  34.1 5.3 %collective-permute-start.3 = (f32[64,128]{1,0:T(8,128)S(1)}, f32[64,128]{1,0:T(8,128)S(1)}, u32[]{:S(2)}, u32[]{:S(2)}) collective-permute-start(f32[64,128]{1,0:T(8,128)S(1)} %get-tuple-element.22), channel_id=1, source_target_pairs={{1,2},{3,4},{5,6},{7,8},{9,10},{11,12},{13,14},{15,16},{17,18},{19... | collective-permute-start | bytes 98312 | tf_op jit(solution)/shard_map/ppermute | solution.py:471
  37.5 1.9 %collective-permute-start.4 = (f32[64,128]{1,0:T(8,128)S(1)}, f32[64,128]{1,0:T(8,128)S(1)}, u32[]{:S(2)}, u32[]{:S(2)}) collective-permute-start(f32[64,128]{1,0:T(8,128)S(1)} %get-tuple-element.23), channel_id=1, source_target_pairs={{0,1},{1,0},{2,3},{3,2},{4,5},{5,4},{6,7},{7,6},{8,9},{9,8},{10,11... | collective-permute-start | bytes 98312 | tf_op jit(solution)/shard_map/ppermute | solution.py:472
  40.8 5.6 %collective-permute-start.5 = (f32[128,128]{1,0:T(8,128)S(1)}, f32[128,128]{1,0:T(8,128)S(1)}, u32[]{:S(2)}, u32[]{:S(2)}) collective-permute-start(f32[128,128]{1,0:T(8,128)S(1)} %get-tuple-element.30), channel_id=1, source_target_pairs={{1,2},{3,4},{5,6},{7,8},{9,10},{11,12},{13,14},{15,16},{17,18},{19... | collective-permute-start | bytes 196616 | tf_op jit(solution)/shard_map/ppermute | solution.py:471
  44.2 2.2 %collective-permute-start.6 = (f32[128,128]{1,0:T(8,128)S(1)}, f32[128,128]{1,0:T(8,128)S(1)}, u32[]{:S(2)}, u32[]{:S(2)}) collective-permute-start(f32[128,128]{1,0:T(8,128)S(1)} %get-tuple-element.31), channel_id=1, source_target_pairs={{0,1},{1,0},{2,3},{3,2},{4,5},{5,4},{6,7},{7,6},{8,9},{9,8},{10,11... | collective-permute-start | bytes 196616 | tf_op jit(solution)/shard_map/ppermute | solution.py:472
